TPU v7x, 512 devices: a whole 4x4x16 slice. The times are simulated.
512 devices in a mesh: grp: 32 (over y, x, core), shard: 16 (over z).
Axes of the slice: x: 4, y: 4, z: 16, core: 2. Of those that a mesh axis runs over, the one named last changes fastest.
Arguments:
- grads: bfloat16 [2, 32, 16, 768, 768], P(None, 'grp', 'shard')
- vec_grads: bfloat16 [2, 32, 16, 8, 768], P(None, 'grp', 'shard'), may hold values from -0.5 to 0.5
- weight: float32 [768, 768], P('shard'), may hold values from -0.21875 to 0.21875
- basis: float32 [768, 256], replicated, may hold values from -0.21875 to 0.21875
- moment: float32 [768, 256], P('shard'), may hold values from -4 to 4
- second: float32 [768, 256], P('shard'), may hold values from 0.01 to 1
- vectors: float32 [8, 768], P(None, 'shard'), may hold values from -6 to 6
- vec_moment: float32 [8, 768], P(None, 'shard'), may hold values from -1.5 to 1.5
- vec_second: float32 [8, 768], P(None, 'shard'), may hold values from 0.001 to 0.1
Outputs:
- new_weight: float32 [768, 768], P('shard')
- update: bfloat16 [768, 768], P('shard')
- new_moment: float32 [768, 256], P('shard')
- new_second: float32 [768, 256], P('shard')
- new_basis: float32 [768, 256], replicated
- new_vectors: float32 [8, 768], P(None, 'shard')
- new_vec_moment: float32 [8, 768], P(None, 'shard')
- new_vec_second: float32 [8, 768], P(None, 'shard')
All inputs are finite; a program needn't handle non-finite values.
Results may differ from a plain program's by a relative error of at most 0.001.
Values sent between devices are 32-bit elements; how exact they have to be, the bound alone decides.
A program may use at most 64 MiB of HBM per device.

v0:
```python
import jax
import jax.numpy as jnp
from jax import lax
from jax.sharding import PartitionSpec as P

NS_STEPS = 5
STEP = 100


HIGH = lax.Precision.HIGHEST


def matmul(left, right):
    return jnp.dot(left, right, precision=HIGH, preferred_element_type=jnp.float32)


def per_device(grads, vec_grads, weight, basis, moment, second, vectors, vec_moment, vec_second):
    shards = lax.axis_size("shard")
    width = grads.shape[-1]
    summed = grads[0, 0, 0].astype(jnp.float32) + grads[1, 0, 0].astype(jnp.float32)
    vec_local = vec_grads[0, 0, 0].astype(jnp.float32) + vec_grads[1, 0, 0].astype(jnp.float32)
    row_sum, vec_part = (
        lax.psum_scatter(summed, "shard", scatter_dimension=0, tiled=True),
        lax.psum_scatter(vec_local.T, "shard", scatter_dimension=0, tiled=True),
    )
    row_sum, vec_part = lax.psum((row_sum, vec_part), "grp")
    vec_sum = vec_part.T
    projected = matmul(row_sum, basis)
    partial_value = lax.dot_general(
        row_sum,
        projected,
        (((0,), (0,)), ((), ())),
        precision=HIGH,
        preferred_element_type=jnp.float32,
    )
    local_squares = jnp.sum(row_sum * row_sum) + jnp.sum(vec_sum * vec_sum)
    subspace, squares = lax.psum((partial_value, local_squares), "shard")
    iterate = subspace / jnp.sqrt(jnp.sum(subspace * subspace) + 1e-06)
    for step in range(NS_STEPS):
        gram = matmul(iterate.T, iterate)
        iterate = 1.5 * iterate - 0.5 * matmul(iterate, gram)
    factor = 1.0 / jnp.maximum(jnp.sqrt(squares / (width * width + vec_sum.size * shards)), 1.0)
    first_fix = 1.0 - 0.9**STEP
    second_fix = 1.0 - 0.999**STEP
    grad_low = factor * projected
    new_moment = 0.9 * moment + 0.1 * grad_low
    new_second = 0.999 * second + 0.001 * grad_low * grad_low
    normalized = new_moment / first_fix / (jnp.sqrt(new_second / second_fix) + 1e-08)
    full = lax.dot_general(
        normalized,
        basis,
        (((1,), (1,)), ((), ())),
        precision=HIGH,
        preferred_element_type=jnp.float32,
    )
    new_weight = weight - 0.001 * (0.25 * full + 0.01 * weight)
    vec_grad = factor * vec_sum
    new_vec_moment = 0.9 * vec_moment + 0.1 * vec_grad
    new_vec_second = 0.999 * vec_second + 0.001 * vec_grad * vec_grad
    vec_step = new_vec_moment / first_fix / (jnp.sqrt(new_vec_second / second_fix) + 1e-08)
    new_vectors = vectors - 0.001 * (vec_step + 0.01 * vectors)
    return (
        new_weight,
        full.astype(jnp.bfloat16),
        new_moment,
        new_second,
        iterate,
        new_vectors,
        new_vec_moment,
        new_vec_second,
    )


def solution(mesh):
    return jax.shard_map(
        per_device,
        mesh=mesh,
        in_specs=(
            P(None, "grp", "shard", None, None),
            P(None, "grp", "shard", None, None),
            P("shard", None),
            P(),
            P("shard", None),
            P("shard", None),
            P(None, "shard"),
            P(None, "shard"),
            P(None, "shard"),
        ),
        out_specs=(
            P("shard", None),
            P("shard", None),
            P("shard", None),
            P("shard", None),
            P(),
            P(None, "shard"),
            P(None, "shard"),
            P(None, "shard"),
        ),
        check_vma=False,
    )
```

profile of v0, /device:TPU:1, one launch (start us, length us, event | category | flops | bytes accessed | tf_op | source)
XLA Modules:
  0.0 476.0 jit_solution(4367489584696683417)
XLA Ops:
  7.2 0.0 copy-start
  7.2 0.0 reduce-scatter.7.cloned.1.call-start
  7.2 0.8 add_bitcast_fusion.1
  8.0 0.9 copy.17
  8.9 0.0 reduce-scatter.7.cloned.1.call-update
  9.0 0.0 reduce-scatter.5.cloned.1.call-start
  9.0 3.3 add_bitcast_fusion
  12.3 0.0 copy-start.9
  12.3 0.0 copy-start.4
  12.3 0.0 reduce-scatter.5.cloned.1.call-update
  12.4 0.0 all-reduce.3.cloned.1.call-start
  12.4 62.3 %reduce-scatter.7.cloned.1.call-done = f32[48,8]{1,0:T(8,128)} async-done(((f32[768,8]{1,0:T(8,128)}), f32[48,8]{1,0:T(8,128)}) %reduce-scatter.7.cloned.1.call-update) | async-done | bytes 1552
  74.7 0.8 copy.18
  75.5 73.7 %psum.29 = f32[48,8]{0,1:T(8,128)S(1)} all-reduce(f32[48,8]{0,1:T(8,128)S(1)} %copy.18), channel_id=1, replica_groups=mesh['grp'=32,'shard'=16] {'grp'}, use_global_device_ids=true, to_apply=%region_4.0 | all-reduce | flops 384 | bytes 3072 | tf_op jit(solution)/shard_map/psum | solution.py:26
  149.2 1.6 reduce-scatter.5.cloned.1.call-done
  150.8 0.0 all-reduce.3.cloned.1.call-update
  150.8 0.0 all-reduce.5.cloned.1.call-start
  150.8 0.6 multiply_reduce_fusion.2
  151.4 139.8 %all-reduce.3.cloned.1.call-done = f32[48,768]{1,0:T(8,128)} async-done(((f32[48,768]{1,0:T(8,128)}), f32[48,768]{1,0:T(8,128)}) %all-reduce.3.cloned.1.call-update) | async-done | bytes 147472 | tf_op jit(solution)/shard_map/psum | solution.py:26
  291.3 1.6 multiply_reduce_fusion.1
  294.1 24.5 %psum.30 = f32[]{:T(128)} all-reduce(f32[]{:T(128)S(6)} %add.64), channel_id=1, replica_groups=mesh['grp'=32,'shard'=16] {'shard'}, use_global_device_ids=true, to_apply=%region_6.0 | all-reduce | flops 1 | bytes 8 | tf_op jit(solution)/shard_map/psum | solution.py:37
  319.4 0.0 copy-done
  319.4 0.0 copy-done.5
  319.4 0.0 copy-done.6
  319.4 1.4 multiply_add_fusion
  320.8 0.0 copy-start.2
  320.8 0.0 copy-start.3
  320.9 2.6 fusion.24
  323.5 0.0 all-reduce.5.cloned.1.call-update
  323.5 0.0 copy-done.7
  323.5 0.0 copy-done.8
  323.5 0.0 copy-done.9
  323.6 0.6 multiply_subtract_fusion.1
  324.2 0.0 copy-done.4
  324.2 1.5 fusion.23
  325.7 127.7 %all-reduce.5.cloned.1.call-done = f32[768,256]{1,0:T(8,128)} async-done(((f32[768,256]{1,0:T(8,128)}), f32[768,256]{1,0:T(8,128)}) %all-reduce.5.cloned.1.call-update) | async-done | bytes 786448 | tf_op jit(solution)/shard_map/psum | solution.py:37
  453.4 2.0 multiply_reduce_fusion
  456.1 2.8 fusion.5
  458.9 0.0 copy-done.2
  458.9 0.8 fusion.4
  459.7 1.4 fusion.25
  461.2 0.8 fusion.3
  462.0 1.4 fusion.26
  463.4 0.8 fusion.2
  464.2 1.4 fusion.27
  465.6 0.8 fusion.1
  466.4 1.4 fusion.28
  467.8 1.7 fusion
  (7 shorter events, 0.0 us)
Async XLA Ops:
  7.2 312.2 %copy-start = (f32[768,256]{1,0:T(8,128)S(1)}, f32[768,256]{1,0:T(8,128)}, u32[]{:S(2)}) copy-start(f32[768,256]{1,0:T(8,128)} %param.12) | copy-start | bytes 2359300
  7.2 67.5 %reduce-scatter.7.cloned.1.call-start = ((), (), s32[]{:S(2)}) async-start(), calls=%async_computation.5 | async-start | bytes 417792
  9.0 141.8 %reduce-scatter.5.cloned.1.call-start = ((), (), s32[]{:S(2)}) async-start(), calls=%async_computation.2 | async-start | bytes 2506752 | tf_op jit(solution)/shard_map/reduce_scatter | solution.py:23
  12.3 307.1 %copy-start.5 = (f32[48,256]{1,0:T(8,128)S(1)}, f32[48,256]{1,0:T(8,128)}, u32[]{:S(2)}) copy-start(f32[48,256]{1,0:T(8,128)} %param.13) | copy-start | bytes 147460
  12.3 307.1 %copy-start.6 = (f32[48,256]{1,0:T(8,128)S(1)}, f32[48,256]{1,0:T(8,128)}, u32[]{:S(2)}) copy-start(f32[48,256]{1,0:T(8,128)} %param.14) | copy-start | bytes 147460
  12.3 311.2 %copy-start.7 = (f32[8,48]{1,0:T(8,128)S(1)}, f32[8,48]{1,0:T(8,128)}, u32[]{:S(2)}) copy-start(f32[8,48]{1,0:T(8,128)} %param.15) | copy-start | bytes 4612
  12.3 311.2 %copy-start.8 = (f32[8,48]{1,0:T(8,128)S(1)}, f32[8,48]{1,0:T(8,128)}, u32[]{:S(2)}) copy-start(f32[8,48]{1,0:T(8,128)} %param.16) | copy-start | bytes 4612
  12.3 311.2 %copy-start.9 = (f32[8,48]{1,0:T(8,128)S(1)}, f32[8,48]{1,0:T(8,128)}, u32[]{:S(2)}) copy-start(f32[8,48]{1,0:T(8,128)} %param.17) | copy-start | bytes 4612
  12.3 311.9 %copy-start.4 = (f32[48,768]{1,0:T(8,128)S(1)}, f32[48,768]{1,0:T(8,128)}, u32[]{:S(2)}) copy-start(f32[48,768]{1,0:T(8,128)} %param.11) | copy-start | bytes 442372
  12.4 278.9 %all-reduce.3.cloned.1.call-start = ((), (), s32[]{:S(2)}) async-start(), calls=%async_computation.3 | async-start | bytes 294912 | tf_op jit(solution)/shard_map/psum | solution.py:26
  150.8 302.6 %all-reduce.5.cloned.1.call-start = ((), (), s32[]{:S(2)}) async-start(), calls=%async_computation.4 | async-start | bytes 1572864 | tf_op jit(solution)/shard_map/psum | solution.py:37
  320.8 138.1 %copy-start.2 = (f32[48,256]{1,0:T(8,128)}, f32[48,256]{1,0:T(8,128)S(1)}, u32[]{:S(2)}) copy-start(f32[48,256]{1,0:T(8,128)S(1)} %get-tuple-element.13) | copy-start | bytes 147460
  320.8 138.1 %copy-start.3 = (f32[48,256]{1,0:T(8,128)}, f32[48,256]{1,0:T(8,128)S(1)}, u32[]{:S(2)}) copy-start(f32[48,256]{1,0:T(8,128)S(1)} %get-tuple-element.14) | copy-start | bytes 147460
  453.4 5.5 %copy-start.1 = (f32[768,256]{1,0:T(8,128)S(1)}, f32[768,256]{1,0:T(8,128)}, u32[]{:S(2)}) copy-start(f32[768,256]{1,0:T(8,128)} %all-reduce.5.cloned.1.call-done) | copy-start | bytes 2359300
Sparse Core Ops, SparseCore 0:
  11.4 63.2 reduce-scatter.6
  77.7 72.9 reduce-scatter.4
  154.4 136.8 all-reduce.2
  323.6 129.7 all-reduce.4
where the time goes:
time: 485 us; the launch traced here: 476 us
  waiting for transfers between devices  331 us (68%)
  blocking collectives  98.3 us (20%)
  matrix products  18.9 us (4%)
  between operations  16.7 us (3%)
  other arithmetic  8.87 us (2%)
    psum x1, waiting for transfers between devices, per_device(): row_sum, vec_part = lax.psum((row_sum, vec_part), 'grp')  140 us
    psum x1, waiting for transfers between devices, per_device(): subspace, squares = lax.psum((partial_value, local_squares), 'shard')  128 us
    psum x1, blocking collectives, per_device(): row_sum, vec_part = lax.psum((row_sum, vec_part), 'grp')  73.7 us
    unnamed x5, waiting for transfers between devices  62.3 us
    psum x1, blocking collectives, per_device(): subspace, squares = lax.psum((partial_value, local_squares), 'shard')  24.5 us
    dot_general x11, matrix products, matmul(): jnp.dot(left, right, precision=HIGH, preferred_element_type=jnp.float32)  14.7 us
  transfers between devices with their start and end apart: 4, of which 4 were waited for; matrix products, arithmetic and copies ran while one was open for 1% of the time, Pallas kernels for 0%

commit v1 on v0

--- a/solution.py
+++ b/solution.py
@@ -17,29 +17,31 @@
 def per_device(grads, vec_grads, weight, basis, moment, second, vectors, vec_moment, vec_second):
     shards = lax.axis_size("shard")
     width = grads.shape[-1]
+    rows = weight.shape[0]
+    cols = vectors.shape[1]
+    me = lax.axis_index("shard")
     summed = grads[0, 0, 0].astype(jnp.float32) + grads[1, 0, 0].astype(jnp.float32)
     vec_local = vec_grads[0, 0, 0].astype(jnp.float32) + vec_grads[1, 0, 0].astype(jnp.float32)
-    row_sum, vec_part = (
-        lax.psum_scatter(summed, "shard", scatter_dimension=0, tiled=True),
-        lax.psum_scatter(vec_local.T, "shard", scatter_dimension=0, tiled=True),
-    )
-    row_sum, vec_part = lax.psum((row_sum, vec_part), "grp")
-    vec_sum = vec_part.T
-    projected = matmul(row_sum, basis)
-    partial_value = lax.dot_general(
-        row_sum,
-        projected,
+    packed = jnp.concatenate([summed, vec_local], axis=0)
+    packed = lax.psum(packed, ("grp", "shard"))
+    total = packed[:width]
+    vec_total = packed[width:]
+    projected_all = matmul(total, basis)
+    subspace = lax.dot_general(
+        total,
+        projected_all,
         (((0,), (0,)), ((), ())),
         precision=HIGH,
         preferred_element_type=jnp.float32,
     )
-    local_squares = jnp.sum(row_sum * row_sum) + jnp.sum(vec_sum * vec_sum)
-    subspace, squares = lax.psum((partial_value, local_squares), "shard")
+    squares = jnp.sum(total * total) + jnp.sum(vec_total * vec_total)
     iterate = subspace / jnp.sqrt(jnp.sum(subspace * subspace) + 1e-06)
     for step in range(NS_STEPS):
         gram = matmul(iterate.T, iterate)
         iterate = 1.5 * iterate - 0.5 * matmul(iterate, gram)
-    factor = 1.0 / jnp.maximum(jnp.sqrt(squares / (width * width + vec_sum.size * shards)), 1.0)
+    factor = 1.0 / jnp.maximum(jnp.sqrt(squares / (width * width + vec_total.size)), 1.0)
+    projected = lax.dynamic_slice_in_dim(projected_all, me * rows, rows, axis=0)
+    vec_sum = lax.dynamic_slice_in_dim(vec_total, me * cols, cols, axis=1)
     first_fix = 1.0 - 0.9**STEP
     second_fix = 1.0 - 0.999**STEP
     grad_low = factor * projected

time: 485 us -> 535 us (1.10); the launches traced: 476 us -> 535 us
  waiting for transfers between devices: 331 us -> 485 us
  blocking collectives: 98.3 us -> 0 us
    psum x2 -> x1, waiting for transfers between devices: 268 us -> 485 us  [per_device(): packed = lax.psum(packed, ('grp', 'shard'))]
    psum x2 -> x0, blocking collectives: 98.3 us -> none  [the longest x1 73.7 us: per_device(): row_sum, vec_part = lax.psum((row_sum, vec_part), 'grp')]
    unnamed x5 -> x1, waiting for transfers between devices: 62.3 us -> 0.02 us
  transfers between devices with their start and end apart: 4 -> 1, of which waited for: 4 -> 1; matrix products, arithmetic and copies ran while one was open for 1% -> 0% of each run, Pallas kernels for 0% -> 0%
where the time goes in v1:
time: 535 us
  waiting for transfers between devices  485 us (91%)
  matrix products  22.4 us (4%)
  between operations  16.4 us (3%)
  other arithmetic  10.1 us (2%)
    psum x1, waiting for transfers between devices, per_device(): packed = lax.psum(packed, ('grp', 'shard'))  485 us
    dot_general x11, matrix products, matmul(): jnp.dot(left, right, precision=HIGH, preferred_element_type=jnp.float32)  15.6 us
  transfers between devices with their start and end apart: 1, of which 1 were waited for; matrix products, arithmetic and copies ran while one was open for 0% of the time, Pallas kernels for 0%

profile of v1, /device:TPU:1, one launch (start us, length us, event | category | flops | bytes accessed | tf_op | source)
XLA Modules:
  0.0 534.5 jit_solution(420021904912794236)
XLA Ops:
  7.2 0.0 copy-start
  7.2 0.0 all-reduce.2.cloned.1.call-start
  7.2 0.8 add_bitcast_fusion.1
  8.0 1.9 add_bitcast_fusion
  9.9 1.6 pad_maximum_fusion
  11.5 0.0 all-reduce.2.cloned.1.call-update
  11.5 485.5 %all-reduce.2.cloned.1.call-done = f32[776,768]{1,0:T(8,128)} async-done(((f32[776,768]{1,0:T(8,128)}), f32[776,768]{1,0:T(8,128)}) %all-reduce.2.cloned.1.call-update) | async-done | bytes 2383888 | tf_op jit(solution)/shard_map/psum | solution.py:26
  497.0 0.0 copy-start.1
  497.0 3.0 multiply_reduce_fusion
  500.0 1.3 fusion.25
  502.7 0.0 copy-done
  502.7 0.0 copy-done.1
  502.7 2.0 fusion.2
  504.7 0.0 copy-start.2
  504.8 5.3 multiply_reduce_fusion.1
  510.1 0.0 copy-done.2
  510.1 0.0 copy-start.3
  510.9 2.9 fusion.9
  513.8 0.0 copy-done.3
  513.8 0.8 fusion.8
  514.6 1.4 fusion.27
  516.0 0.8 fusion.7
  516.8 1.6 fusion.28
  518.4 0.8 fusion.6
  519.2 1.4 fusion.29
  520.6 0.0 copy-start.7
  520.6 0.0 copy-start.8
  520.7 0.8 fusion.5
  521.4 0.0 copy-start.6
  521.5 0.0 copy-start.9
  521.5 0.0 copy-start.10
  521.5 0.0 copy-start.11
  521.5 1.4 fusion.30
  522.9 1.7 fusion.4
  524.6 0.0 copy-done.7
  524.6 0.0 copy-done.8
  524.6 0.8 multiply_add_fusion
  525.4 0.0 copy-start.4
  525.4 0.0 copy-start.5
  525.4 0.0 copy-done.6
  525.5 1.5 fusion.26
  527.0 0.0 copy-done.9
  527.0 0.0 copy-done.10
  527.0 0.0 copy-done.11
  527.0 0.7 multiply_subtract_fusion.1
  527.7 0.0 copy-done.4
  527.7 0.0 copy-done.5
Async XLA Ops:
  7.2 495.5 %copy-start = (f32[768,256]{1,0:T(8,128)S(1)}, f32[768,256]{1,0:T(8,128)}, u32[]{:S(2)}) copy-start(f32[768,256]{1,0:T(8,128)} %param.12) | copy-start | bytes 2359300
  7.2 489.8 %all-reduce.2.cloned.1.call-start = ((), (), s32[]{:S(2)}) async-start(), calls=%async_computation | async-start | bytes 4767744 | tf_op jit(solution)/shard_map/psum | solution.py:26
  497.0 5.8 %copy-start.1 = (f32[776,768]{1,0:T(8,128)S(1)}, f32[776,768]{1,0:T(8,128)}, u32[]{:S(2)}) copy-start(f32[776,768]{1,0:T(8,128)} %all-reduce.2.cloned.1.call-done) | copy-start | bytes 7151620
  504.7 5.3 %copy-start.2 = (f32[768,256]{1,0:T(8,128)}, f32[768,256]{1,0:T(8,128)S(1)}, u32[]{:S(2)}) copy-start(f32[768,256]{1,0:T(8,128)S(1)} %fusion.2) | copy-start | bytes 2359300
  510.1 3.7 copy-start.3
  520.6 4.0 copy-start.7
  520.6 4.0 copy-start.8
  521.4 4.0 copy-start.6
  521.5 5.5 %copy-start.9 = (f32[8,48]{1,0:T(8,128)S(1)}, f32[8,48]{1,0:T(8,128)}, u32[]{:S(2)}) copy-start(f32[8,48]{1,0:T(8,128)} %param.15) | copy-start | bytes 4612
  521.5 5.5 %copy-start.10 = (f32[8,48]{1,0:T(8,128)S(1)}, f32[8,48]{1,0:T(8,128)}, u32[]{:S(2)}) copy-start(f32[8,48]{1,0:T(8,128)} %param.16) | copy-start | bytes 4612
  521.5 5.5 %copy-start.11 = (f32[8,48]{1,0:T(8,128)S(1)}, f32[8,48]{1,0:T(8,128)}, u32[]{:S(2)}) copy-start(f32[8,48]{1,0:T(8,128)} %param.17) | copy-start | bytes 4612
  525.4 2.3 copy-start.4
  525.4 2.3 copy-start.5
Sparse Core Ops, SparseCore 0:
  13.4 483.5 all-reduce.1

commit v2 on v1

--- a/solution.py
+++ b/solution.py
@@ -1,10 +1,16 @@
+import functools
+import math
+
 import jax
 import jax.numpy as jnp
 from jax import lax
+from jax.experimental import pallas as pl
+from jax.experimental.pallas import tpu as pltpu
 from jax.sharding import PartitionSpec as P
 
 NS_STEPS = 5
 STEP = 100
+MESH = pl.DeviceIdType.MESH
 
 
 HIGH = lax.Precision.HIGHEST
@@ -14,18 +20,166 @@
     return jnp.dot(left, right, precision=HIGH, preferred_element_type=jnp.float32)
 
 
-def per_device(grads, vec_grads, weight, basis, moment, second, vectors, vec_moment, vec_second):
+def _allreduce_kernel(nx, ny, nz, x_ref, out_ref, core_recv, core_sum, x_recv, x_sum, y_recv, y_sum,
+                      z_recv, z_sum, pair_recv, z_full, y_out, x_out, core_out, send_sem, recv_sem):
+    rows, cols = x_ref.shape
+    nh = nz // 2
+    rc, rx, ry, cz = rows // 2, rows // 2 // nx, rows // 2 // nx // ny, cols // nh
+    g = lax.axis_index("grp")
+    z = lax.axis_index("shard")
+    core = g % 2
+    xi = (g // 2) % nx
+    yi = g // (2 * nx)
+    zp = z % 2
+    zi = z // 2
+
+    def core_dev(_):
+        return (g + 1 - 2 * core, z)
+
+    def x_dev(j):
+        return (g + 2 * (j - xi), z)
+
+    def y_dev(j):
+        return (g + 2 * nx * (j - yi), z)
+
+    def z_dev(j):
+        return (g, zp + 2 * j)
+
+    pair_dev = (g, z + 1 - 2 * zp)
+
+    barrier = pltpu.get_barrier_semaphore()
+    peers = [core_dev(0), pair_dev]
+    peers += [x_dev((xi + k) % nx) for k in range(1, nx)]
+    peers += [y_dev((yi + k) % ny) for k in range(1, ny)]
+    peers += [z_dev((zi + k) % nh) for k in range(1, nh)]
+    for dev in peers:
+        pl.semaphore_signal(barrier, inc=1, device_id=dev, device_id_type=MESH)
+    pl.semaphore_wait(barrier, len(peers))
+
+    counter = [0]
+
+    def next_sem():
+        s = counter[0]
+        counter[0] += 1
+        return s
+
+    def row_slice(j, size):
+        return pl.ds(pl.multiple_of(j * size, 8), size)
+
+    def col_slice(j, size):
+        return (slice(None), pl.ds(pl.multiple_of(j * size, 128), size))
+
+    def reduce_stage(src, n, me, dev_of, recv, dst, piece):
+        copies = []
+        for k in range(1, n):
+            j = (me + k) % n
+            s = next_sem()
+            c = pltpu.make_async_remote_copy(
+                src_ref=src.at[piece(j)], dst_ref=recv.at[k - 1], send_sem=send_sem.at[s],
+                recv_sem=recv_sem.at[s], device_id=dev_of(j), device_id_type=MESH)
+            c.start()
+            copies.append(c)
+        for c in copies:
+            c.wait()
+        acc = src[piece(me)]
+        for k in range(1, n):
+            acc = acc + recv[k - 1]
+        dst[...] = acc
+
+    def gather_stage(src, n, me, dev_of, dst, piece):
+        copies = []
+        for k in range(1, n):
+            j = (me + k) % n
+            s = next_sem()
+            c = pltpu.make_async_remote_copy(
+                src_ref=src, dst_ref=dst.at[piece(me)], send_sem=send_sem.at[s],
+                recv_sem=recv_sem.at[s], device_id=dev_of(j), device_id_type=MESH)
+            c.start()
+            copies.append((c, s, k))
+        dst[piece(me)] = src[...]
+        for c, s, k in copies:
+            c.wait_send()
+            j = (me + n - k) % n
+            pltpu.make_async_remote_copy(
+                src_ref=src, dst_ref=dst.at[piece(j)], send_sem=send_sem.at[s],
+                recv_sem=recv_sem.at[s], device_id=dev_of(j), device_id_type=MESH).wait_recv()
+
+    core_piece = lambda j: row_slice(j, rc)
+    x_piece = lambda j: row_slice(j, rx)
+    y_piece = lambda j: row_slice(j, ry)
+    z_piece = lambda j: col_slice(j, cz)
+
+    reduce_stage(x_ref, 2, core, core_dev, core_recv, core_sum, core_piece)
+    reduce_stage(core_sum, nx, xi, x_dev, x_recv, x_sum, x_piece)
+    reduce_stage(x_sum, ny, yi, y_dev, y_recv, y_sum, y_piece)
+    reduce_stage(y_sum, nh, zi, z_dev, z_recv, z_sum, z_piece)
+
+    s = next_sem()
+    c = pltpu.make_async_remote_copy(
+        src_ref=z_sum, dst_ref=pair_recv, send_sem=send_sem.at[s], recv_sem=recv_sem.at[s],
+        device_id=pair_dev, device_id_type=MESH)
+    c.start()
+    c.wait()
+    z_full[...] = z_sum[...] + pair_recv[...]
+
+    gather_stage(z_full, nh, zi, z_dev, y_out, z_piece)
+    gather_stage(y_out, ny, yi, y_dev, x_out, y_piece)
+    gather_stage(x_out, nx, xi, x_dev, core_out, x_piece)
+    gather_stage(core_out, 2, core, core_dev, out_ref, core_piece)
+
+
+def allreduce(x, nx, ny, nz):
+    rows, cols = x.shape
+    nh = nz // 2
+    rc = rows // 2
+    rx = rc // nx
+    ry = rx // ny
+    cz = cols // nh
+    n_sems = 2 * (1 + (nx - 1) + (ny - 1) + (nh - 1)) + 1
+    f32 = jnp.float32
+    return pl.pallas_call(
+        functools.partial(_allreduce_kernel, nx, ny, nz),
+        out_shape=jax.ShapeDtypeStruct((rows, cols), f32),
+        in_specs=[pl.BlockSpec(memory_space=pltpu.VMEM)],
+        out_specs=pl.BlockSpec(memory_space=pltpu.VMEM),
+        scratch_shapes=[
+            pltpu.VMEM((1, rc, cols), f32),
+            pltpu.VMEM((rc, cols), f32),
+            pltpu.VMEM((nx - 1, rx, cols), f32),
+            pltpu.VMEM((rx, cols), f32),
+            pltpu.VMEM((ny - 1, ry, cols), f32),
+            pltpu.VMEM((ry, cols), f32),
+            pltpu.VMEM((nh - 1, ry, cz), f32),
+            pltpu.VMEM((ry, cz), f32),
+            pltpu.VMEM((ry, cz), f32),
+            pltpu.VMEM((ry, cz), f32),
+            pltpu.VMEM((ry, cols), f32),
+            pltpu.VMEM((rx, cols), f32),
+            pltpu.VMEM((rc, cols), f32),
+            pltpu.SemaphoreType.DMA((n_sems,)),
+            pltpu.SemaphoreType.DMA((n_sems,)),
+        ],
+        compiler_params=pltpu.CompilerParams(
+            collective_id=0, has_side_effects=True, vmem_limit_bytes=48 * 1024 * 1024),
+    )(x)
+
+
+def per_device(nx, ny, grads, vec_grads, weight, basis, moment, second, vectors, vec_moment, vec_second):
     shards = lax.axis_size("shard")
     width = grads.shape[-1]
     rows = weight.shape[0]
     cols = vectors.shape[1]
+    vec_n = vectors.shape[0]
     me = lax.axis_index("shard")
     summed = grads[0, 0, 0].astype(jnp.float32) + grads[1, 0, 0].astype(jnp.float32)
     vec_local = vec_grads[0, 0, 0].astype(jnp.float32) + vec_grads[1, 0, 0].astype(jnp.float32)
-    packed = jnp.concatenate([summed, vec_local], axis=0)
-    packed = lax.psum(packed, ("grp", "shard"))
-    total = packed[:width]
-    vec_total = packed[width:]
+    lanes = 128 * (shards // 2)
+    padded = lanes * ((width + vec_n + lanes - 1) // lanes)
+    pad = jnp.zeros((width, padded - width - vec_n), jnp.float32)
+    packed = jnp.concatenate([summed, vec_local.T, pad], axis=1)
+    packed = allreduce(packed, nx, ny, shards)
+    total = packed[:, :width]
+    vec_total = packed[:, width:width + vec_n].T
     projected_all = matmul(total, basis)
     subspace = lax.dot_general(
         total,
@@ -73,9 +227,12 @@
     )
 
 
-def solution(mesh):
+def solution(mesh, nx=None):
+    if nx is None:
+        nx = math.isqrt(mesh.shape["grp"] // 2)
+    ny = mesh.shape["grp"] // 2 // nx
     return jax.shard_map(
-        per_device,
+        functools.partial(per_device, nx, ny),
         mesh=mesh,
         in_specs=(
             P(None, "grp", "shard", None, None),

time: 535 us -> 126 us (0.24)
  waiting for transfers between devices: 485 us -> 0 us
  Pallas kernels: 0 us -> 93.1 us
  between operations: 16.4 us -> 2.96 us
    psum x1 -> x0, waiting for transfers between devices: 485 us -> none  [per_device(): packed = lax.psum(packed, ('grp', 'shard'))]
    pallas_call x0 -> x1, Pallas kernels: none -> 93.1 us  [allreduce(): pl.pallas_call(functools.partial(_allreduce_kernel, nx, ny, nz), out_shap...]
  transfers between devices with their start and end apart: 1 -> 0, of which waited for: 1 -> 0; matrix products, arithmetic and copies ran while one was open for 0% -> 0% of each run, Pallas kernels for 0% -> 0%
where the time goes in v2:
time: 126 us
  Pallas kernels  93.1 us (74%)
  matrix products  20.1 us (16%)
  other arithmetic  6.66 us (5%)
  local copies, waits for them, and re-layouts  3.35 us (3%)
  between operations  2.96 us (2%)
    pallas_call x1, Pallas kernels, allreduce(): pl.pallas_call(functools.partial(_allreduce_kernel, nx, ny, nz), out_shap...  93.1 us
    dot_general x11, matrix products, matmul(): jnp.dot(left, right, precision=HIGH, preferred_element_type=jnp.float32)  14.1 us
    dot_general x1, matrix products, per_device(): lax.dot_general(total, projected_all, (((0,), (0,)), ((), ())), precision...  4.44 us

profile of v2, /device:TPU:1, one launch (start us, length us, event | category | flops | bytes accessed | tf_op | source)
XLA Modules:
  0.0 126.2 jit_solution(774822176942451835)
XLA Ops:
  0.6 0.0 copy-start
  0.6 0.0 copy-start.8
  0.7 1.9 %add_bitcast_fusion = f32[768,768]{1,0:T(8,128)S(1)} fusion(bf16[2,1,1,768,768]{4,3,2,1,0:T(8,128)(2,1)} %param.9), kind=kLoop, calls=%fused_computation.2 | loop fusion | flops 1769472 | bytes 4718592 | tf_op jit(solution)/shard_map/add | solution.py:174
  2.6 0.0 copy-done.8
  2.6 0.6 convert_add_fusion
  3.2 0.9 copy.29
  4.1 0.1 pad.2.clone
  4.2 2.1 %maximum_maximum_fusion.x_ref = f32[768,1024]{1,0:T(8,128)} fusion(f32[768,8]{1,0:T(8,128)S(1)} %bitcast.32, f32[768,768]{1,0:T(8,128)S(1)} %add_bitcast_fusion, f32[1024]{0:T(1024)S(1)} %pad.2.clone), kind=kLoop, calls=%fused_computation | loop fusion | flops 1572864 | bytes 5533696 | tf_op jit(solution)/shard_map/concatenate | solution.py:179
  6.3 93.1 %shard_map.152 = f32[768,1024]{1,0:T(8,128)S(1)} custom-call(f32[768,1024]{1,0:T(8,128)} %maximum_maximum_fusion.x_ref), custom_call_target="tpu_custom_call" | custom-call | tf_op jit(solution)/shard_map/pallas_call | solution.py:140
  99.5 0.0 copy-done
  99.5 0.0 copy-start.1
  99.5 2.0 %fusion.2 = f32[768,256]{1,0:T(8,128)S(1)} fusion(f32[768,256]{1,0:T(8,128)S(1)} %copy-done, f32[768,1024]{1,0:T(8,128)S(1)} %shard_map.152), kind=kOutput, calls=%fused_computation.5 | convolution fusion | flops 1811939328 | bytes 3932160 | tf_op jit(solution)/shard_map/dot_general | solution.py:20
  101.5 4.4 %multiply_reduce_fusion.1 = (f32[]{:T(128)}, f32[768,256]{1,0:T(8,128)S(1)}) fusion(f32[768,256]{1,0:T(8,128)S(1)} %fusion.2, f32[768,1024]{1,0:T(8,128)S(1)} %shard_map.152), kind=kOutput, calls=%fused_computation.17 | convolution fusion | flops 1812332544 | bytes 3932164 | tf_op jit(solution)/shard_map/dot_general | solution.py:184
  105.9 0.0 copy-done.1
  106.6 1.4 %fusion.9 = f32[256,256]{1,0:T(8,128)S(1)} fusion(f32[768,256]{1,0:T(8,128)S(1)} %get-tuple-element.34, f32[]{:T(128)S(6)} %sqrt.14), kind=kOutput, calls=%fused_computation.20 | convolution fusion | flops 604176384 | bytes 1048580 | tf_op jit(solution)/shard_map/dot_general | solution.py:20
  108.1 0.8 fusion.8
  108.9 1.4 %fusion.29 = f32[256,256]{1,0:T(8,128)S(1)} fusion(f32[768,256]{1,0:T(8,128)S(1)} %fusion.8), kind=kOutput, calls=%fused_computation.50 | convolution fusion | flops 603979776 | bytes 1048576 | tf_op jit(solution)/shard_map/dot_general | solution.py:20
  110.3 0.8 fusion.7
  111.1 1.6 %fusion.30 = f32[256,256]{1,0:T(8,128)S(1)} fusion(f32[768,256]{1,0:T(8,128)S(1)} %fusion.7), kind=kOutput, calls=%fused_computation.51 | convolution fusion | flops 603979776 | bytes 1048576 | tf_op jit(solution)/shard_map/dot_general | solution.py:20
  112.7 0.8 fusion.6
  113.5 1.4 %fusion.31 = f32[256,256]{1,0:T(8,128)S(1)} fusion(f32[768,256]{1,0:T(8,128)S(1)} %fusion.6), kind=kOutput, calls=%fused_computation.52 | convolution fusion | flops 603979776 | bytes 1048576 | tf_op jit(solution)/shard_map/dot_general | solution.py:20
  114.9 0.0 copy-start.2
  114.9 0.8 fusion.5
  115.7 1.4 %fusion.32 = f32[256,256]{1,0:T(8,128)S(1)} fusion(f32[768,256]{1,0:T(8,128)S(1)} %fusion.5), kind=kOutput, calls=%fused_computation.53 | convolution fusion | flops 603979776 | bytes 1048576 | tf_op jit(solution)/shard_map/dot_general | solution.py:20
  117.2 0.0 copy-start.6
  117.2 0.0 copy-start.7
  117.2 0.0 copy-start.5
  117.2 1.7 %fusion.4 = f32[768,256]{1,0:T(8,128)} fusion(f32[768,256]{1,0:T(8,128)S(1)} %fusion.5, f32[256,256]{1,0:T(8,128)S(1)} %fusion.32), kind=kOutput, calls=%fused_computation.8 | convolution fusion | flops 604569600 | bytes 1835008 | tf_op jit(solution)/shard_map/dot_general | solution.py:20
  118.9 0.0 copy-done.2
  118.9 0.7 fusion.27
  119.6 1.2 multiply_reduce_fusion
  122.2 0.0 copy-done.6
  122.2 0.0 copy-done.7
  122.2 0.0 copy-start.3
  122.2 0.0 copy-start.4
  122.3 0.0 copy-done.5
  122.3 1.5 %fusion.28 = (bf16[48,768]{1,0:T(8,128)(2,1)}, f32[48,768]{1,0:T(8,128)}) fusion(f32[48,768]{1,0:T(8,128)S(1)} %copy-done.5, f32[768,256]{1,0:T(8,128)S(1)} %copy-done, f32[48,256]{1,0:T(8,128)S(1)} %get-tuple-element.30, f32[48,256]{1,0:T(8,128)S(1)} %get-tuple-element.29), kind=kOutput, calls=%fused_computation.49 | convolution fusion | flops 113516544 | bytes 1253376 | tf_op jit(solution)/shard_map/dot_general | solution.py:205
  123.8 0.0 copy-done.10
  123.8 0.1 copy.31
  123.9 0.0 copy-done.11
  123.9 0.1 copy.32
  124.0 0.0 copy-done.9
  124.0 0.1 copy.33
  124.1 0.1 copy.34
  124.2 0.7 copy.35
  124.8 0.7 copy.36
  125.5 0.7 copy.37
  126.2 0.0 copy-done.4
  (10 shorter events, 0.1 us)
Async XLA Ops:
  0.6 98.8 %copy-start = (f32[768,256]{1,0:T(8,128)S(1)}, f32[768,256]{1,0:T(8,128)}, u32[]{:S(2)}) copy-start(f32[768,256]{1,0:T(8,128)} %param.12) | copy-start | bytes 2359300
  0.6 2.0 %copy-start.8 = (bf16[2,1,1,8,768]{4,3,2,1,0:T(8,128)(2,1)S(1)}, bf16[2,1,1,8,768]{4,3,2,1,0:T(8,128)(2,1)}, u32[]{:S(2)}) copy-start(bf16[2,1,1,8,768]{4,3,2,1,0:T(8,128)(2,1)} %param.10) | copy-start | bytes 73732
  99.5 6.5 %copy-start.1 = (f32[768,1024]{1,0:T(8,128)}, f32[768,1024]{1,0:T(8,128)S(1)}, u32[]{:S(2)}) copy-start(f32[768,1024]{1,0:T(8,128)S(1)} %shard_map.152) | copy-start | bytes 9437188
  114.9 3.9 %copy-start.2 = (f32[768,1024]{1,0:T(8,128)S(1)}, f32[768,1024]{1,0:T(8,128)}, u32[]{:S(2)}) copy-start(f32[768,1024]{1,0:T(8,128)} %copy-done.1) | copy-start | bytes 9437188
  117.2 5.0 %copy-start.6 = (f32[48,256]{1,0:T(8,128)S(1)}, f32[48,256]{1,0:T(8,128)}, u32[]{:S(2)}) copy-start(f32[48,256]{1,0:T(8,128)} %param.13) | copy-start | bytes 147460
  117.2 5.0 %copy-start.7 = (f32[48,256]{1,0:T(8,128)S(1)}, f32[48,256]{1,0:T(8,128)}, u32[]{:S(2)}) copy-start(f32[48,256]{1,0:T(8,128)} %param.14) | copy-start | bytes 147460
  117.2 5.1 %copy-start.5 = (f32[48,768]{1,0:T(8,128)S(1)}, f32[48,768]{1,0:T(8,128)}, u32[]{:S(2)}) copy-start(f32[48,768]{1,0:T(8,128)} %param.11) | copy-start | bytes 442372
  118.9 4.9 %copy-start.10 = (f32[8,48]{1,0:T(8,128)S(1)}, f32[8,48]{1,0:T(8,128)}, u32[]{:S(2)}) copy-start(f32[8,48]{1,0:T(8,128)} %param.16) | copy-start | bytes 4612
  118.9 5.0 %copy-start.11 = (f32[8,48]{1,0:T(8,128)S(1)}, f32[8,48]{1,0:T(8,128)}, u32[]{:S(2)}) copy-start(f32[8,48]{1,0:T(8,128)} %param.17) | copy-start | bytes 4612
  118.9 5.1 %copy-start.9 = (f32[8,48]{1,0:T(8,128)S(1)}, f32[8,48]{1,0:T(8,128)}, u32[]{:S(2)}) copy-start(f32[8,48]{1,0:T(8,128)} %param.15) | copy-start | bytes 4612
  122.2 3.9 %copy-start.3 = (f32[48,256]{1,0:T(8,128)}, f32[48,256]{1,0:T(8,128)S(1)}, u32[]{:S(2)}) copy-start(f32[48,256]{1,0:T(8,128)S(1)} %get-tuple-element.29) | copy-start | bytes 147460
  122.2 3.9 %copy-start.4 = (f32[48,256]{1,0:T(8,128)}, f32[48,256]{1,0:T(8,128)S(1)}, u32[]{:S(2)}) copy-start(f32[48,256]{1,0:T(8,128)S(1)} %get-tuple-element.30) | copy-start | bytes 147460

commit v3 on v2

--- a/solution.py
+++ b/solution.py
@@ -13,16 +13,19 @@
 MESH = pl.DeviceIdType.MESH
 
 
-HIGH = lax.Precision.HIGHEST
+HIGH = lax.Precision.HIGH
 
 
 def matmul(left, right):
     return jnp.dot(left, right, precision=HIGH, preferred_element_type=jnp.float32)
 
 
-def _allreduce_kernel(nx, ny, nz, x_ref, out_ref, core_recv, core_sum, x_recv, x_sum, y_recv, y_sum,
+def _allreduce_kernel(nx, ny, nz, g_ref, tail_ref, out_ref, sq_ref, x_ref, core_recv, core_sum, x_recv, x_sum, y_recv, y_sum,
                       z_recv, z_sum, pair_recv, z_full, y_out, x_out, core_out, send_sem, recv_sem):
     rows, cols = x_ref.shape
+    width = g_ref.shape[-1]
+    x_ref[:, :width] = g_ref[0].astype(jnp.float32) + g_ref[1].astype(jnp.float32)
+    x_ref[:, width:] = tail_ref[...]
     nh = nz // 2
     rc, rx, ry, cz = rows // 2, rows // 2 // nx, rows // 2 // nx // ny, cols // nh
     g = lax.axis_index("grp")
@@ -36,11 +39,16 @@
     def core_dev(_):
         return (g + 1 - 2 * core, z)
 
+    stride_a = 2 + (2 * nx - 2) * core
+    pos_a = xi + (yi - xi) * core
+    stride_b = 2 * nx - (2 * nx - 2) * core
+    pos_b = yi + (xi - yi) * core
+
     def x_dev(j):
-        return (g + 2 * (j - xi), z)
+        return (g + stride_a * (j - pos_a), z)
 
     def y_dev(j):
-        return (g + 2 * nx * (j - yi), z)
+        return (g + stride_b * (j - pos_b), z)
 
     def z_dev(j):
         return (g, zp + 2 * j)
@@ -49,8 +57,8 @@
 
     barrier = pltpu.get_barrier_semaphore()
     peers = [core_dev(0), pair_dev]
-    peers += [x_dev((xi + k) % nx) for k in range(1, nx)]
-    peers += [y_dev((yi + k) % ny) for k in range(1, ny)]
+    peers += [x_dev((pos_a + k) % nx) for k in range(1, nx)]
+    peers += [y_dev((pos_b + k) % ny) for k in range(1, ny)]
     peers += [z_dev((zi + k) % nh) for k in range(1, nh)]
     for dev in peers:
         pl.semaphore_signal(barrier, inc=1, device_id=dev, device_id_type=MESH)
@@ -110,8 +118,8 @@
     z_piece = lambda j: col_slice(j, cz)
 
     reduce_stage(x_ref, 2, core, core_dev, core_recv, core_sum, core_piece)
-    reduce_stage(core_sum, nx, xi, x_dev, x_recv, x_sum, x_piece)
-    reduce_stage(x_sum, ny, yi, y_dev, y_recv, y_sum, y_piece)
+    reduce_stage(core_sum, nx, pos_a, x_dev, x_recv, x_sum, x_piece)
+    reduce_stage(x_sum, ny, pos_b, y_dev, y_recv, y_sum, y_piece)
     reduce_stage(y_sum, nh, zi, z_dev, z_recv, z_sum, z_piece)
 
     s = next_sem()
@@ -123,13 +131,18 @@
     z_full[...] = z_sum[...] + pair_recv[...]
 
     gather_stage(z_full, nh, zi, z_dev, y_out, z_piece)
-    gather_stage(y_out, ny, yi, y_dev, x_out, y_piece)
-    gather_stage(x_out, nx, xi, x_dev, core_out, x_piece)
+    gather_stage(y_out, ny, pos_b, y_dev, x_out, y_piece)
+    gather_stage(x_out, nx, pos_a, x_dev, core_out, x_piece)
     gather_stage(core_out, 2, core, core_dev, out_ref, core_piece)
-
-
-def allreduce(x, nx, ny, nz):
-    rows, cols = x.shape
+    full = out_ref[...]
+    part = jnp.sum(full * full, axis=0, keepdims=True)
+    sq_ref[...] = jnp.broadcast_to(jnp.sum(part, axis=1, keepdims=True), sq_ref.shape)
+
+
+def allreduce(g, tail, nx, ny, nz):
+    assert nx == ny
+    rows = g.shape[1]
+    cols = g.shape[2] + tail.shape[1]
     nh = nz // 2
     rc = rows // 2
     rx = rc // nx
@@ -139,10 +152,11 @@
     f32 = jnp.float32
     return pl.pallas_call(
         functools.partial(_allreduce_kernel, nx, ny, nz),
-        out_shape=jax.ShapeDtypeStruct((rows, cols), f32),
-        in_specs=[pl.BlockSpec(memory_space=pltpu.VMEM)],
-        out_specs=pl.BlockSpec(memory_space=pltpu.VMEM),
+        out_shape=(jax.ShapeDtypeStruct((rows, cols), f32), jax.ShapeDtypeStruct((8, 128), f32)),
+        in_specs=[pl.BlockSpec(memory_space=pltpu.VMEM)] * 2,
+        out_specs=(pl.BlockSpec(memory_space=pltpu.VMEM),) * 2,
         scratch_shapes=[
+            pltpu.VMEM((rows, cols), f32),
             pltpu.VMEM((1, rc, cols), f32),
             pltpu.VMEM((rc, cols), f32),
             pltpu.VMEM((nx - 1, rx, cols), f32),
@@ -161,7 +175,7 @@
         ],
         compiler_params=pltpu.CompilerParams(
             collective_id=0, has_side_effects=True, vmem_limit_bytes=48 * 1024 * 1024),
-    )(x)
+    )(g, tail)
 
 
 def per_device(nx, ny, grads, vec_grads, weight, basis, moment, second, vectors, vec_moment, vec_second):
@@ -171,13 +185,12 @@
     cols = vectors.shape[1]
     vec_n = vectors.shape[0]
     me = lax.axis_index("shard")
-    summed = grads[0, 0, 0].astype(jnp.float32) + grads[1, 0, 0].astype(jnp.float32)
     vec_local = vec_grads[0, 0, 0].astype(jnp.float32) + vec_grads[1, 0, 0].astype(jnp.float32)
     lanes = 128 * (shards // 2)
     padded = lanes * ((width + vec_n + lanes - 1) // lanes)
     pad = jnp.zeros((width, padded - width - vec_n), jnp.float32)
-    packed = jnp.concatenate([summed, vec_local.T, pad], axis=1)
-    packed = allreduce(packed, nx, ny, shards)
+    tail = jnp.concatenate([vec_local.T, pad], axis=1)
+    packed, sq = allreduce(grads[:, 0, 0], tail, nx, ny, shards)
     total = packed[:, :width]
     vec_total = packed[:, width:width + vec_n].T
     projected_all = matmul(total, basis)
@@ -188,7 +201,7 @@
         precision=HIGH,
         preferred_element_type=jnp.float32,
     )
-    squares = jnp.sum(total * total) + jnp.sum(vec_total * vec_total)
+    squares = sq[0, 0]
     iterate = subspace / jnp.sqrt(jnp.sum(subspace * subspace) + 1e-06)
     for step in range(NS_STEPS):
         gram = matmul(iterate.T, iterate)

time: 126 us -> 109 us (0.87)
  Pallas kernels: 93.1 us -> 82.8 us
  matrix products: 20.1 us -> 14.1 us
  other arithmetic: 6.66 us -> 2.93 us
  local copies, waits for them, and re-layouts: 3.35 us -> 6.44 us
    pallas_call x1, Pallas kernels: 93.1 us -> 82.8 us  [allreduce(): pl.pallas_call(functools.partial(_allreduce_kernel, nx, ny, nz), out_shap...]
    dot_general x11, matrix products: 14.1 us -> 10.2 us  [matmul(): jnp.dot(left, right, precision=HIGH, preferred_element_type=jnp.float32)]
    unnamed x28 -> x20, local copies, waits for them, and re-layouts: 2.13 us -> 4.45 us
    concatenate x1 -> x0, other arithmetic: 2.11 us -> none  [per_device(): packed = jnp.concatenate([summed, vec_local.T, pad], axis=1)]
    add x1 -> x0, other arithmetic: 1.95 us -> none  [per_device(): grads[0, 0, 0].astype(jnp.float32) + grads[1, 0, 0].astype(jnp.float32)]
    dot_general x1, matrix products: 4.44 us -> 2.67 us  [per_device(): lax.dot_general(total, projected_all, (((0,), (0,)), ((), ())), precision...]
    slice x0 -> x2, local copies, waits for them, and re-layouts: none -> 1.54 us  [the longest x1 1.02 us: per_device(): vec_total = packed[:, width:width + vec_n].T]
where the time goes in v3:
time: 109 us
  Pallas kernels  82.8 us (76%)
  matrix products  14.1 us (13%)
  local copies, waits for them, and re-layouts  6.44 us (6%)
  other arithmetic  2.93 us (3%)
  between operations  2.28 us (2%)
    pallas_call x1, Pallas kernels, allreduce(): pl.pallas_call(functools.partial(_allreduce_kernel, nx, ny, nz), out_shap...  82.8 us
    dot_general x11, matrix products, matmul(): jnp.dot(left, right, precision=HIGH, preferred_element_type=jnp.float32)  10.2 us
    unnamed x20, local copies, waits for them, and re-layouts  4.45 us
    dot_general x1, matrix products, per_device(): lax.dot_general(total, projected_all, (((0,), (0,)), ((), ())), precision...  2.67 us

profile of v3, /device:TPU:1, one launch (start us, length us, event | category | flops | bytes accessed | tf_op | source)
XLA Modules:
  0.0 108.5 jit_solution(13757390905170410102)
XLA Ops:
  0.6 0.0 copy-start
  0.7 0.8 broadcast_multiply_fusion.2
  1.4 0.7 broadcast_multiply_fusion.1
  2.1 0.7 broadcast_multiply_fusion
  2.8 0.1 copy.33
  2.9 0.1 copy.32
  3.0 0.1 copy.31
  3.0 0.7 convert_add_fusion
  3.8 0.8 copy.34
  4.5 0.2 copy.29
  4.7 0.1 concatenate.3.tail_ref
  4.8 0.0 copy-start.1
  4.8 1.7 %copy-done.1 = bf16[2,1,1,768,768]{4,3,2,1,0:T(8,128)(2,1)S(1)} copy-done((bf16[2,1,1,768,768]{4,3,2,1,0:T(8,128)(2,1)S(1)}, bf16[2,1,1,768,768]{4,3,2,1,0:T(8,128)(2,1)}, u32[]{:S(2)}) %copy-start.1) | copy-done | bytes 2359320
  6.4 82.8 %shard_map.152 = (f32[768,1024]{1,0:T(8,128)}, f32[8,128]{1,0:T(8,128)S(1)}) custom-call(bf16[2,768,768]{2,1,0:T(8,128)(2,1)S(1)} %bitcast.32, f32[768,256]{1,0:T(8,128)S(1)} %concatenate.3.tail_ref), custom_call_target="tpu_custom_call" | custom-call | tf_op jit(solution)/shard_map/pallas_call | solution.py:153
  89.2 0.5 slice.17
  90.4 1.0 slice.19
  91.5 0.7 copy.35
  92.2 0.7 copy.36
  92.8 0.7 copy.37
  93.5 0.0 copy-done
  93.5 0.0 copy-start.2
  93.5 0.0 copy-start.6
  93.5 0.0 copy-start.7
  93.5 0.0 copy-start.5
  93.5 2.9 %fusion.2 = f32[768,256]{1,0:T(8,128)S(1)} fusion(f32[768,256]{1,0:T(8,128)S(1)} %copy-done, f32[768,1024]{1,0:T(8,128)} %get-tuple-element.11), kind=kOutput, calls=%fused_computation.2 | convolution fusion | flops 905969664 | bytes 3932160 | tf_op jit(solution)/shard_map/dot_general | solution.py:20
  96.4 0.0 copy-done.2
  96.4 2.7 %multiply_reduce_fusion = (f32[]{:T(128)}, f32[768,256]{1,0:T(8,128)S(1)}) fusion(f32[768,256]{1,0:T(8,128)S(1)} %fusion.2, f32[768,1024]{1,0:T(8,128)S(1)} %copy-done.2), kind=kOutput, calls=%fused_computation.14 | convolution fusion | flops 906362880 | bytes 3932164 | tf_op jit(solution)/shard_map/dot_general | solution.py:197
  99.8 0.0 copy-done.6
  99.8 0.0 copy-done.7
  99.9 0.0 copy-start.3
  99.9 0.0 copy-start.4
  99.9 0.0 copy-done.5
  99.9 1.2 %fusion.27 = (bf16[48,768]{1,0:T(8,128)(2,1)}, f32[48,768]{1,0:T(8,128)}) fusion(f32[48,768]{1,0:T(8,128)S(1)} %copy-done.5, f32[768,256]{1,0:T(8,128)S(1)} %copy-done, f32[48,256]{1,0:T(8,128)S(1)} %get-tuple-element.32, f32[48,256]{1,0:T(8,128)S(1)} %get-tuple-element.31), kind=kOutput, calls=%fused_computation.44 | convolution fusion | flops 56893440 | bytes 1253376 | tf_op jit(solution)/shard_map/dot_general | solution.py:218
  101.1 0.8 fusion.9
  101.9 0.5 fusion.8
  102.4 0.0 copy-done.3
  102.4 0.0 copy-done.4
  102.4 0.8 fusion.28
  103.2 0.5 fusion.7
  103.7 0.8 fusion.29
  104.5 0.5 fusion.6
  105.0 0.8 fusion.30
  105.8 0.5 fusion.5
  106.3 0.8 fusion.31
  107.1 1.4 %fusion.4 = f32[768,256]{1,0:T(8,128)} fusion(f32[768,256]{1,0:T(8,128)S(1)} %fusion.5, f32[256,256]{1,0:T(8,128)S(1)} %fusion.31), kind=kOutput, calls=%fused_computation.5 | convolution fusion | flops 302579712 | bytes 1835008 | tf_op jit(solution)/shard_map/dot_general | solution.py:20
  (2 shorter events, 0.1 us)
Async XLA Ops:
  0.6 92.9 %copy-start = (f32[768,256]{1,0:T(8,128)S(1)}, f32[768,256]{1,0:T(8,128)}, u32[]{:S(2)}) copy-start(f32[768,256]{1,0:T(8,128)} %param.12) | copy-start | bytes 2359300
  4.8 1.7 %copy-start.1 = (bf16[2,1,1,768,768]{4,3,2,1,0:T(8,128)(2,1)S(1)}, bf16[2,1,1,768,768]{4,3,2,1,0:T(8,128)(2,1)}, u32[]{:S(2)}) copy-start(bf16[2,1,1,768,768]{4,3,2,1,0:T(8,128)(2,1)} %param.9) | copy-start | bytes 7077892
  93.5 2.9 %copy-start.2 = (f32[768,1024]{1,0:T(8,128)S(1)}, f32[768,1024]{1,0:T(8,128)}, u32[]{:S(2)}) copy-start(f32[768,1024]{1,0:T(8,128)} %get-tuple-element.11) | copy-start | bytes 9437188
  93.5 6.3 %copy-start.6 = (f32[48,256]{1,0:T(8,128)S(1)}, f32[48,256]{1,0:T(8,128)}, u32[]{:S(2)}) copy-start(f32[48,256]{1,0:T(8,128)} %param.13) | copy-start | bytes 147460
  93.5 6.3 %copy-start.7 = (f32[48,256]{1,0:T(8,128)S(1)}, f32[48,256]{1,0:T(8,128)}, u32[]{:S(2)}) copy-start(f32[48,256]{1,0:T(8,128)} %param.14) | copy-start | bytes 147460
  93.5 6.4 %copy-start.5 = (f32[48,768]{1,0:T(8,128)S(1)}, f32[48,768]{1,0:T(8,128)}, u32[]{:S(2)}) copy-start(f32[48,768]{1,0:T(8,128)} %param.11) | copy-start | bytes 442372
  99.9 2.5 %copy-start.3 = (f32[48,256]{1,0:T(8,128)}, f32[48,256]{1,0:T(8,128)S(1)}, u32[]{:S(2)}) copy-start(f32[48,256]{1,0:T(8,128)S(1)} %get-tuple-element.31) | copy-start | bytes 147460
  99.9 2.5 %copy-start.4 = (f32[48,256]{1,0:T(8,128)}, f32[48,256]{1,0:T(8,128)S(1)}, u32[]{:S(2)}) copy-start(f32[48,256]{1,0:T(8,128)S(1)} %get-tuple-element.32) | copy-start | bytes 147460

commit v4 on v3

--- a/solution.py
+++ b/solution.py
@@ -20,14 +20,15 @@
     return jnp.dot(left, right, precision=HIGH, preferred_element_type=jnp.float32)
 
 
-def _allreduce_kernel(nx, ny, nz, g_ref, tail_ref, out_ref, sq_ref, x_ref, core_recv, core_sum, x_recv, x_sum, y_recv, y_sum,
-                      z_recv, z_sum, pair_recv, z_full, y_out, x_out, core_out, send_sem, recv_sem):
+def _allreduce_kernel(nx, ny, nz, g_ref, tail_ref, out_ref, sq_ref, x_ref, core_recv, core_sum, x_recv, x_sum, y_recv,
+                      y_pad, z_recv, z_sum, pair_recv, z_full, y_out, x_out, core_out, send_sem, recv_sem):
     rows, cols = x_ref.shape
+    zcols = y_pad.shape[1]
     width = g_ref.shape[-1]
     x_ref[:, :width] = g_ref[0].astype(jnp.float32) + g_ref[1].astype(jnp.float32)
     x_ref[:, width:] = tail_ref[...]
     nh = nz // 2
-    rc, rx, ry, cz = rows // 2, rows // 2 // nx, rows // 2 // nx // ny, cols // nh
+    rc, rx, ry, cz = rows // 2, rows // 2 // nx, rows // 2 // nx // ny, zcols // nh
     g = lax.axis_index("grp")
     z = lax.axis_index("shard")
     core = g % 2
@@ -119,8 +120,10 @@
 
     reduce_stage(x_ref, 2, core, core_dev, core_recv, core_sum, core_piece)
     reduce_stage(core_sum, nx, pos_a, x_dev, x_recv, x_sum, x_piece)
-    reduce_stage(x_sum, ny, pos_b, y_dev, y_recv, y_sum, y_piece)
-    reduce_stage(y_sum, nh, zi, z_dev, z_recv, z_sum, z_piece)
+    if zcols > cols:
+        y_pad[:, cols:] = jnp.zeros((ry, zcols - cols), jnp.float32)
+    reduce_stage(x_sum, ny, pos_b, y_dev, y_recv, y_pad.at[:, pl.ds(0, cols)], y_piece)
+    reduce_stage(y_pad, nh, zi, z_dev, z_recv, z_sum, z_piece)
 
     s = next_sem()
     c = pltpu.make_async_remote_copy(
@@ -131,7 +134,7 @@
     z_full[...] = z_sum[...] + pair_recv[...]
 
     gather_stage(z_full, nh, zi, z_dev, y_out, z_piece)
-    gather_stage(y_out, ny, pos_b, y_dev, x_out, y_piece)
+    gather_stage(y_out.at[:, pl.ds(0, cols)], ny, pos_b, y_dev, x_out, y_piece)
     gather_stage(x_out, nx, pos_a, x_dev, core_out, x_piece)
     gather_stage(core_out, 2, core, core_dev, out_ref, core_piece)
     full = out_ref[...]
@@ -147,7 +150,8 @@
     rc = rows // 2
     rx = rc // nx
     ry = rx // ny
-    cz = cols // nh
+    zcols = 128 * nh * ((cols + 128 * nh - 1) // (128 * nh))
+    cz = zcols // nh
     n_sems = 2 * (1 + (nx - 1) + (ny - 1) + (nh - 1)) + 1
     f32 = jnp.float32
     return pl.pallas_call(
@@ -162,12 +166,12 @@
             pltpu.VMEM((nx - 1, rx, cols), f32),
             pltpu.VMEM((rx, cols), f32),
             pltpu.VMEM((ny - 1, ry, cols), f32),
-            pltpu.VMEM((ry, cols), f32),
+            pltpu.VMEM((ry, zcols), f32),
             pltpu.VMEM((nh - 1, ry, cz), f32),
             pltpu.VMEM((ry, cz), f32),
             pltpu.VMEM((ry, cz), f32),
             pltpu.VMEM((ry, cz), f32),
-            pltpu.VMEM((ry, cols), f32),
+            pltpu.VMEM((ry, zcols), f32),
             pltpu.VMEM((rx, cols), f32),
             pltpu.VMEM((rc, cols), f32),
             pltpu.SemaphoreType.DMA((n_sems,)),
@@ -186,8 +190,7 @@
     vec_n = vectors.shape[0]
     me = lax.axis_index("shard")
     vec_local = vec_grads[0, 0, 0].astype(jnp.float32) + vec_grads[1, 0, 0].astype(jnp.float32)
-    lanes = 128 * (shards // 2)
-    padded = lanes * ((width + vec_n + lanes - 1) // lanes)
+    padded = 128 * ((width + vec_n + 127) // 128)
     pad = jnp.zeros((width, padded - width - vec_n), jnp.float32)
     tail = jnp.concatenate([vec_local.T, pad], axis=1)
     packed, sq = allreduce(grads[:, 0, 0], tail, nx, ny, shards)

time: 109 us -> 110 us (level)
  Pallas kernels: 82.8 us -> 77.6 us
  local copies, waits for them, and re-layouts: 6.44 us -> 10.1 us
  other arithmetic: 2.93 us -> 4.39 us
  matrix products: 14.1 us -> 15.5 us
    pallas_call x1, Pallas kernels: 82.8 us -> 77.6 us  [allreduce(): pl.pallas_call(functools.partial(_allreduce_kernel, nx, ny, nz), out_shap...]
    unnamed x20 -> x24, local copies, waits for them, and re-layouts: 4.45 us -> 7.28 us
where the time goes in v4:
time: 110 us
  Pallas kernels  77.6 us (71%)
  matrix products  15.5 us (14%)
  local copies, waits for them, and re-layouts  10.1 us (9%)
  other arithmetic  4.39 us (4%)
  between operations  2.39 us (2%)
    pallas_call x1, Pallas kernels, allreduce(): pl.pallas_call(functools.partial(_allreduce_kernel, nx, ny, nz), out_shap...  77.6 us
    dot_general x11, matrix products, matmul(): jnp.dot(left, right, precision=HIGH, preferred_element_type=jnp.float32)  9.8 us
    unnamed x24, local copies, waits for them, and re-layouts  7.28 us
    dot_general x1, matrix products, per_device(): lax.dot_general(total, projected_all, (((0,), (0,)), ((), ())), precision...  3.54 us

profile of v4, /device:TPU:1, one launch (start us, length us, event | category | flops | bytes accessed | tf_op | source)
XLA Modules:
  0.0 109.9 jit_solution(18428687345300220358)
XLA Ops:
  0.6 0.0 copy-start
  0.7 0.8 broadcast_multiply_fusion.2
  1.4 0.7 broadcast_multiply_fusion.1
  2.1 0.7 broadcast_multiply_fusion
  2.8 0.7 copy.33
  3.5 0.7 copy.32
  4.2 0.7 copy.31
  4.9 0.7 convert_add_fusion
  5.6 1.4 %copy.34 = f32[8,48]{0,1:T(8,128)} copy(f32[8,48]{1,0:T(8,128)} %param.15) | data formatting | bytes 3072 | tf_op args[6]
  7.0 0.2 copy.29
  7.1 0.0 copy-start.6
  7.1 0.0 copy-start.7
  7.1 0.0 copy-start.8
  7.2 0.0 copy-start.9
  7.2 0.0 copy-start.1
  7.2 1.7 %copy-done.1 = bf16[2,1,1,768,768]{4,3,2,1,0:T(8,128)(2,1)S(1)} copy-done((bf16[2,1,1,768,768]{4,3,2,1,0:T(8,128)(2,1)S(1)}, bf16[2,1,1,768,768]{4,3,2,1,0:T(8,128)(2,1)}, u32[]{:S(2)}) %copy-start.1) | copy-done | bytes 2359320
  8.9 77.6 %shard_map.152 = (f32[768,896]{1,0:T(8,128)S(1)}, f32[8,128]{1,0:T(8,128)S(1)}) custom-call(bf16[2,768,768]{2,1,0:T(8,128)(2,1)S(1)} %bitcast.32, f32[768,128]{1,0:T(8,128)S(1)} %concatenate.3.tail_ref), custom_call_target="tpu_custom_call" | custom-call | tf_op jit(solution)/shard_map/pallas_call | solution.py:157
  86.4 0.5 slice.17
  87.7 0.0 copy-done.6
  87.7 0.0 copy-done.7
  87.7 0.0 copy-done.8
  87.7 0.0 copy-done.9
  87.8 0.6 multiply_subtract_fusion.1
  88.4 1.4 %copy.35 = f32[8,48]{1,0:T(8,128)} copy(f32[8,48]{0,1:T(8,128)} %get-tuple-element.28) | data formatting | bytes 3072
  89.8 1.4 %copy.36 = f32[8,48]{1,0:T(8,128)} copy(f32[8,48]{0,1:T(8,128)} %get-tuple-element.29) | data formatting | bytes 3072
  91.2 1.4 %copy.37 = f32[8,48]{1,0:T(8,128)} copy(f32[8,48]{0,1:T(8,128)} %get-tuple-element.30) | data formatting | bytes 3072
  92.6 0.0 copy-done
  92.6 1.1 %fusion.2 = f32[768,256]{1,0:T(8,128)S(1)} fusion(f32[768,256]{1,0:T(8,128)S(1)} %copy-done, f32[768,896]{1,0:T(8,128)S(1)} %get-tuple-element.11), kind=kOutput, calls=%fused_computation.2 | convolution fusion | flops 905969664 | bytes 3932160 | tf_op jit(solution)/shard_map/dot_general | solution.py:20
  93.7 0.0 copy-start.2
  93.7 3.5 %multiply_reduce_fusion = (f32[]{:T(128)}, f32[768,256]{1,0:T(8,128)}) fusion(f32[768,256]{1,0:T(8,128)S(1)} %fusion.2, f32[768,896]{1,0:T(8,128)S(1)} %get-tuple-element.11), kind=kOutput, calls=%fused_computation.14 | convolution fusion | flops 906362880 | bytes 3932164 | tf_op jit(solution)/shard_map/dot_general | solution.py:200
  97.3 0.0 copy-done.2
  98.0 0.9 multiply_add_fusion
  98.9 0.0 copy-start.4
  98.9 0.0 copy-start.5
  98.9 2.1 %fusion.27 = (bf16[48,768]{1,0:T(8,128)(2,1)}, f32[48,768]{1,0:T(8,128)}) fusion(f32[48,768]{1,0:T(8,128)} %param.11, f32[768,256]{1,0:T(8,128)S(1)} %copy-done, f32[48,256]{1,0:T(8,128)S(1)} %get-tuple-element.32, f32[48,256]{1,0:T(8,128)S(1)} %get-tuple-element.31), kind=kOutput, calls=%fused_computation.44 | convolution fusion | flops 56893440 | bytes 1253376 | tf_op jit(solution)/shard_map/dot_general | solution.py:221
  101.1 2.2 %fusion.9 = f32[256,256]{1,0:T(8,128)S(1)} fusion(f32[768,256]{1,0:T(8,128)} %get-tuple-element.36, f32[]{:T(128)S(6)} %sqrt.15), kind=kOutput, calls=%fused_computation.16 | convolution fusion | flops 302186496 | bytes 1048580 | tf_op jit(solution)/shard_map/dot_general | solution.py:20
  103.2 0.0 copy-done.3
  103.3 0.5 fusion.8
  103.8 0.0 copy-done.4
  103.8 0.0 copy-done.5
  103.8 0.8 fusion.28
  104.6 0.5 fusion.7
  105.1 0.8 fusion.29
  105.9 0.5 fusion.6
  106.4 0.8 fusion.30
  107.2 0.5 fusion.5
  107.7 0.8 fusion.31
  108.5 1.4 %fusion.4 = f32[768,256]{1,0:T(8,128)} fusion(f32[768,256]{1,0:T(8,128)S(1)} %fusion.5, f32[256,256]{1,0:T(8,128)S(1)} %fusion.31), kind=kOutput, calls=%fused_computation.5 | convolution fusion | flops 302579712 | bytes 1835008 | tf_op jit(solution)/shard_map/dot_general | solution.py:20
  (3 shorter events, 0.1 us)
Async XLA Ops:
  0.6 92.0 %copy-start = (f32[768,256]{1,0:T(8,128)S(1)}, f32[768,256]{1,0:T(8,128)}, u32[]{:S(2)}) copy-start(f32[768,256]{1,0:T(8,128)} %param.12) | copy-start | bytes 2359300
  7.1 80.6 %copy-start.6 = (f32[8,48]{0,1:T(8,128)S(1)}, f32[8,48]{0,1:T(8,128)}, u32[]{:S(2)}) copy-start(f32[8,48]{0,1:T(8,128)} %copy.33) | copy-start | bytes 4612
  7.1 80.6 %copy-start.7 = (f32[8,48]{0,1:T(8,128)S(1)}, f32[8,48]{0,1:T(8,128)}, u32[]{:S(2)}) copy-start(f32[8,48]{0,1:T(8,128)} %copy.32) | copy-start | bytes 4612
  7.1 80.6 %copy-start.8 = (f32[8,48]{0,1:T(8,128)S(1)}, f32[8,48]{0,1:T(8,128)}, u32[]{:S(2)}) copy-start(f32[8,48]{0,1:T(8,128)} %copy.31) | copy-start | bytes 4612
  7.2 80.6 %copy-start.9 = (f32[8,48]{0,1:T(8,128)S(1)}, f32[8,48]{0,1:T(8,128)}, u32[]{:S(2)}) copy-start(f32[8,48]{0,1:T(8,128)} %copy.34) | copy-start | bytes 4612
  7.2 1.7 %copy-start.1 = (bf16[2,1,1,768,768]{4,3,2,1,0:T(8,128)(2,1)S(1)}, bf16[2,1,1,768,768]{4,3,2,1,0:T(8,128)(2,1)}, u32[]{:S(2)}) copy-start(bf16[2,1,1,768,768]{4,3,2,1,0:T(8,128)(2,1)} %param.9) | copy-start | bytes 7077892
  93.7 3.6 %copy-start.2 = (f32[768,256]{1,0:T(8,128)}, f32[768,256]{1,0:T(8,128)S(1)}, u32[]{:S(2)}) copy-start(f32[768,256]{1,0:T(8,128)S(1)} %fusion.2) | copy-start | bytes 2359300
  97.3 6.0 %copy-start.3 = (f32[768,256]{1,0:T(8,128)S(1)}, f32[768,256]{1,0:T(8,128)}, u32[]{:S(2)}) copy-start(f32[768,256]{1,0:T(8,128)} %get-tuple-element.36) | copy-start | bytes 2359300
  98.9 4.8 %copy-start.4 = (f32[48,256]{1,0:T(8,128)}, f32[48,256]{1,0:T(8,128)S(1)}, u32[]{:S(2)}) copy-start(f32[48,256]{1,0:T(8,128)S(1)} %get-tuple-element.31) | copy-start | bytes 147460
  98.9 4.8 %copy-start.5 = (f32[48,256]{1,0:T(8,128)}, f32[48,256]{1,0:T(8,128)S(1)}, u32[]{:S(2)}) copy-start(f32[48,256]{1,0:T(8,128)S(1)} %get-tuple-element.32) | copy-start | bytes 147460

commit v5 on v4

--- a/solution.py
+++ b/solution.py
@@ -190,12 +190,11 @@
     vec_n = vectors.shape[0]
     me = lax.axis_index("shard")
     vec_local = vec_grads[0, 0, 0].astype(jnp.float32) + vec_grads[1, 0, 0].astype(jnp.float32)
-    padded = 128 * ((width + vec_n + 127) // 128)
-    pad = jnp.zeros((width, padded - width - vec_n), jnp.float32)
-    tail = jnp.concatenate([vec_local.T, pad], axis=1)
+    lanes = 128 * ((cols + 127) // 128)
+    placed = vec_local.reshape(vec_n, shards, cols).transpose(1, 0, 2).reshape(shards * vec_n, cols)
+    tail = jnp.pad(placed, ((0, width - shards * vec_n), (0, lanes - cols)))
     packed, sq = allreduce(grads[:, 0, 0], tail, nx, ny, shards)
     total = packed[:, :width]
-    vec_total = packed[:, width:width + vec_n].T
     projected_all = matmul(total, basis)
     subspace = lax.dot_general(
         total,
@@ -209,9 +208,9 @@
     for step in range(NS_STEPS):
         gram = matmul(iterate.T, iterate)
         iterate = 1.5 * iterate - 0.5 * matmul(iterate, gram)
-    factor = 1.0 / jnp.maximum(jnp.sqrt(squares / (width * width + vec_total.size)), 1.0)
+    factor = 1.0 / jnp.maximum(jnp.sqrt(squares / (width * width + vec_n * width)), 1.0)
     projected = lax.dynamic_slice_in_dim(projected_all, me * rows, rows, axis=0)
-    vec_sum = lax.dynamic_slice_in_dim(vec_total, me * cols, cols, axis=1)
+    vec_sum = lax.dynamic_slice(packed, (me * vec_n, width), (vec_n, cols))
     first_fix = 1.0 - 0.9**STEP
     second_fix = 1.0 - 0.999**STEP
     grad_low = factor * projected

time: 110 us -> 96.1 us (0.87)
  local copies, waits for them, and re-layouts: 10.1 us -> 2.37 us
  matrix products: 15.5 us -> 12.2 us
  other arithmetic: 4.39 us -> 1.45 us
    unnamed x24 -> x20, local copies, waits for them, and re-layouts: 7.28 us -> 1.71 us
    mul x3 -> x0, other arithmetic: 2.14 us -> none  [the longest x1 0.76 us: per_device(): new_vec_moment = 0.9 * vec_moment + 0.1 * vec_grad]
    mul x3 -> x0, local copies, waits for them, and re-layouts: 2.06 us -> none  [the longest x1 0.69 us: per_device(): new_vectors = vectors - 0.001 * (vec_step + 0.01 * vectors)]
    dot_general x11, matrix products: 9.8 us -> 8.41 us  [matmul(): jnp.dot(left, right, precision=HIGH, preferred_element_type=jnp.float32)]
where the time goes in v5:
time: 96.1 us; the launch traced here: 95.9 us
  Pallas kernels  77.6 us (81%)
  matrix products  12.2 us (13%)
  local copies, waits for them, and re-layouts  2.37 us (2%)
  between operations  2.33 us (2%)
  other arithmetic  1.45 us (2%)
    pallas_call x1, Pallas kernels, allreduce(): pl.pallas_call(functools.partial(_allreduce_kernel, nx, ny, nz), out_shap...  77.6 us
    dot_general x11, matrix products, matmul(): jnp.dot(left, right, precision=HIGH, preferred_element_type=jnp.float32)  8.41 us
    dot_general x1, matrix products, per_device(): lax.dot_general(total, projected_all, (((0,), (0,)), ((), ())), precision...  2.63 us

profile of v5, /device:TPU:1, one launch (start us, length us, event | category | flops | bytes accessed | tf_op | source)
XLA Modules:
  0.0 95.9 jit_solution(11688528663295807186)
XLA Ops:
  0.6 0.0 copy-start
  0.6 0.0 copy-start.9
  0.7 0.0 copy-start.8
  0.7 0.0 copy-start.7
  0.7 0.8 convert_add_fusion
  1.5 0.1 add.49
  1.6 0.0 copy-start.1
  1.7 1.7 %copy-done.1 = bf16[2,1,1,768,768]{4,3,2,1,0:T(8,128)(2,1)S(1)} copy-done((bf16[2,1,1,768,768]{4,3,2,1,0:T(8,128)(2,1)S(1)}, bf16[2,1,1,768,768]{4,3,2,1,0:T(8,128)(2,1)}, u32[]{:S(2)}) %copy-start.1) | copy-done | bytes 2359320
  3.3 77.6 %shard_map.152 = (f32[768,896]{1,0:T(8,128)S(1)}, f32[8,128]{1,0:T(8,128)S(1)}) custom-call(bf16[2,768,768]{2,1,0:T(8,128)(2,1)S(1)} %bitcast.29, f32[768,128]{1,0:T(8,128)S(1)} %pad.4.tail_ref), custom_call_target="tpu_custom_call" | custom-call | tf_op jit(solution)/shard_map/pallas_call | solution.py:157
  80.9 0.5 slice.14
  82.1 0.0 copy-done.9
  82.1 0.0 copy-done.8
  82.1 0.0 copy-done.7
  82.1 0.6 multiply_subtract_fusion.1
  82.8 0.0 copy-done
  82.8 1.1 %fusion.2 = f32[768,256]{1,0:T(8,128)S(1)} fusion(f32[768,256]{1,0:T(8,128)S(1)} %copy-done, f32[768,896]{1,0:T(8,128)S(1)} %get-tuple-element.11), kind=kOutput, calls=%fused_computation.2 | convolution fusion | flops 905969664 | bytes 3932160 | tf_op jit(solution)/shard_map/dot_general | solution.py:20
  83.9 0.0 copy-start.5
  83.9 0.0 copy-start.6
  83.9 0.0 copy-start.4
  83.9 2.6 %multiply_reduce_fusion = (f32[]{:T(128)}, f32[768,256]{1,0:T(8,128)S(1)}) fusion(f32[768,256]{1,0:T(8,128)S(1)} %fusion.2, f32[768,896]{1,0:T(8,128)S(1)} %get-tuple-element.11), kind=kOutput, calls=%fused_computation.14 | convolution fusion | flops 906362880 | bytes 3932164 | tf_op jit(solution)/shard_map/dot_general | solution.py:199
  87.2 0.0 copy-done.5
  87.2 0.0 copy-done.6
  87.3 0.0 copy-start.2
  87.3 0.0 copy-start.3
  87.3 0.0 copy-done.4
  87.3 1.2 %fusion.25 = (bf16[48,768]{1,0:T(8,128)(2,1)}, f32[48,768]{1,0:T(8,128)}) fusion(f32[48,768]{1,0:T(8,128)S(1)} %copy-done.4, f32[768,256]{1,0:T(8,128)S(1)} %copy-done, f32[48,256]{1,0:T(8,128)S(1)} %get-tuple-element.16, f32[48,256]{1,0:T(8,128)S(1)} %get-tuple-element.15), kind=kOutput, calls=%fused_computation.41 | convolution fusion | flops 56893440 | bytes 1253376 | tf_op jit(solution)/shard_map/dot_general | solution.py:220
  88.5 0.8 fusion.9
  89.3 0.5 fusion.8
  89.8 0.0 copy-done.2
  89.8 0.0 copy-done.3
  89.8 0.8 fusion.26
  90.7 0.5 fusion.7
  91.1 0.8 fusion.27
  92.0 0.5 fusion.6
  92.5 0.8 fusion.28
  93.3 0.5 fusion.5
  93.8 0.8 fusion.29
  94.6 1.4 %fusion.4 = f32[768,256]{1,0:T(8,128)} fusion(f32[768,256]{1,0:T(8,128)S(1)} %fusion.5, f32[256,256]{1,0:T(8,128)S(1)} %fusion.29), kind=kOutput, calls=%fused_computation.5 | convolution fusion | flops 302579712 | bytes 1835008 | tf_op jit(solution)/shard_map/dot_general | solution.py:20
  (3 shorter events, 0.1 us)
Async XLA Ops:
  0.6 82.1 %copy-start = (f32[768,256]{1,0:T(8,128)S(1)}, f32[768,256]{1,0:T(8,128)}, u32[]{:S(2)}) copy-start(f32[768,256]{1,0:T(8,128)} %param.12) | copy-start | bytes 2359300
  0.6 81.5 %copy-start.9 = (f32[8,48]{1,0:T(8,128)S(1)}, f32[8,48]{1,0:T(8,128)}, u32[]{:S(2)}) copy-start(f32[8,48]{1,0:T(8,128)} %param.17) | copy-start | bytes 4612
  0.7 81.5 %copy-start.8 = (f32[8,48]{1,0:T(8,128)S(1)}, f32[8,48]{1,0:T(8,128)}, u32[]{:S(2)}) copy-start(f32[8,48]{1,0:T(8,128)} %param.16) | copy-start | bytes 4612
  0.7 81.5 %copy-start.7 = (f32[8,48]{1,0:T(8,128)S(1)}, f32[8,48]{1,0:T(8,128)}, u32[]{:S(2)}) copy-start(f32[8,48]{1,0:T(8,128)} %param.15) | copy-start | bytes 4612
  1.6 1.7 %copy-start.1 = (bf16[2,1,1,768,768]{4,3,2,1,0:T(8,128)(2,1)S(1)}, bf16[2,1,1,768,768]{4,3,2,1,0:T(8,128)(2,1)}, u32[]{:S(2)}) copy-start(bf16[2,1,1,768,768]{4,3,2,1,0:T(8,128)(2,1)} %param.9) | copy-start | bytes 7077892
  83.9 3.4 %copy-start.5 = (f32[48,256]{1,0:T(8,128)S(1)}, f32[48,256]{1,0:T(8,128)}, u32[]{:S(2)}) copy-start(f32[48,256]{1,0:T(8,128)} %param.13) | copy-start | bytes 147460
  83.9 3.4 %copy-start.6 = (f32[48,256]{1,0:T(8,128)S(1)}, f32[48,256]{1,0:T(8,128)}, u32[]{:S(2)}) copy-start(f32[48,256]{1,0:T(8,128)} %param.14) | copy-start | bytes 147460
  83.9 3.4 %copy-start.4 = (f32[48,768]{1,0:T(8,128)S(1)}, f32[48,768]{1,0:T(8,128)}, u32[]{:S(2)}) copy-start(f32[48,768]{1,0:T(8,128)} %param.11) | copy-start | bytes 442372
  87.3 2.5 %copy-start.2 = (f32[48,256]{1,0:T(8,128)}, f32[48,256]{1,0:T(8,128)S(1)}, u32[]{:S(2)}) copy-start(f32[48,256]{1,0:T(8,128)S(1)} %get-tuple-element.15) | copy-start | bytes 147460
  87.3 2.5 %copy-start.3 = (f32[48,256]{1,0:T(8,128)}, f32[48,256]{1,0:T(8,128)S(1)}, u32[]{:S(2)}) copy-start(f32[48,256]{1,0:T(8,128)S(1)} %get-tuple-element.16) | copy-start | bytes 147460

commit v6 on v5

--- a/solution.py
+++ b/solution.py
@@ -25,8 +25,6 @@
     rows, cols = x_ref.shape
     zcols = y_pad.shape[1]
     width = g_ref.shape[-1]
-    x_ref[:, :width] = g_ref[0].astype(jnp.float32) + g_ref[1].astype(jnp.float32)
-    x_ref[:, width:] = tail_ref[...]
     nh = nz // 2
     rc, rx, ry, cz = rows // 2, rows // 2 // nx, rows // 2 // nx // ny, zcols // nh
     g = lax.axis_index("grp")
@@ -63,7 +61,12 @@
     peers += [z_dev((zi + k) % nh) for k in range(1, nh)]
     for dev in peers:
         pl.semaphore_signal(barrier, inc=1, device_id=dev, device_id_type=MESH)
-    pl.semaphore_wait(barrier, len(peers))
+
+    def pack(j):
+        r = pl.ds(pl.multiple_of(j * (rows // 2), 8), rows // 2)
+        x_ref[r, :width] = g_ref[0, r, :].astype(jnp.float32) + g_ref[1, r, :].astype(jnp.float32)
+        x_ref[r, width:] = tail_ref[r, :]
+
 
     counter = [0]
 
@@ -118,7 +121,16 @@
     y_piece = lambda j: row_slice(j, ry)
     z_piece = lambda j: col_slice(j, cz)
 
-    reduce_stage(x_ref, 2, core, core_dev, core_recv, core_sum, core_piece)
+    pack(1 - core)
+    pl.semaphore_wait(barrier, len(peers))
+    s = next_sem()
+    c = pltpu.make_async_remote_copy(
+        src_ref=x_ref.at[core_piece(1 - core)], dst_ref=core_recv.at[0], send_sem=send_sem.at[s],
+        recv_sem=recv_sem.at[s], device_id=core_dev(0), device_id_type=MESH)
+    c.start()
+    pack(core)
+    c.wait()
+    core_sum[...] = x_ref[core_piece(core)] + core_recv[0]
     reduce_stage(core_sum, nx, pos_a, x_dev, x_recv, x_sum, x_piece)
     if zcols > cols:
         y_pad[:, cols:] = jnp.zeros((ry, zcols - cols), jnp.float32)
@@ -136,10 +148,21 @@
     gather_stage(z_full, nh, zi, z_dev, y_out, z_piece)
     gather_stage(y_out.at[:, pl.ds(0, cols)], ny, pos_b, y_dev, x_out, y_piece)
     gather_stage(x_out, nx, pos_a, x_dev, core_out, x_piece)
-    gather_stage(core_out, 2, core, core_dev, out_ref, core_piece)
-    full = out_ref[...]
-    part = jnp.sum(full * full, axis=0, keepdims=True)
-    sq_ref[...] = jnp.broadcast_to(jnp.sum(part, axis=1, keepdims=True), sq_ref.shape)
+    s = next_sem()
+    c = pltpu.make_async_remote_copy(
+        src_ref=core_out, dst_ref=out_ref.at[core_piece(core)], send_sem=send_sem.at[s],
+        recv_sem=recv_sem.at[s], device_id=core_dev(0), device_id_type=MESH)
+    c.start()
+    mine = core_out[...]
+    out_ref[core_piece(core)] = mine
+    own = jnp.sum(jnp.sum(mine * mine, axis=0, keepdims=True), axis=1, keepdims=True)
+    c.wait_send()
+    pltpu.make_async_remote_copy(
+        src_ref=core_out, dst_ref=out_ref.at[core_piece(1 - core)], send_sem=send_sem.at[s],
+        recv_sem=recv_sem.at[s], device_id=core_dev(0), device_id_type=MESH).wait_recv()
+    other = out_ref[core_piece(1 - core)]
+    rest = jnp.sum(jnp.sum(other * other, axis=0, keepdims=True), axis=1, keepdims=True)
+    sq_ref[...] = jnp.broadcast_to(own + rest, sq_ref.shape)
 
 
 def allreduce(g, tail, nx, ny, nz):

time: 96.1 us -> 95.8 us (level)
  no operation moved by 1% of the time
where the time goes in v6:
time: 95.8 us; the launch traced here: 95.6 us
  Pallas kernels  77.2 us (81%)
  matrix products  12.2 us (13%)
  local copies, waits for them, and re-layouts  2.37 us (2%)
  between operations  2.33 us (2%)
  other arithmetic  1.45 us (2%)
    pallas_call x1, Pallas kernels, allreduce(): pl.pallas_call(functools.partial(_allreduce_kernel, nx, ny, nz), out_shap...  77.2 us
    dot_general x11, matrix products, matmul(): jnp.dot(left, right, precision=HIGH, preferred_element_type=jnp.float32)  8.42 us
    dot_general x1, matrix products, per_device(): lax.dot_general(total, projected_all, (((0,), (0,)), ((), ())), precision...  2.63 us

profile of v6, /device:TPU:1, one launch (start us, length us, event | category | flops | bytes accessed | tf_op | source)
XLA Modules:
  0.0 95.6 jit_solution(2226229715635171977)
XLA Ops:
  0.6 0.0 copy-start
  0.6 0.0 copy-start.9
  0.7 0.0 copy-start.8
  0.7 0.0 copy-start.7
  0.7 0.8 convert_add_fusion
  1.5 0.1 add.49
  1.6 0.0 copy-start.1
  1.7 1.7 %copy-done.1 = bf16[2,1,1,768,768]{4,3,2,1,0:T(8,128)(2,1)S(1)} copy-done((bf16[2,1,1,768,768]{4,3,2,1,0:T(8,128)(2,1)S(1)}, bf16[2,1,1,768,768]{4,3,2,1,0:T(8,128)(2,1)}, u32[]{:S(2)}) %copy-start.1) | copy-done | bytes 2359320
  3.3 77.2 %shard_map.152 = (f32[768,896]{1,0:T(8,128)S(1)}, f32[8,128]{1,0:T(8,128)S(1)}) custom-call(bf16[2,768,768]{2,1,0:T(8,128)(2,1)S(1)} %bitcast.29, f32[768,128]{1,0:T(8,128)S(1)} %pad.4.tail_ref), custom_call_target="tpu_custom_call" | custom-call | tf_op jit(solution)/shard_map/pallas_call | solution.py:180
  80.5 0.5 slice.14
  81.8 0.0 copy-done.9
  81.8 0.0 copy-done.8
  81.8 0.0 copy-done.7
  81.8 0.6 multiply_subtract_fusion.1
  82.4 0.0 copy-done
  82.4 1.1 %fusion.2 = f32[768,256]{1,0:T(8,128)S(1)} fusion(f32[768,256]{1,0:T(8,128)S(1)} %copy-done, f32[768,896]{1,0:T(8,128)S(1)} %get-tuple-element.11), kind=kOutput, calls=%fused_computation.2 | convolution fusion | flops 905969664 | bytes 3932160 | tf_op jit(solution)/shard_map/dot_general | solution.py:20
  83.5 0.0 copy-start.5
  83.5 0.0 copy-start.6
  83.5 0.0 copy-start.4
  83.6 2.6 %multiply_reduce_fusion = (f32[]{:T(128)}, f32[768,256]{1,0:T(8,128)S(1)}) fusion(f32[768,256]{1,0:T(8,128)S(1)} %fusion.2, f32[768,896]{1,0:T(8,128)S(1)} %get-tuple-element.11), kind=kOutput, calls=%fused_computation.14 | convolution fusion | flops 906362880 | bytes 3932164 | tf_op jit(solution)/shard_map/dot_general | solution.py:222
  86.9 0.0 copy-done.5
  86.9 0.0 copy-done.6
  86.9 0.0 copy-start.2
  86.9 0.0 copy-start.3
  87.0 0.0 copy-done.4
  87.0 1.2 %fusion.25 = (bf16[48,768]{1,0:T(8,128)(2,1)}, f32[48,768]{1,0:T(8,128)}) fusion(f32[48,768]{1,0:T(8,128)S(1)} %copy-done.4, f32[768,256]{1,0:T(8,128)S(1)} %copy-done, f32[48,256]{1,0:T(8,128)S(1)} %get-tuple-element.16, f32[48,256]{1,0:T(8,128)S(1)} %get-tuple-element.15), kind=kOutput, calls=%fused_computation.41 | convolution fusion | flops 56893440 | bytes 1253376 | tf_op jit(solution)/shard_map/dot_general | solution.py:243
  88.2 0.8 fusion.9
  89.0 0.5 fusion.8
  89.5 0.0 copy-done.2
  89.5 0.0 copy-done.3
  89.5 0.8 fusion.26
  90.3 0.5 fusion.7
  90.8 0.8 fusion.27
  91.6 0.5 fusion.6
  92.1 0.8 fusion.28
  92.9 0.5 fusion.5
  93.4 0.8 fusion.29
  94.2 1.4 %fusion.4 = f32[768,256]{1,0:T(8,128)} fusion(f32[768,256]{1,0:T(8,128)S(1)} %fusion.5, f32[256,256]{1,0:T(8,128)S(1)} %fusion.29), kind=kOutput, calls=%fused_computation.5 | convolution fusion | flops 302579712 | bytes 1835008 | tf_op jit(solution)/shard_map/dot_general | solution.py:20
  (3 shorter events, 0.1 us)
Async XLA Ops:
  0.6 81.8 %copy-start = (f32[768,256]{1,0:T(8,128)S(1)}, f32[768,256]{1,0:T(8,128)}, u32[]{:S(2)}) copy-start(f32[768,256]{1,0:T(8,128)} %param.12) | copy-start | bytes 2359300
  0.6 81.1 %copy-start.9 = (f32[8,48]{1,0:T(8,128)S(1)}, f32[8,48]{1,0:T(8,128)}, u32[]{:S(2)}) copy-start(f32[8,48]{1,0:T(8,128)} %param.17) | copy-start | bytes 4612
  0.7 81.1 %copy-start.8 = (f32[8,48]{1,0:T(8,128)S(1)}, f32[8,48]{1,0:T(8,128)}, u32[]{:S(2)}) copy-start(f32[8,48]{1,0:T(8,128)} %param.16) | copy-start | bytes 4612
  0.7 81.1 %copy-start.7 = (f32[8,48]{1,0:T(8,128)S(1)}, f32[8,48]{1,0:T(8,128)}, u32[]{:S(2)}) copy-start(f32[8,48]{1,0:T(8,128)} %param.15) | copy-start | bytes 4612
  1.6 1.7 %copy-start.1 = (bf16[2,1,1,768,768]{4,3,2,1,0:T(8,128)(2,1)S(1)}, bf16[2,1,1,768,768]{4,3,2,1,0:T(8,128)(2,1)}, u32[]{:S(2)}) copy-start(bf16[2,1,1,768,768]{4,3,2,1,0:T(8,128)(2,1)} %param.9) | copy-start | bytes 7077892
  83.5 3.4 %copy-start.5 = (f32[48,256]{1,0:T(8,128)S(1)}, f32[48,256]{1,0:T(8,128)}, u32[]{:S(2)}) copy-start(f32[48,256]{1,0:T(8,128)} %param.13) | copy-start | bytes 147460
  83.5 3.4 %copy-start.6 = (f32[48,256]{1,0:T(8,128)S(1)}, f32[48,256]{1,0:T(8,128)}, u32[]{:S(2)}) copy-start(f32[48,256]{1,0:T(8,128)} %param.14) | copy-start | bytes 147460
  83.5 3.4 %copy-start.4 = (f32[48,768]{1,0:T(8,128)S(1)}, f32[48,768]{1,0:T(8,128)}, u32[]{:S(2)}) copy-start(f32[48,768]{1,0:T(8,128)} %param.11) | copy-start | bytes 442372
  86.9 2.5 %copy-start.2 = (f32[48,256]{1,0:T(8,128)}, f32[48,256]{1,0:T(8,128)S(1)}, u32[]{:S(2)}) copy-start(f32[48,256]{1,0:T(8,128)S(1)} %get-tuple-element.15) | copy-start | bytes 147460
  86.9 2.5 %copy-start.3 = (f32[48,256]{1,0:T(8,128)}, f32[48,256]{1,0:T(8,128)S(1)}, u32[]{:S(2)}) copy-start(f32[48,256]{1,0:T(8,128)S(1)} %get-tuple-element.16) | copy-start | bytes 147460

commit v7 on v6

--- a/solution.py
+++ b/solution.py
@@ -20,7 +20,7 @@
     return jnp.dot(left, right, precision=HIGH, preferred_element_type=jnp.float32)
 
 
-def _allreduce_kernel(nx, ny, nz, g_ref, tail_ref, out_ref, sq_ref, x_ref, core_recv, core_sum, x_recv, x_sum, y_recv,
+def _allreduce_kernel(nx, ny, nz, g_hbm, tail_ref, out_ref, sq_ref, g_ref, in_sem, x_ref, core_recv, core_sum, x_recv, x_sum, y_recv,
                       y_pad, z_recv, z_sum, pair_recv, z_full, y_out, x_out, core_out, send_sem, recv_sem):
     rows, cols = x_ref.shape
     zcols = y_pad.shape[1]
@@ -53,6 +53,14 @@
         return (g, zp + 2 * j)
 
     pair_dev = (g, z + 1 - 2 * zp)
+
+    half = rows // 2
+    loads = []
+    for j in (1 - core, core):
+        r = pl.ds(pl.multiple_of(j * half, 8), half)
+        load = pltpu.make_async_copy(g_hbm.at[:, r, :], g_ref.at[:, r, :], in_sem.at[len(loads)])
+        load.start()
+        loads.append(load)
 
     barrier = pltpu.get_barrier_semaphore()
     peers = [core_dev(0), pair_dev]
@@ -121,6 +129,7 @@
     y_piece = lambda j: row_slice(j, ry)
     z_piece = lambda j: col_slice(j, cz)
 
+    loads[0].wait()
     pack(1 - core)
     pl.semaphore_wait(barrier, len(peers))
     s = next_sem()
@@ -128,6 +137,7 @@
         src_ref=x_ref.at[core_piece(1 - core)], dst_ref=core_recv.at[0], send_sem=send_sem.at[s],
         recv_sem=recv_sem.at[s], device_id=core_dev(0), device_id_type=MESH)
     c.start()
+    loads[1].wait()
     pack(core)
     c.wait()
     core_sum[...] = x_ref[core_piece(core)] + core_recv[0]
@@ -180,9 +190,11 @@
     return pl.pallas_call(
         functools.partial(_allreduce_kernel, nx, ny, nz),
         out_shape=(jax.ShapeDtypeStruct((rows, cols), f32), jax.ShapeDtypeStruct((8, 128), f32)),
-        in_specs=[pl.BlockSpec(memory_space=pltpu.VMEM)] * 2,
+        in_specs=[pl.BlockSpec(memory_space=pl.ANY), pl.BlockSpec(memory_space=pltpu.VMEM)],
         out_specs=(pl.BlockSpec(memory_space=pltpu.VMEM),) * 2,
         scratch_shapes=[
+            pltpu.VMEM(g.shape, g.dtype),
+            pltpu.SemaphoreType.DMA((2,)),
             pltpu.VMEM((rows, cols), f32),
             pltpu.VMEM((1, rc, cols), f32),
             pltpu.VMEM((rc, cols), f32),

time: 95.8 us -> 96.2 us (level)
  no operation moved by 1% of the time
where the time goes in v7:
time: 96.2 us; the launch traced here: 96 us
  Pallas kernels  77.6 us (81%)
  matrix products  12.2 us (13%)
  local copies, waits for them, and re-layouts  2.37 us (2%)
  between operations  2.33 us (2%)
  other arithmetic  1.45 us (2%)
    pallas_call x1, Pallas kernels, allreduce(): pl.pallas_call(functools.partial(_allreduce_kernel, nx, ny, nz), out_shap...  77.6 us
    dot_general x11, matrix products, matmul(): jnp.dot(left, right, precision=HIGH, preferred_element_type=jnp.float32)  8.42 us
    dot_general x1, matrix products, per_device(): lax.dot_general(total, projected_all, (((0,), (0,)), ((), ())), precision...  2.63 us

profile of v7, /device:TPU:1, one launch (start us, length us, event | category | flops | bytes accessed | tf_op | source)
XLA Modules:
  0.0 96.0 jit_solution(15833071462848556044)
XLA Ops:
  0.6 0.0 copy-start
  0.6 0.0 copy-start.9
  0.7 0.0 copy-start.8
  0.7 0.0 copy-start.7
  0.7 0.8 convert_add_fusion
  1.5 0.1 add.49
  1.6 0.0 copy-start.1
  1.7 1.7 %copy-done.1 = bf16[2,1,1,768,768]{4,3,2,1,0:T(8,128)(2,1)S(1)} copy-done((bf16[2,1,1,768,768]{4,3,2,1,0:T(8,128)(2,1)S(1)}, bf16[2,1,1,768,768]{4,3,2,1,0:T(8,128)(2,1)}, u32[]{:S(2)}) %copy-start.1) | copy-done | bytes 2359320
  3.3 77.6 %shard_map.152 = (f32[768,896]{1,0:T(8,128)S(1)}, f32[8,128]{1,0:T(8,128)S(1)}) custom-call(bf16[2,768,768]{2,1,0:T(8,128)(2,1)S(1)} %bitcast.29, f32[768,128]{1,0:T(8,128)S(1)} %pad.4.tail_ref), custom_call_target="tpu_custom_call" | custom-call | tf_op jit(solution)/shard_map/pallas_call | solution.py:190
  80.9 0.5 slice.14
  82.2 0.0 copy-done.9
  82.2 0.0 copy-done.8
  82.2 0.0 copy-done.7
  82.2 0.6 multiply_subtract_fusion.1
  82.8 0.0 copy-done
  82.8 1.1 %fusion.2 = f32[768,256]{1,0:T(8,128)S(1)} fusion(f32[768,256]{1,0:T(8,128)S(1)} %copy-done, f32[768,896]{1,0:T(8,128)S(1)} %get-tuple-element.11), kind=kOutput, calls=%fused_computation.2 | convolution fusion | flops 905969664 | bytes 3932160 | tf_op jit(solution)/shard_map/dot_general | solution.py:20
  83.9 0.0 copy-start.5
  83.9 0.0 copy-start.6
  84.0 0.0 copy-start.4
  84.0 2.6 %multiply_reduce_fusion = (f32[]{:T(128)}, f32[768,256]{1,0:T(8,128)S(1)}) fusion(f32[768,256]{1,0:T(8,128)S(1)} %fusion.2, f32[768,896]{1,0:T(8,128)S(1)} %get-tuple-element.11), kind=kOutput, calls=%fused_computation.14 | convolution fusion | flops 906362880 | bytes 3932164 | tf_op jit(solution)/shard_map/dot_general | solution.py:234
  87.3 0.0 copy-done.5
  87.3 0.0 copy-done.6
  87.3 0.0 copy-start.2
  87.4 0.0 copy-start.3
  87.4 0.0 copy-done.4
  87.4 1.2 %fusion.25 = (bf16[48,768]{1,0:T(8,128)(2,1)}, f32[48,768]{1,0:T(8,128)}) fusion(f32[48,768]{1,0:T(8,128)S(1)} %copy-done.4, f32[768,256]{1,0:T(8,128)S(1)} %copy-done, f32[48,256]{1,0:T(8,128)S(1)} %get-tuple-element.16, f32[48,256]{1,0:T(8,128)S(1)} %get-tuple-element.15), kind=kOutput, calls=%fused_computation.41 | convolution fusion | flops 56893440 | bytes 1253376 | tf_op jit(solution)/shard_map/dot_general | solution.py:255
  88.6 0.8 fusion.9
  89.4 0.5 fusion.8
  89.9 0.0 copy-done.2
  89.9 0.0 copy-done.3
  89.9 0.8 fusion.26
  90.7 0.5 fusion.7
  91.2 0.8 fusion.27
  92.0 0.5 fusion.6
  92.5 0.8 fusion.28
  93.3 0.5 fusion.5
  93.8 0.8 fusion.29
  94.6 1.4 %fusion.4 = f32[768,256]{1,0:T(8,128)} fusion(f32[768,256]{1,0:T(8,128)S(1)} %fusion.5, f32[256,256]{1,0:T(8,128)S(1)} %fusion.29), kind=kOutput, calls=%fused_computation.5 | convolution fusion | flops 302579712 | bytes 1835008 | tf_op jit(solution)/shard_map/dot_general | solution.py:20
  (3 shorter events, 0.1 us)
Async XLA Ops:
  0.6 82.2 %copy-start = (f32[768,256]{1,0:T(8,128)S(1)}, f32[768,256]{1,0:T(8,128)}, u32[]{:S(2)}) copy-start(f32[768,256]{1,0:T(8,128)} %param.12) | copy-start | bytes 2359300
  0.6 81.5 %copy-start.9 = (f32[8,48]{1,0:T(8,128)S(1)}, f32[8,48]{1,0:T(8,128)}, u32[]{:S(2)}) copy-start(f32[8,48]{1,0:T(8,128)} %param.17) | copy-start | bytes 4612
  0.7 81.5 %copy-start.8 = (f32[8,48]{1,0:T(8,128)S(1)}, f32[8,48]{1,0:T(8,128)}, u32[]{:S(2)}) copy-start(f32[8,48]{1,0:T(8,128)} %param.16) | copy-start | bytes 4612
  0.7 81.5 %copy-start.7 = (f32[8,48]{1,0:T(8,128)S(1)}, f32[8,48]{1,0:T(8,128)}, u32[]{:S(2)}) copy-start(f32[8,48]{1,0:T(8,128)} %param.15) | copy-start | bytes 4612
  1.6 1.7 %copy-start.1 = (bf16[2,1,1,768,768]{4,3,2,1,0:T(8,128)(2,1)S(1)}, bf16[2,1,1,768,768]{4,3,2,1,0:T(8,128)(2,1)}, u32[]{:S(2)}) copy-start(bf16[2,1,1,768,768]{4,3,2,1,0:T(8,128)(2,1)} %param.9) | copy-start | bytes 7077892
  83.9 3.4 %copy-start.5 = (f32[48,256]{1,0:T(8,128)S(1)}, f32[48,256]{1,0:T(8,128)}, u32[]{:S(2)}) copy-start(f32[48,256]{1,0:T(8,128)} %param.13) | copy-start | bytes 147460
  83.9 3.4 %copy-start.6 = (f32[48,256]{1,0:T(8,128)S(1)}, f32[48,256]{1,0:T(8,128)}, u32[]{:S(2)}) copy-start(f32[48,256]{1,0:T(8,128)} %param.14) | copy-start | bytes 147460
  84.0 3.4 %copy-start.4 = (f32[48,768]{1,0:T(8,128)S(1)}, f32[48,768]{1,0:T(8,128)}, u32[]{:S(2)}) copy-start(f32[48,768]{1,0:T(8,128)} %param.11) | copy-start | bytes 442372
  87.3 2.5 %copy-start.2 = (f32[48,256]{1,0:T(8,128)}, f32[48,256]{1,0:T(8,128)S(1)}, u32[]{:S(2)}) copy-start(f32[48,256]{1,0:T(8,128)S(1)} %get-tuple-element.15) | copy-start | bytes 147460
  87.4 2.5 %copy-start.3 = (f32[48,256]{1,0:T(8,128)}, f32[48,256]{1,0:T(8,128)S(1)}, u32[]{:S(2)}) copy-start(f32[48,256]{1,0:T(8,128)S(1)} %get-tuple-element.16) | copy-start | bytes 147460

commit v8 on v7

--- a/solution.py
+++ b/solution.py
@@ -190,7 +190,7 @@
     return pl.pallas_call(
         functools.partial(_allreduce_kernel, nx, ny, nz),
         out_shape=(jax.ShapeDtypeStruct((rows, cols), f32), jax.ShapeDtypeStruct((8, 128), f32)),
-        in_specs=[pl.BlockSpec(memory_space=pl.ANY), pl.BlockSpec(memory_space=pltpu.VMEM)],
+        in_specs=[pl.BlockSpec(memory_space=pltpu.HBM), pl.BlockSpec(memory_space=pltpu.VMEM)],
         out_specs=(pl.BlockSpec(memory_space=pltpu.VMEM),) * 2,
         scratch_shapes=[
             pltpu.VMEM(g.shape, g.dtype),
@@ -213,7 +213,7 @@
             pltpu.SemaphoreType.DMA((n_sems,)),
         ],
         compiler_params=pltpu.CompilerParams(
-            collective_id=0, has_side_effects=True, vmem_limit_bytes=48 * 1024 * 1024),
+            collective_id=0, has_side_effects=True),
     )(g, tail)
 
 

time: 96.2 us -> 101 us (1.050)
  Pallas kernels: 77.6 us -> 79.6 us
  matrix products: 12.2 us -> 14 us
    pallas_call x1, Pallas kernels: 77.6 us -> 79.6 us  [allreduce(): pl.pallas_call(functools.partial(_allreduce_kernel, nx, ny, nz), out_shap...]
    dot_general x11, matrix products: 8.42 us -> 10.1 us  [matmul(): jnp.dot(left, right, precision=HIGH, preferred_element_type=jnp.float32)]
    unnamed x20, local copies, waits for them, and re-layouts: 1.71 us -> 0.06 us
where the time goes in v8:
time: 101 us; the launch traced here: 100 us
  Pallas kernels  79.6 us (79%)
  matrix products  14 us (14%)
  between operations  2.33 us (2%)
  local copies, waits for them, and re-layouts  2.27 us (2%)
  other arithmetic  2.13 us (2%)
    pallas_call x1, Pallas kernels, allreduce(): pl.pallas_call(functools.partial(_allreduce_kernel, nx, ny, nz), out_shap...  79.6 us
    dot_general x11, matrix products, matmul(): jnp.dot(left, right, precision=HIGH, preferred_element_type=jnp.float32)  10.1 us
    dot_general x1, matrix products, per_device(): lax.dot_general(total, projected_all, (((0,), (0,)), ((), ())), precision...  2.67 us

profile of v8, /device:TPU:1, one launch (start us, length us, event | category | flops | bytes accessed | tf_op | source)
XLA Modules:
  0.0 100.3 jit_solution(4507926381656179710)
XLA Ops:
  0.6 0.0 copy-start
  0.6 0.0 copy-start.9
  0.7 0.0 copy-start.8
  0.7 0.0 copy-start.7
  0.7 0.8 convert_add_fusion
  1.5 0.1 add.49
  1.6 0.8 pad.4.tail_ref
  2.4 79.6 %shard_map.152 = (f32[768,896]{1,0:T(8,128)}, f32[8,128]{1,0:T(8,128)}) custom-call(bf16[2,768,768]{2,1,0:T(8,128)(2,1)} %bitcast.29, f32[768,128]{1,0:T(8,128)} %pad.4.tail_ref), custom_call_target="tpu_custom_call" | custom-call | tf_op jit(solution)/shard_map/pallas_call | solution.py:190
  82.0 0.0 copy-start.1
  82.0 1.3 %slice.14 = f32[1,1]{1,0:T(1,128)} slice(f32[8,128]{1,0:T(8,128)} %get-tuple-element.10), slice={[0:1], [0:1]} | slice | bytes 8 | tf_op jit(solution)/shard_map/slice | solution.py:241
  84.1 0.0 copy-done.9
  84.1 0.0 copy-done.8
  84.1 0.0 copy-done.7
  84.1 1.3 %multiply_subtract_fusion.1 = (f32[8,48]{1,0:T(8,128)}, f32[8,48]{1,0:T(8,128)}, f32[8,48]{1,0:T(8,128)}) fusion(f32[8,48]{1,0:T(8,128)S(1)} %copy-done.7, f32[768,896]{1,0:T(8,128)} %get-tuple-element.11, s32[]{:T(128)S(6)} %select_n.7, f32[]{:T(128)} %bitcast.3, f32[8,48]{1,0:T(8,128)S(1)} %copy-done.8, f32[8,48]{1,0:T(8,128)S(1)} %copy-done.9), kind=kLoop, calls=%fused_computation.35 | loop fusion | flops 6144 | bytes 10760 | tf_op jit(solution)/shard_map/sub | solution.py:267
  85.4 0.0 copy-done
  85.4 2.8 %fusion.2 = f32[768,256]{1,0:T(8,128)S(1)} fusion(f32[768,256]{1,0:T(8,128)S(1)} %copy-done, f32[768,896]{1,0:T(8,128)} %get-tuple-element.11), kind=kOutput, calls=%fused_computation.2 | convolution fusion | flops 905969664 | bytes 3932160 | tf_op jit(solution)/shard_map/dot_general | solution.py:20
  88.2 0.0 copy-done.1
  88.2 0.0 copy-start.5
  88.2 0.0 copy-start.6
  88.2 0.0 copy-start.4
  88.3 2.7 %multiply_reduce_fusion = (f32[]{:T(128)}, f32[768,256]{1,0:T(8,128)S(1)}) fusion(f32[768,256]{1,0:T(8,128)S(1)} %fusion.2, f32[768,896]{1,0:T(8,128)S(1)} %copy-done.1), kind=kOutput, calls=%fused_computation.14 | convolution fusion | flops 906362880 | bytes 3932164 | tf_op jit(solution)/shard_map/dot_general | solution.py:234
  91.6 0.0 copy-done.5
  91.6 0.0 copy-done.6
  91.7 0.0 copy-start.2
  91.7 0.0 copy-start.3
  91.7 0.0 copy-done.4
  91.7 1.2 %fusion.25 = (bf16[48,768]{1,0:T(8,128)(2,1)}, f32[48,768]{1,0:T(8,128)}) fusion(f32[48,768]{1,0:T(8,128)S(1)} %copy-done.4, f32[768,256]{1,0:T(8,128)S(1)} %copy-done, f32[48,256]{1,0:T(8,128)S(1)} %get-tuple-element.16, f32[48,256]{1,0:T(8,128)S(1)} %get-tuple-element.15), kind=kOutput, calls=%fused_computation.41 | convolution fusion | flops 56893440 | bytes 1253376 | tf_op jit(solution)/shard_map/dot_general | solution.py:255
  92.9 0.8 fusion.9
  93.7 0.5 fusion.8
  94.2 0.0 copy-done.2
  94.2 0.0 copy-done.3
  94.2 0.8 fusion.26
  95.0 0.5 fusion.7
  95.5 0.8 fusion.27
  96.3 0.5 fusion.6
  96.8 0.8 fusion.28
  97.6 0.5 fusion.5
  98.1 0.8 fusion.29
  99.0 1.4 %fusion.4 = f32[768,256]{1,0:T(8,128)} fusion(f32[768,256]{1,0:T(8,128)S(1)} %fusion.5, f32[256,256]{1,0:T(8,128)S(1)} %fusion.29), kind=kOutput, calls=%fused_computation.5 | convolution fusion | flops 302579712 | bytes 1835008 | tf_op jit(solution)/shard_map/dot_general | solution.py:20
  (2 shorter events, 0.1 us)
Async XLA Ops:
  0.6 84.8 %copy-start = (f32[768,256]{1,0:T(8,128)S(1)}, f32[768,256]{1,0:T(8,128)}, u32[]{:S(2)}) copy-start(f32[768,256]{1,0:T(8,128)} %param.12) | copy-start | bytes 2359300
  0.6 83.4 %copy-start.9 = (f32[8,48]{1,0:T(8,128)S(1)}, f32[8,48]{1,0:T(8,128)}, u32[]{:S(2)}) copy-start(f32[8,48]{1,0:T(8,128)} %param.17) | copy-start | bytes 4612
  0.7 83.4 %copy-start.8 = (f32[8,48]{1,0:T(8,128)S(1)}, f32[8,48]{1,0:T(8,128)}, u32[]{:S(2)}) copy-start(f32[8,48]{1,0:T(8,128)} %param.16) | copy-start | bytes 4612
  0.7 83.4 %copy-start.7 = (f32[8,48]{1,0:T(8,128)S(1)}, f32[8,48]{1,0:T(8,128)}, u32[]{:S(2)}) copy-start(f32[8,48]{1,0:T(8,128)} %param.15) | copy-start | bytes 4612
  82.0 6.2 %copy-start.1 = (f32[768,896]{1,0:T(8,128)S(1)}, f32[768,896]{1,0:T(8,128)}, u32[]{:S(2)}) copy-start(f32[768,896]{1,0:T(8,128)} %get-tuple-element.11) | copy-start | bytes 8257540
  88.2 3.4 %copy-start.5 = (f32[48,256]{1,0:T(8,128)S(1)}, f32[48,256]{1,0:T(8,128)}, u32[]{:S(2)}) copy-start(f32[48,256]{1,0:T(8,128)} %param.13) | copy-start | bytes 147460
  88.2 3.4 %copy-start.6 = (f32[48,256]{1,0:T(8,128)S(1)}, f32[48,256]{1,0:T(8,128)}, u32[]{:S(2)}) copy-start(f32[48,256]{1,0:T(8,128)} %param.14) | copy-start | bytes 147460
  88.2 3.5 %copy-start.4 = (f32[48,768]{1,0:T(8,128)S(1)}, f32[48,768]{1,0:T(8,128)}, u32[]{:S(2)}) copy-start(f32[48,768]{1,0:T(8,128)} %param.11) | copy-start | bytes 442372
  91.7 2.5 %copy-start.2 = (f32[48,256]{1,0:T(8,128)}, f32[48,256]{1,0:T(8,128)S(1)}, u32[]{:S(2)}) copy-start(f32[48,256]{1,0:T(8,128)S(1)} %get-tuple-element.15) | copy-start | bytes 147460
  91.7 2.5 %copy-start.3 = (f32[48,256]{1,0:T(8,128)}, f32[48,256]{1,0:T(8,128)S(1)}, u32[]{:S(2)}) copy-start(f32[48,256]{1,0:T(8,128)S(1)} %get-tuple-element.16) | copy-start | bytes 147460

commit v9 on v6

--- a/solution.py
+++ b/solution.py
@@ -147,19 +147,53 @@
 
     gather_stage(z_full, nh, zi, z_dev, y_out, z_piece)
     gather_stage(y_out.at[:, pl.ds(0, cols)], ny, pos_b, y_dev, x_out, y_piece)
-    gather_stage(x_out, nx, pos_a, x_dev, core_out, x_piece)
+    half_off = core * rc
+    other_off = (1 - core) * rc
+
+    def out_rows(off, j):
+        return pl.ds(pl.multiple_of(off + j * rx, 8), rx)
+
+    a_sends = []
+    for k in range(1, nx):
+        j = (pos_a + k) % nx
+        s = next_sem()
+        c = pltpu.make_async_remote_copy(
+            src_ref=x_out, dst_ref=core_out.at[x_piece(pos_a)], send_sem=send_sem.at[s],
+            recv_sem=recv_sem.at[s], device_id=x_dev(j), device_id_type=MESH)
+        c.start()
+        a_sends.append((c, s, k))
+    fwd = []
     s = next_sem()
     c = pltpu.make_async_remote_copy(
-        src_ref=core_out, dst_ref=out_ref.at[core_piece(core)], send_sem=send_sem.at[s],
+        src_ref=x_out, dst_ref=out_ref.at[out_rows(half_off, pos_a)], send_sem=send_sem.at[s],
         recv_sem=recv_sem.at[s], device_id=core_dev(0), device_id_type=MESH)
     c.start()
+    fwd.append((c, s, pos_a))
+    core_out[x_piece(pos_a)] = x_out[...]
+    for c, s, k in a_sends:
+        j = (pos_a + nx - k) % nx
+        pltpu.make_async_remote_copy(
+            src_ref=x_out, dst_ref=core_out.at[x_piece(j)], send_sem=send_sem.at[s],
+            recv_sem=recv_sem.at[s], device_id=x_dev(j), device_id_type=MESH).wait_recv()
+        s2 = next_sem()
+        c2 = pltpu.make_async_remote_copy(
+            src_ref=core_out.at[x_piece(j)], dst_ref=out_ref.at[out_rows(half_off, j)], send_sem=send_sem.at[s2],
+            recv_sem=recv_sem.at[s2], device_id=core_dev(0), device_id_type=MESH)
+        c2.start()
+        fwd.append((c2, s2, j))
+    for c, s, k in a_sends:
+        c.wait_send()
     mine = core_out[...]
     out_ref[core_piece(core)] = mine
     own = jnp.sum(jnp.sum(mine * mine, axis=0, keepdims=True), axis=1, keepdims=True)
-    c.wait_send()
-    pltpu.make_async_remote_copy(
-        src_ref=core_out, dst_ref=out_ref.at[core_piece(1 - core)], send_sem=send_sem.at[s],
-        recv_sem=recv_sem.at[s], device_id=core_dev(0), device_id_type=MESH).wait_recv()
+    for c, s, j in fwd:
+        c.wait_send()
+    partner_pos = xi + (yi - xi) * (1 - core)
+    for idx, (c, s, j) in enumerate(fwd):
+        jp = (partner_pos + nx - idx) % nx
+        pltpu.make_async_remote_copy(
+            src_ref=x_out, dst_ref=out_ref.at[out_rows(other_off, jp)], send_sem=send_sem.at[s],
+            recv_sem=recv_sem.at[s], device_id=core_dev(0), device_id_type=MESH).wait_recv()
     other = out_ref[core_piece(1 - core)]
     rest = jnp.sum(jnp.sum(other * other, axis=0, keepdims=True), axis=1, keepdims=True)
     sq_ref[...] = jnp.broadcast_to(own + rest, sq_ref.shape)
@@ -175,7 +209,7 @@
     ry = rx // ny
     zcols = 128 * nh * ((cols + 128 * nh - 1) // (128 * nh))
     cz = zcols // nh
-    n_sems = 2 * (1 + (nx - 1) + (ny - 1) + (nh - 1)) + 1
+    n_sems = 2 * (1 + (nx - 1) + (ny - 1) + (nh - 1)) + 1 + (nx - 1)
     f32 = jnp.float32
     return pl.pallas_call(
         functools.partial(_allreduce_kernel, nx, ny, nz),

time: 95.8 us -> 94.8 us (0.990)
  no operation moved by 1% of the time
where the time goes in v9:
time: 94.8 us; the launch traced here: 94.7 us
  Pallas kernels  76.3 us (80%)
  matrix products  12.2 us (13%)
  local copies, waits for them, and re-layouts  2.37 us (2%)
  between operations  2.33 us (2%)
  other arithmetic  1.45 us (2%)
    pallas_call x1, Pallas kernels, allreduce(): pl.pallas_call(functools.partial(_allreduce_kernel, nx, ny, nz), out_shap...  76.3 us
    dot_general x11, matrix products, matmul(): jnp.dot(left, right, precision=HIGH, preferred_element_type=jnp.float32)  8.42 us
    dot_general x1, matrix products, per_device(): lax.dot_general(total, projected_all, (((0,), (0,)), ((), ())), precision...  2.63 us

profile of v9, /device:TPU:1, one launch (start us, length us, event | category | flops | bytes accessed | tf_op | source)
XLA Modules:
  0.0 94.7 jit_solution(2836573549215397711)
XLA Ops:
  0.6 0.0 copy-start
  0.6 0.0 copy-start.9
  0.7 0.0 copy-start.8
  0.7 0.0 copy-start.7
  0.7 0.8 convert_add_fusion
  1.5 0.1 add.49
  1.6 0.0 copy-start.1
  1.7 1.7 %copy-done.1 = bf16[2,1,1,768,768]{4,3,2,1,0:T(8,128)(2,1)S(1)} copy-done((bf16[2,1,1,768,768]{4,3,2,1,0:T(8,128)(2,1)S(1)}, bf16[2,1,1,768,768]{4,3,2,1,0:T(8,128)(2,1)}, u32[]{:S(2)}) %copy-start.1) | copy-done | bytes 2359320
  3.3 76.3 %shard_map.152 = (f32[768,896]{1,0:T(8,128)S(1)}, f32[8,128]{1,0:T(8,128)S(1)}) custom-call(bf16[2,768,768]{2,1,0:T(8,128)(2,1)S(1)} %bitcast.29, f32[768,128]{1,0:T(8,128)S(1)} %pad.4.tail_ref), custom_call_target="tpu_custom_call" | custom-call | tf_op jit(solution)/shard_map/pallas_call | solution.py:214
  79.6 0.5 slice.14
  80.8 0.0 copy-done.9
  80.8 0.0 copy-done.8
  80.8 0.0 copy-done.7
  80.9 0.6 multiply_subtract_fusion.1
  81.5 0.0 copy-done
  81.5 1.1 %fusion.2 = f32[768,256]{1,0:T(8,128)S(1)} fusion(f32[768,256]{1,0:T(8,128)S(1)} %copy-done, f32[768,896]{1,0:T(8,128)S(1)} %get-tuple-element.11), kind=kOutput, calls=%fused_computation.2 | convolution fusion | flops 905969664 | bytes 3932160 | tf_op jit(solution)/shard_map/dot_general | solution.py:20
  82.6 0.0 copy-start.5
  82.6 0.0 copy-start.6
  82.6 0.0 copy-start.4
  82.6 2.6 %multiply_reduce_fusion = (f32[]{:T(128)}, f32[768,256]{1,0:T(8,128)S(1)}) fusion(f32[768,256]{1,0:T(8,128)S(1)} %fusion.2, f32[768,896]{1,0:T(8,128)S(1)} %get-tuple-element.11), kind=kOutput, calls=%fused_computation.14 | convolution fusion | flops 906362880 | bytes 3932164 | tf_op jit(solution)/shard_map/dot_general | solution.py:256
  85.9 0.0 copy-done.5
  86.0 0.0 copy-done.6
  86.0 0.0 copy-start.2
  86.0 0.0 copy-start.3
  86.0 0.0 copy-done.4
  86.0 1.2 %fusion.25 = (bf16[48,768]{1,0:T(8,128)(2,1)}, f32[48,768]{1,0:T(8,128)}) fusion(f32[48,768]{1,0:T(8,128)S(1)} %copy-done.4, f32[768,256]{1,0:T(8,128)S(1)} %copy-done, f32[48,256]{1,0:T(8,128)S(1)} %get-tuple-element.16, f32[48,256]{1,0:T(8,128)S(1)} %get-tuple-element.15), kind=kOutput, calls=%fused_computation.41 | convolution fusion | flops 56893440 | bytes 1253376 | tf_op jit(solution)/shard_map/dot_general | solution.py:277
  87.2 0.8 fusion.9
  88.0 0.5 fusion.8
  88.5 0.0 copy-done.2
  88.5 0.0 copy-done.3
  88.6 0.8 fusion.26
  89.4 0.5 fusion.7
  89.9 0.8 fusion.27
  90.7 0.5 fusion.6
  91.2 0.8 fusion.28
  92.0 0.5 fusion.5
  92.5 0.8 fusion.29
  93.3 1.4 %fusion.4 = f32[768,256]{1,0:T(8,128)} fusion(f32[768,256]{1,0:T(8,128)S(1)} %fusion.5, f32[256,256]{1,0:T(8,128)S(1)} %fusion.29), kind=kOutput, calls=%fused_computation.5 | convolution fusion | flops 302579712 | bytes 1835008 | tf_op jit(solution)/shard_map/dot_general | solution.py:20
  (3 shorter events, 0.1 us)
Async XLA Ops:
  0.6 80.8 %copy-start = (f32[768,256]{1,0:T(8,128)S(1)}, f32[768,256]{1,0:T(8,128)}, u32[]{:S(2)}) copy-start(f32[768,256]{1,0:T(8,128)} %param.12) | copy-start | bytes 2359300
  0.6 80.2 %copy-start.9 = (f32[8,48]{1,0:T(8,128)S(1)}, f32[8,48]{1,0:T(8,128)}, u32[]{:S(2)}) copy-start(f32[8,48]{1,0:T(8,128)} %param.17) | copy-start | bytes 4612
  0.7 80.2 %copy-start.8 = (f32[8,48]{1,0:T(8,128)S(1)}, f32[8,48]{1,0:T(8,128)}, u32[]{:S(2)}) copy-start(f32[8,48]{1,0:T(8,128)} %param.16) | copy-start | bytes 4612
  0.7 80.2 %copy-start.7 = (f32[8,48]{1,0:T(8,128)S(1)}, f32[8,48]{1,0:T(8,128)}, u32[]{:S(2)}) copy-start(f32[8,48]{1,0:T(8,128)} %param.15) | copy-start | bytes 4612
  1.6 1.7 %copy-start.1 = (bf16[2,1,1,768,768]{4,3,2,1,0:T(8,128)(2,1)S(1)}, bf16[2,1,1,768,768]{4,3,2,1,0:T(8,128)(2,1)}, u32[]{:S(2)}) copy-start(bf16[2,1,1,768,768]{4,3,2,1,0:T(8,128)(2,1)} %param.9) | copy-start | bytes 7077892
  82.6 3.4 %copy-start.5 = (f32[48,256]{1,0:T(8,128)S(1)}, f32[48,256]{1,0:T(8,128)}, u32[]{:S(2)}) copy-start(f32[48,256]{1,0:T(8,128)} %param.13) | copy-start | bytes 147460
  82.6 3.4 %copy-start.6 = (f32[48,256]{1,0:T(8,128)S(1)}, f32[48,256]{1,0:T(8,128)}, u32[]{:S(2)}) copy-start(f32[48,256]{1,0:T(8,128)} %param.14) | copy-start | bytes 147460
  82.6 3.4 %copy-start.4 = (f32[48,768]{1,0:T(8,128)S(1)}, f32[48,768]{1,0:T(8,128)}, u32[]{:S(2)}) copy-start(f32[48,768]{1,0:T(8,128)} %param.11) | copy-start | bytes 442372
  86.0 2.5 %copy-start.2 = (f32[48,256]{1,0:T(8,128)}, f32[48,256]{1,0:T(8,128)S(1)}, u32[]{:S(2)}) copy-start(f32[48,256]{1,0:T(8,128)S(1)} %get-tuple-element.15) | copy-start | bytes 147460
  86.0 2.5 %copy-start.3 = (f32[48,256]{1,0:T(8,128)}, f32[48,256]{1,0:T(8,128)S(1)}, u32[]{:S(2)}) copy-start(f32[48,256]{1,0:T(8,128)S(1)} %get-tuple-element.16) | copy-start | bytes 147460

commit v10 on v9

--- a/solution.py
+++ b/solution.py
@@ -81,9 +81,12 @@
     def col_slice(j, size):
         return (slice(None), pl.ds(pl.multiple_of(j * size, 128), size))
 
+    def far_first(n):
+        return sorted(range(1, n), key=lambda k: (-min(k, n - k), k))
+
     def reduce_stage(src, n, me, dev_of, recv, dst, piece):
         copies = []
-        for k in range(1, n):
+        for k in far_first(n):
             j = (me + k) % n
             s = next_sem()
             c = pltpu.make_async_remote_copy(
@@ -100,7 +103,7 @@
 
     def gather_stage(src, n, me, dev_of, dst, piece):
         copies = []
-        for k in range(1, n):
+        for k in far_first(n):
             j = (me + k) % n
             s = next_sem()
             c = pltpu.make_async_remote_copy(

time: 94.8 us -> 93.7 us (0.988); the launches traced: 94.7 us -> 92.6 us
  Pallas kernels: 76.3 us -> 74.2 us
    pallas_call x1, Pallas kernels: 76.3 us -> 74.2 us  [allreduce(): pl.pallas_call(functools.partial(_allreduce_kernel, nx, ny, nz), out_shap...]
where the time goes in v10:
time: 93.7 us; the launch traced here: 92.6 us
  Pallas kernels  74.2 us (79%)
  matrix products  12.2 us (13%)
  local copies, waits for them, and re-layouts  2.37 us (3%)
  between operations  2.33 us (2%)
  other arithmetic  1.45 us (2%)
    pallas_call x1, Pallas kernels, allreduce(): pl.pallas_call(functools.partial(_allreduce_kernel, nx, ny, nz), out_shap...  74.2 us
    dot_general x11, matrix products, matmul(): jnp.dot(left, right, precision=HIGH, preferred_element_type=jnp.float32)  8.42 us
    dot_general x1, matrix products, per_device(): lax.dot_general(total, projected_all, (((0,), (0,)), ((), ())), precision...  2.63 us

profile of v10, /device:TPU:1, one launch (start us, length us, event | category | flops | bytes accessed | tf_op | source)
XLA Modules:
  0.0 92.6 jit_solution(8166076036205810914)
XLA Ops:
  0.6 0.0 copy-start
  0.6 0.0 copy-start.9
  0.7 0.0 copy-start.8
  0.7 0.0 copy-start.7
  0.7 0.8 convert_add_fusion
  1.5 0.1 add.49
  1.6 0.0 copy-start.1
  1.7 1.7 %copy-done.1 = bf16[2,1,1,768,768]{4,3,2,1,0:T(8,128)(2,1)S(1)} copy-done((bf16[2,1,1,768,768]{4,3,2,1,0:T(8,128)(2,1)S(1)}, bf16[2,1,1,768,768]{4,3,2,1,0:T(8,128)(2,1)}, u32[]{:S(2)}) %copy-start.1) | copy-done | bytes 2359320
  3.3 74.2 %shard_map.152 = (f32[768,896]{1,0:T(8,128)S(1)}, f32[8,128]{1,0:T(8,128)S(1)}) custom-call(bf16[2,768,768]{2,1,0:T(8,128)(2,1)S(1)} %bitcast.29, f32[768,128]{1,0:T(8,128)S(1)} %pad.4.tail_ref), custom_call_target="tpu_custom_call" | custom-call | tf_op jit(solution)/shard_map/pallas_call | solution.py:217
  77.5 0.5 slice.14
  78.7 0.0 copy-done.9
  78.7 0.0 copy-done.8
  78.8 0.0 copy-done.7
  78.8 0.6 multiply_subtract_fusion.1
  79.4 0.0 copy-done
  79.4 1.1 %fusion.2 = f32[768,256]{1,0:T(8,128)S(1)} fusion(f32[768,256]{1,0:T(8,128)S(1)} %copy-done, f32[768,896]{1,0:T(8,128)S(1)} %get-tuple-element.11), kind=kOutput, calls=%fused_computation.2 | convolution fusion | flops 905969664 | bytes 3932160 | tf_op jit(solution)/shard_map/dot_general | solution.py:20
  80.5 0.0 copy-start.5
  80.5 0.0 copy-start.6
  80.5 0.0 copy-start.4
  80.5 2.6 %multiply_reduce_fusion = (f32[]{:T(128)}, f32[768,256]{1,0:T(8,128)S(1)}) fusion(f32[768,256]{1,0:T(8,128)S(1)} %fusion.2, f32[768,896]{1,0:T(8,128)S(1)} %get-tuple-element.11), kind=kOutput, calls=%fused_computation.14 | convolution fusion | flops 906362880 | bytes 3932164 | tf_op jit(solution)/shard_map/dot_general | solution.py:259
  83.9 0.0 copy-done.5
  83.9 0.0 copy-done.6
  83.9 0.0 copy-start.2
  83.9 0.0 copy-start.3
  83.9 0.0 copy-done.4
  83.9 1.2 %fusion.25 = (bf16[48,768]{1,0:T(8,128)(2,1)}, f32[48,768]{1,0:T(8,128)}) fusion(f32[48,768]{1,0:T(8,128)S(1)} %copy-done.4, f32[768,256]{1,0:T(8,128)S(1)} %copy-done, f32[48,256]{1,0:T(8,128)S(1)} %get-tuple-element.16, f32[48,256]{1,0:T(8,128)S(1)} %get-tuple-element.15), kind=kOutput, calls=%fused_computation.41 | convolution fusion | flops 56893440 | bytes 1253376 | tf_op jit(solution)/shard_map/dot_general | solution.py:280
  85.1 0.8 fusion.9
  85.9 0.5 fusion.8
  86.4 0.0 copy-done.2
  86.5 0.0 copy-done.3
  86.5 0.8 fusion.26
  87.3 0.5 fusion.7
  87.8 0.8 fusion.27
  88.6 0.5 fusion.6
  89.1 0.8 fusion.28
  89.9 0.5 fusion.5
  90.4 0.8 fusion.29
  91.2 1.4 %fusion.4 = f32[768,256]{1,0:T(8,128)} fusion(f32[768,256]{1,0:T(8,128)S(1)} %fusion.5, f32[256,256]{1,0:T(8,128)S(1)} %fusion.29), kind=kOutput, calls=%fused_computation.5 | convolution fusion | flops 302579712 | bytes 1835008 | tf_op jit(solution)/shard_map/dot_general | solution.py:20
  (3 shorter events, 0.1 us)
Async XLA Ops:
  0.6 78.8 %copy-start = (f32[768,256]{1,0:T(8,128)S(1)}, f32[768,256]{1,0:T(8,128)}, u32[]{:S(2)}) copy-start(f32[768,256]{1,0:T(8,128)} %param.12) | copy-start | bytes 2359300
  0.6 78.1 %copy-start.9 = (f32[8,48]{1,0:T(8,128)S(1)}, f32[8,48]{1,0:T(8,128)}, u32[]{:S(2)}) copy-start(f32[8,48]{1,0:T(8,128)} %param.17) | copy-start | bytes 4612
  0.7 78.1 %copy-start.8 = (f32[8,48]{1,0:T(8,128)S(1)}, f32[8,48]{1,0:T(8,128)}, u32[]{:S(2)}) copy-start(f32[8,48]{1,0:T(8,128)} %param.16) | copy-start | bytes 4612
  0.7 78.1 %copy-start.7 = (f32[8,48]{1,0:T(8,128)S(1)}, f32[8,48]{1,0:T(8,128)}, u32[]{:S(2)}) copy-start(f32[8,48]{1,0:T(8,128)} %param.15) | copy-start | bytes 4612
  1.6 1.7 %copy-start.1 = (bf16[2,1,1,768,768]{4,3,2,1,0:T(8,128)(2,1)S(1)}, bf16[2,1,1,768,768]{4,3,2,1,0:T(8,128)(2,1)}, u32[]{:S(2)}) copy-start(bf16[2,1,1,768,768]{4,3,2,1,0:T(8,128)(2,1)} %param.9) | copy-start | bytes 7077892
  80.5 3.4 %copy-start.5 = (f32[48,256]{1,0:T(8,128)S(1)}, f32[48,256]{1,0:T(8,128)}, u32[]{:S(2)}) copy-start(f32[48,256]{1,0:T(8,128)} %param.13) | copy-start | bytes 147460
  80.5 3.4 %copy-start.6 = (f32[48,256]{1,0:T(8,128)S(1)}, f32[48,256]{1,0:T(8,128)}, u32[]{:S(2)}) copy-start(f32[48,256]{1,0:T(8,128)} %param.14) | copy-start | bytes 147460
  80.5 3.4 %copy-start.4 = (f32[48,768]{1,0:T(8,128)S(1)}, f32[48,768]{1,0:T(8,128)}, u32[]{:S(2)}) copy-start(f32[48,768]{1,0:T(8,128)} %param.11) | copy-start | bytes 442372
  83.9 2.5 %copy-start.2 = (f32[48,256]{1,0:T(8,128)}, f32[48,256]{1,0:T(8,128)S(1)}, u32[]{:S(2)}) copy-start(f32[48,256]{1,0:T(8,128)S(1)} %get-tuple-element.15) | copy-start | bytes 147460
  83.9 2.5 %copy-start.3 = (f32[48,256]{1,0:T(8,128)}, f32[48,256]{1,0:T(8,128)S(1)}, u32[]{:S(2)}) copy-start(f32[48,256]{1,0:T(8,128)S(1)} %get-tuple-element.16) | copy-start | bytes 147460

commit v11 on v10

--- a/solution.py
+++ b/solution.py
@@ -157,7 +157,7 @@
         return pl.ds(pl.multiple_of(off + j * rx, 8), rx)
 
     a_sends = []
-    for k in range(1, nx):
+    for k in far_first(nx):
         j = (pos_a + k) % nx
         s = next_sem()
         c = pltpu.make_async_remote_copy(
@@ -173,7 +173,8 @@
     c.start()
     fwd.append((c, s, pos_a))
     core_out[x_piece(pos_a)] = x_out[...]
-    for c, s, k in a_sends:
+    near_first = sorted(a_sends, key=lambda t: (min(t[2], nx - t[2]), t[2]))
+    for c, s, k in near_first:
         j = (pos_a + nx - k) % nx
         pltpu.make_async_remote_copy(
             src_ref=x_out, dst_ref=core_out.at[x_piece(j)], send_sem=send_sem.at[s],
@@ -192,8 +193,9 @@
     for c, s, j in fwd:
         c.wait_send()
     partner_pos = xi + (yi - xi) * (1 - core)
+    fwd_k = [0] + [t[2] for t in near_first]
     for idx, (c, s, j) in enumerate(fwd):
-        jp = (partner_pos + nx - idx) % nx
+        jp = (partner_pos + nx - fwd_k[idx]) % nx
         pltpu.make_async_remote_copy(
             src_ref=x_out, dst_ref=out_ref.at[out_rows(other_off, jp)], send_sem=send_sem.at[s],
             recv_sem=recv_sem.at[s], device_id=core_dev(0), device_id_type=MESH).wait_recv()

time: 93.7 us -> 95.4 us (1.018); the launches traced: 92.6 us -> 95.2 us
  Pallas kernels: 74.2 us -> 76.9 us
    pallas_call x1, Pallas kernels: 74.2 us -> 76.9 us  [allreduce(): pl.pallas_call(functools.partial(_allreduce_kernel, nx, ny, nz), out_shap...]
where the time goes in v11:
time: 95.4 us; the launch traced here: 95.2 us
  Pallas kernels  76.9 us (81%)
  matrix products  12.2 us (13%)
  local copies, waits for them, and re-layouts  2.37 us (2%)
  between operations  2.33 us (2%)
  other arithmetic  1.45 us (2%)
    pallas_call x1, Pallas kernels, allreduce(): pl.pallas_call(functools.partial(_allreduce_kernel, nx, ny, nz), out_shap...  76.9 us
    dot_general x11, matrix products, matmul(): jnp.dot(left, right, precision=HIGH, preferred_element_type=jnp.float32)  8.42 us
    dot_general x1, matrix products, per_device(): lax.dot_general(total, projected_all, (((0,), (0,)), ((), ())), precision...  2.63 us

profile of v11, /device:TPU:1, one launch (start us, length us, event | category | flops | bytes accessed | tf_op | source)
XLA Modules:
  0.0 95.2 jit_solution(12636435389745453725)
XLA Ops:
  0.6 0.0 copy-start
  0.6 0.0 copy-start.9
  0.7 0.0 copy-start.8
  0.7 0.0 copy-start.7
  0.7 0.8 convert_add_fusion
  1.5 0.1 add.49
  1.6 0.0 copy-start.1
  1.7 1.7 %copy-done.1 = bf16[2,1,1,768,768]{4,3,2,1,0:T(8,128)(2,1)S(1)} copy-done((bf16[2,1,1,768,768]{4,3,2,1,0:T(8,128)(2,1)S(1)}, bf16[2,1,1,768,768]{4,3,2,1,0:T(8,128)(2,1)}, u32[]{:S(2)}) %copy-start.1) | copy-done | bytes 2359320
  3.3 76.9 %shard_map.152 = (f32[768,896]{1,0:T(8,128)S(1)}, f32[8,128]{1,0:T(8,128)S(1)}) custom-call(bf16[2,768,768]{2,1,0:T(8,128)(2,1)S(1)} %bitcast.29, f32[768,128]{1,0:T(8,128)S(1)} %pad.4.tail_ref), custom_call_target="tpu_custom_call" | custom-call | tf_op jit(solution)/shard_map/pallas_call | solution.py:219
  80.2 0.5 slice.14
  81.4 0.0 copy-done.9
  81.4 0.0 copy-done.8
  81.4 0.0 copy-done.7
  81.4 0.6 multiply_subtract_fusion.1
  82.1 0.0 copy-done
  82.1 1.1 %fusion.2 = f32[768,256]{1,0:T(8,128)S(1)} fusion(f32[768,256]{1,0:T(8,128)S(1)} %copy-done, f32[768,896]{1,0:T(8,128)S(1)} %get-tuple-element.11), kind=kOutput, calls=%fused_computation.2 | convolution fusion | flops 905969664 | bytes 3932160 | tf_op jit(solution)/shard_map/dot_general | solution.py:20
  83.2 0.0 copy-start.5
  83.2 0.0 copy-start.6
  83.2 0.0 copy-start.4
  83.2 2.6 %multiply_reduce_fusion = (f32[]{:T(128)}, f32[768,256]{1,0:T(8,128)S(1)}) fusion(f32[768,256]{1,0:T(8,128)S(1)} %fusion.2, f32[768,896]{1,0:T(8,128)S(1)} %get-tuple-element.11), kind=kOutput, calls=%fused_computation.14 | convolution fusion | flops 906362880 | bytes 3932164 | tf_op jit(solution)/shard_map/dot_general | solution.py:261
  86.5 0.0 copy-done.5
  86.5 0.0 copy-done.6
  86.6 0.0 copy-start.2
  86.6 0.0 copy-start.3
  86.6 0.0 copy-done.4
  86.6 1.2 %fusion.25 = (bf16[48,768]{1,0:T(8,128)(2,1)}, f32[48,768]{1,0:T(8,128)}) fusion(f32[48,768]{1,0:T(8,128)S(1)} %copy-done.4, f32[768,256]{1,0:T(8,128)S(1)} %copy-done, f32[48,256]{1,0:T(8,128)S(1)} %get-tuple-element.16, f32[48,256]{1,0:T(8,128)S(1)} %get-tuple-element.15), kind=kOutput, calls=%fused_computation.41 | convolution fusion | flops 56893440 | bytes 1253376 | tf_op jit(solution)/shard_map/dot_general | solution.py:282
  87.8 0.8 fusion.9
  88.6 0.5 fusion.8
  89.1 0.0 copy-done.2
  89.1 0.0 copy-done.3
  89.1 0.8 fusion.26
  90.0 0.5 fusion.7
  90.5 0.8 fusion.27
  91.3 0.5 fusion.6
  91.8 0.8 fusion.28
  92.6 0.5 fusion.5
  93.1 0.8 fusion.29
  93.9 1.4 %fusion.4 = f32[768,256]{1,0:T(8,128)} fusion(f32[768,256]{1,0:T(8,128)S(1)} %fusion.5, f32[256,256]{1,0:T(8,128)S(1)} %fusion.29), kind=kOutput, calls=%fused_computation.5 | convolution fusion | flops 302579712 | bytes 1835008 | tf_op jit(solution)/shard_map/dot_general | solution.py:20
  (3 shorter events, 0.1 us)
Async XLA Ops:
  0.6 81.4 %copy-start = (f32[768,256]{1,0:T(8,128)S(1)}, f32[768,256]{1,0:T(8,128)}, u32[]{:S(2)}) copy-start(f32[768,256]{1,0:T(8,128)} %param.12) | copy-start | bytes 2359300
  0.6 80.8 %copy-start.9 = (f32[8,48]{1,0:T(8,128)S(1)}, f32[8,48]{1,0:T(8,128)}, u32[]{:S(2)}) copy-start(f32[8,48]{1,0:T(8,128)} %param.17) | copy-start | bytes 4612
  0.7 80.8 %copy-start.8 = (f32[8,48]{1,0:T(8,128)S(1)}, f32[8,48]{1,0:T(8,128)}, u32[]{:S(2)}) copy-start(f32[8,48]{1,0:T(8,128)} %param.16) | copy-start | bytes 4612
  0.7 80.8 %copy-start.7 = (f32[8,48]{1,0:T(8,128)S(1)}, f32[8,48]{1,0:T(8,128)}, u32[]{:S(2)}) copy-start(f32[8,48]{1,0:T(8,128)} %param.15) | copy-start | bytes 4612
  1.6 1.7 %copy-start.1 = (bf16[2,1,1,768,768]{4,3,2,1,0:T(8,128)(2,1)S(1)}, bf16[2,1,1,768,768]{4,3,2,1,0:T(8,128)(2,1)}, u32[]{:S(2)}) copy-start(bf16[2,1,1,768,768]{4,3,2,1,0:T(8,128)(2,1)} %param.9) | copy-start | bytes 7077892
  83.2 3.4 %copy-start.5 = (f32[48,256]{1,0:T(8,128)S(1)}, f32[48,256]{1,0:T(8,128)}, u32[]{:S(2)}) copy-start(f32[48,256]{1,0:T(8,128)} %param.13) | copy-start | bytes 147460
  83.2 3.4 %copy-start.6 = (f32[48,256]{1,0:T(8,128)S(1)}, f32[48,256]{1,0:T(8,128)}, u32[]{:S(2)}) copy-start(f32[48,256]{1,0:T(8,128)} %param.14) | copy-start | bytes 147460
  83.2 3.4 %copy-start.4 = (f32[48,768]{1,0:T(8,128)S(1)}, f32[48,768]{1,0:T(8,128)}, u32[]{:S(2)}) copy-start(f32[48,768]{1,0:T(8,128)} %param.11) | copy-start | bytes 442372
  86.6 2.5 %copy-start.2 = (f32[48,256]{1,0:T(8,128)}, f32[48,256]{1,0:T(8,128)S(1)}, u32[]{:S(2)}) copy-start(f32[48,256]{1,0:T(8,128)S(1)} %get-tuple-element.15) | copy-start | bytes 147460
  86.6 2.5 %copy-start.3 = (f32[48,256]{1,0:T(8,128)}, f32[48,256]{1,0:T(8,128)S(1)}, u32[]{:S(2)}) copy-start(f32[48,256]{1,0:T(8,128)S(1)} %get-tuple-element.16) | copy-start | bytes 147460

commit v12 on v10

--- a/solution.py
+++ b/solution.py
@@ -126,15 +126,45 @@
 
     pack(1 - core)
     pl.semaphore_wait(barrier, len(peers))
-    s = next_sem()
-    c = pltpu.make_async_remote_copy(
-        src_ref=x_ref.at[core_piece(1 - core)], dst_ref=core_recv.at[0], send_sem=send_sem.at[s],
-        recv_sem=recv_sem.at[s], device_id=core_dev(0), device_id_type=MESH)
-    c.start()
+    order = far_first(nx) + [0]
+    partner_pos = xi + (yi - xi) * (1 - core)
+
+    def half_rows(h, q):
+        return pl.ds(pl.multiple_of(h * rc + q * rx, 8), rx)
+
+    core_copies = []
+    for k in order:
+        q = (partner_pos + k) % nx
+        s = next_sem()
+        c = pltpu.make_async_remote_copy(
+            src_ref=x_ref.at[half_rows(1 - core, q)], dst_ref=core_recv.at[0].at[x_piece(q)],
+            send_sem=send_sem.at[s], recv_sem=recv_sem.at[s], device_id=core_dev(0), device_id_type=MESH)
+        c.start()
+        core_copies.append((c, s))
     pack(core)
-    c.wait()
-    core_sum[...] = x_ref[core_piece(core)] + core_recv[0]
-    reduce_stage(core_sum, nx, pos_a, x_dev, x_recv, x_sum, x_piece)
+    a_copies = []
+    for (c, s), k in zip(core_copies, order):
+        q = (pos_a + k) % nx
+        pltpu.make_async_remote_copy(
+            src_ref=x_ref.at[half_rows(1 - core, q)], dst_ref=core_recv.at[0].at[x_piece(q)],
+            send_sem=send_sem.at[s], recv_sem=recv_sem.at[s], device_id=core_dev(0),
+            device_id_type=MESH).wait_recv()
+        core_sum[x_piece(q)] = x_ref[half_rows(core, q)] + core_recv[0, x_piece(q)]
+        if k != 0:
+            s2 = next_sem()
+            c2 = pltpu.make_async_remote_copy(
+                src_ref=core_sum.at[x_piece(q)], dst_ref=x_recv.at[k - 1], send_sem=send_sem.at[s2],
+                recv_sem=recv_sem.at[s2], device_id=x_dev(q), device_id_type=MESH)
+            c2.start()
+            a_copies.append(c2)
+    for c, s in core_copies:
+        c.wait_send()
+    for c2 in a_copies:
+        c2.wait()
+    acc = core_sum[x_piece(pos_a)]
+    for k in range(1, nx):
+        acc = acc + x_recv[k - 1]
+    x_sum[...] = acc
     if zcols > cols:
         y_pad[:, cols:] = jnp.zeros((ry, zcols - cols), jnp.float32)
     reduce_stage(x_sum, ny, pos_b, y_dev, y_recv, y_pad.at[:, pl.ds(0, cols)], y_piece)
@@ -212,7 +242,7 @@
     ry = rx // ny
     zcols = 128 * nh * ((cols + 128 * nh - 1) // (128 * nh))
     cz = zcols // nh
-    n_sems = 2 * (1 + (nx - 1) + (ny - 1) + (nh - 1)) + 1 + (nx - 1)
+    n_sems = 2 * (1 + (nx - 1) + (ny - 1) + (nh - 1)) + 1 + 2 * (nx - 1)
     f32 = jnp.float32
     return pl.pallas_call(
         functools.partial(_allreduce_kernel, nx, ny, nz),

time: 93.7 us -> 92.3 us (0.985)
  no operation moved by 1% of the time
where the time goes in v12:
time: 92.3 us; the launch traced here: 92.1 us
  Pallas kernels  73.7 us (80%)
  matrix products  12.2 us (13%)
  local copies, waits for them, and re-layouts  2.37 us (3%)
  between operations  2.33 us (3%)
  other arithmetic  1.45 us (2%)
    pallas_call x1, Pallas kernels, allreduce(): pl.pallas_call(functools.partial(_allreduce_kernel, nx, ny, nz), out_shap...  73.7 us
    dot_general x11, matrix products, matmul(): jnp.dot(left, right, precision=HIGH, preferred_element_type=jnp.float32)  8.42 us
    dot_general x1, matrix products, per_device(): lax.dot_general(total, projected_all, (((0,), (0,)), ((), ())), precision...  2.63 us

profile of v12, /device:TPU:1, one launch (start us, length us, event | category | flops | bytes accessed | tf_op | source)
XLA Modules:
  0.0 92.1 jit_solution(1584842304032879257)
XLA Ops:
  0.6 0.0 copy-start
  0.6 0.0 copy-start.9
  0.7 0.0 copy-start.8
  0.7 0.0 copy-start.7
  0.7 0.8 convert_add_fusion
  1.5 0.1 add.49
  1.6 0.0 copy-start.1
  1.7 1.7 %copy-done.1 = bf16[2,1,1,768,768]{4,3,2,1,0:T(8,128)(2,1)S(1)} copy-done((bf16[2,1,1,768,768]{4,3,2,1,0:T(8,128)(2,1)S(1)}, bf16[2,1,1,768,768]{4,3,2,1,0:T(8,128)(2,1)}, u32[]{:S(2)}) %copy-start.1) | copy-done | bytes 2359320
  3.3 73.7 %shard_map.152 = (f32[768,896]{1,0:T(8,128)S(1)}, f32[8,128]{1,0:T(8,128)S(1)}) custom-call(bf16[2,768,768]{2,1,0:T(8,128)(2,1)S(1)} %bitcast.29, f32[768,128]{1,0:T(8,128)S(1)} %pad.4.tail_ref), custom_call_target="tpu_custom_call" | custom-call | tf_op jit(solution)/shard_map/pallas_call | solution.py:247
  77.0 0.5 slice.14
  78.2 0.0 copy-done.9
  78.2 0.0 copy-done.8
  78.3 0.0 copy-done.7
  78.3 0.6 multiply_subtract_fusion.1
  78.9 0.0 copy-done
  78.9 1.1 %fusion.2 = f32[768,256]{1,0:T(8,128)S(1)} fusion(f32[768,256]{1,0:T(8,128)S(1)} %copy-done, f32[768,896]{1,0:T(8,128)S(1)} %get-tuple-element.11), kind=kOutput, calls=%fused_computation.2 | convolution fusion | flops 905969664 | bytes 3932160 | tf_op jit(solution)/shard_map/dot_general | solution.py:20
  80.0 0.0 copy-start.5
  80.0 0.0 copy-start.6
  80.0 0.0 copy-start.4
  80.0 2.6 %multiply_reduce_fusion = (f32[]{:T(128)}, f32[768,256]{1,0:T(8,128)S(1)}) fusion(f32[768,256]{1,0:T(8,128)S(1)} %fusion.2, f32[768,896]{1,0:T(8,128)S(1)} %get-tuple-element.11), kind=kOutput, calls=%fused_computation.14 | convolution fusion | flops 906362880 | bytes 3932164 | tf_op jit(solution)/shard_map/dot_general | solution.py:289
  83.4 0.0 copy-done.5
  83.4 0.0 copy-done.6
  83.4 0.0 copy-start.2
  83.4 0.0 copy-start.3
  83.4 0.0 copy-done.4
  83.4 1.2 %fusion.25 = (bf16[48,768]{1,0:T(8,128)(2,1)}, f32[48,768]{1,0:T(8,128)}) fusion(f32[48,768]{1,0:T(8,128)S(1)} %copy-done.4, f32[768,256]{1,0:T(8,128)S(1)} %copy-done, f32[48,256]{1,0:T(8,128)S(1)} %get-tuple-element.16, f32[48,256]{1,0:T(8,128)S(1)} %get-tuple-element.15), kind=kOutput, calls=%fused_computation.41 | convolution fusion | flops 56893440 | bytes 1253376 | tf_op jit(solution)/shard_map/dot_general | solution.py:310
  84.6 0.8 fusion.9
  85.5 0.5 fusion.8
  85.9 0.0 copy-done.2
  86.0 0.0 copy-done.3
  86.0 0.8 fusion.26
  86.8 0.5 fusion.7
  87.3 0.8 fusion.27
  88.1 0.5 fusion.6
  88.6 0.8 fusion.28
  89.4 0.5 fusion.5
  89.9 0.8 fusion.29
  90.7 1.4 %fusion.4 = f32[768,256]{1,0:T(8,128)} fusion(f32[768,256]{1,0:T(8,128)S(1)} %fusion.5, f32[256,256]{1,0:T(8,128)S(1)} %fusion.29), kind=kOutput, calls=%fused_computation.5 | convolution fusion | flops 302579712 | bytes 1835008 | tf_op jit(solution)/shard_map/dot_general | solution.py:20
  (3 shorter events, 0.1 us)
Async XLA Ops:
  0.6 78.3 %copy-start = (f32[768,256]{1,0:T(8,128)S(1)}, f32[768,256]{1,0:T(8,128)}, u32[]{:S(2)}) copy-start(f32[768,256]{1,0:T(8,128)} %param.12) | copy-start | bytes 2359300
  0.6 77.6 %copy-start.9 = (f32[8,48]{1,0:T(8,128)S(1)}, f32[8,48]{1,0:T(8,128)}, u32[]{:S(2)}) copy-start(f32[8,48]{1,0:T(8,128)} %param.17) | copy-start | bytes 4612
  0.7 77.6 %copy-start.8 = (f32[8,48]{1,0:T(8,128)S(1)}, f32[8,48]{1,0:T(8,128)}, u32[]{:S(2)}) copy-start(f32[8,48]{1,0:T(8,128)} %param.16) | copy-start | bytes 4612
  0.7 77.6 %copy-start.7 = (f32[8,48]{1,0:T(8,128)S(1)}, f32[8,48]{1,0:T(8,128)}, u32[]{:S(2)}) copy-start(f32[8,48]{1,0:T(8,128)} %param.15) | copy-start | bytes 4612
  1.6 1.7 %copy-start.1 = (bf16[2,1,1,768,768]{4,3,2,1,0:T(8,128)(2,1)S(1)}, bf16[2,1,1,768,768]{4,3,2,1,0:T(8,128)(2,1)}, u32[]{:S(2)}) copy-start(bf16[2,1,1,768,768]{4,3,2,1,0:T(8,128)(2,1)} %param.9) | copy-start | bytes 7077892
  80.0 3.4 %copy-start.5 = (f32[48,256]{1,0:T(8,128)S(1)}, f32[48,256]{1,0:T(8,128)}, u32[]{:S(2)}) copy-start(f32[48,256]{1,0:T(8,128)} %param.13) | copy-start | bytes 147460
  80.0 3.4 %copy-start.6 = (f32[48,256]{1,0:T(8,128)S(1)}, f32[48,256]{1,0:T(8,128)}, u32[]{:S(2)}) copy-start(f32[48,256]{1,0:T(8,128)} %param.14) | copy-start | bytes 147460
  80.0 3.4 %copy-start.4 = (f32[48,768]{1,0:T(8,128)S(1)}, f32[48,768]{1,0:T(8,128)}, u32[]{:S(2)}) copy-start(f32[48,768]{1,0:T(8,128)} %param.11) | copy-start | bytes 442372
  83.4 2.5 %copy-start.2 = (f32[48,256]{1,0:T(8,128)}, f32[48,256]{1,0:T(8,128)S(1)}, u32[]{:S(2)}) copy-start(f32[48,256]{1,0:T(8,128)S(1)} %get-tuple-element.15) | copy-start | bytes 147460
  83.4 2.5 %copy-start.3 = (f32[48,256]{1,0:T(8,128)}, f32[48,256]{1,0:T(8,128)S(1)}, u32[]{:S(2)}) copy-start(f32[48,256]{1,0:T(8,128)S(1)} %get-tuple-element.16) | copy-start | bytes 147460

commit v13 on v12

--- a/solution.py
+++ b/solution.py
@@ -21,7 +21,7 @@
 
 
 def _allreduce_kernel(nx, ny, nz, g_ref, tail_ref, out_ref, sq_ref, x_ref, core_recv, core_sum, x_recv, x_sum, y_recv,
-                      y_pad, z_recv, z_sum, pair_recv, z_full, y_out, x_out, core_out, send_sem, recv_sem):
+                      y_pad, z_recv, z_sum, pair_recv, z_full, y_out, x_wide, core_out, send_sem, recv_sem):
     rows, cols = x_ref.shape
     zcols = y_pad.shape[1]
     width = g_ref.shape[-1]
@@ -178,8 +178,62 @@
     c.wait()
     z_full[...] = z_sum[...] + pair_recv[...]
 
-    gather_stage(z_full, nh, zi, z_dev, y_out, z_piece)
-    gather_stage(y_out.at[:, pl.ds(0, cols)], ny, pos_b, y_dev, x_out, y_piece)
+    x_out = x_wide.at[:, pl.ds(0, cols)]
+
+    def slab(q):
+        return pl.ds(pl.multiple_of(q * cz, 128), cz)
+
+    z_sends = []
+    for k in far_first(nh):
+        j = (zi + k) % nh
+        s = next_sem()
+        c = pltpu.make_async_remote_copy(
+            src_ref=z_full, dst_ref=y_out.at[:, slab(zi)], send_sem=send_sem.at[s],
+            recv_sem=recv_sem.at[s], device_id=z_dev(j), device_id_type=MESH)
+        c.start()
+        z_sends.append((c, s, k))
+    y_out[:, slab(zi)] = z_full[...]
+    fwd_base = counter[0]
+    counter[0] += nh * (ny - 1)
+    slab_order = [0] + sorted(range(1, nh), key=lambda k: (min(k, nh - k), k))
+    b_copies = []
+
+    def forward(t, k):
+        q = (zi + nh - k) % nh
+        src_slab = z_full if k == 0 else y_out.at[:, slab(q)]
+        for kb in range(1, ny):
+            jb = (pos_b + kb) % ny
+            sb = fwd_base + t * (ny - 1) + kb - 1
+            cb = pltpu.make_async_remote_copy(
+                src_ref=src_slab, dst_ref=x_wide.at[y_piece(pos_b), slab(q)], send_sem=send_sem.at[sb],
+                recv_sem=recv_sem.at[sb], device_id=y_dev(jb), device_id_type=MESH)
+            cb.start()
+            b_copies.append(cb)
+
+    forward(0, 0)
+    z_by_k = {k: (c, s) for c, s, k in z_sends}
+    for t, k in enumerate(slab_order):
+        if k == 0:
+            continue
+        c, s = z_by_k[k]
+        q = (zi + nh - k) % nh
+        pltpu.make_async_remote_copy(
+            src_ref=z_full, dst_ref=y_out.at[:, slab(q)], send_sem=send_sem.at[s],
+            recv_sem=recv_sem.at[s], device_id=z_dev(q), device_id_type=MESH).wait_recv()
+        forward(t, k)
+    x_wide[y_piece(pos_b), :] = y_out[...]
+    for c, s, k in z_sends:
+        c.wait_send()
+    for cb in b_copies:
+        cb.wait_send()
+    for t, k in enumerate(slab_order):
+        q = (zi + nh - k) % nh
+        for kb in range(1, ny):
+            jb = (pos_b + ny - kb) % ny
+            sb = fwd_base + t * (ny - 1) + kb - 1
+            pltpu.make_async_remote_copy(
+                src_ref=z_full, dst_ref=x_wide.at[y_piece(jb), slab(q)], send_sem=send_sem.at[sb],
+                recv_sem=recv_sem.at[sb], device_id=y_dev(jb), device_id_type=MESH).wait_recv()
     half_off = core * rc
     other_off = (1 - core) * rc
 
@@ -242,7 +296,7 @@
     ry = rx // ny
     zcols = 128 * nh * ((cols + 128 * nh - 1) // (128 * nh))
     cz = zcols // nh
-    n_sems = 2 * (1 + (nx - 1) + (ny - 1) + (nh - 1)) + 1 + 2 * (nx - 1)
+    n_sems = 2 * (1 + (nx - 1) + (ny - 1) + (nh - 1)) + 1 + 2 * (nx - 1) + (nh - 1) * (ny - 1)
     f32 = jnp.float32
     return pl.pallas_call(
         functools.partial(_allreduce_kernel, nx, ny, nz),
@@ -262,7 +316,7 @@
             pltpu.VMEM((ry, cz), f32),
             pltpu.VMEM((ry, cz), f32),
             pltpu.VMEM((ry, zcols), f32),
-            pltpu.VMEM((rx, cols), f32),
+            pltpu.VMEM((rx, zcols), f32),
             pltpu.VMEM((rc, cols), f32),
             pltpu.SemaphoreType.DMA((n_sems,)),
             pltpu.SemaphoreType.DMA((n_sems,)),

time: 92.3 us -> 89.7 us (0.972)
  Pallas kernels: 73.7 us -> 70.8 us
    pallas_call x1, Pallas kernels: 73.7 us -> 70.8 us  [allreduce(): pl.pallas_call(functools.partial(_allreduce_kernel, nx, ny, nz), out_shap...]
where the time goes in v13:
time: 89.7 us; the launch traced here: 89.2 us
  Pallas kernels  70.8 us (79%)
  matrix products  12.2 us (14%)
  local copies, waits for them, and re-layouts  2.37 us (3%)
  between operations  2.33 us (3%)
  other arithmetic  1.45 us (2%)
    pallas_call x1, Pallas kernels, allreduce(): pl.pallas_call(functools.partial(_allreduce_kernel, nx, ny, nz), out_shap...  70.8 us
    dot_general x11, matrix products, matmul(): jnp.dot(left, right, precision=HIGH, preferred_element_type=jnp.float32)  8.41 us
    dot_general x1, matrix products, per_device(): lax.dot_general(total, projected_all, (((0,), (0,)), ((), ())), precision...  2.63 us

profile of v13, /device:TPU:1, one launch (start us, length us, event | category | flops | bytes accessed | tf_op | source)
XLA Modules:
  0.0 89.2 jit_solution(9386475719319832951)
XLA Ops:
  0.6 0.0 copy-start
  0.6 0.0 copy-start.9
  0.7 0.0 copy-start.8
  0.7 0.0 copy-start.7
  0.7 0.8 convert_add_fusion
  1.5 0.1 add.49
  1.6 0.0 copy-start.1
  1.7 1.7 %copy-done.1 = bf16[2,1,1,768,768]{4,3,2,1,0:T(8,128)(2,1)S(1)} copy-done((bf16[2,1,1,768,768]{4,3,2,1,0:T(8,128)(2,1)S(1)}, bf16[2,1,1,768,768]{4,3,2,1,0:T(8,128)(2,1)}, u32[]{:S(2)}) %copy-start.1) | copy-done | bytes 2359320
  3.3 70.8 %shard_map.152 = (f32[768,896]{1,0:T(8,128)S(1)}, f32[8,128]{1,0:T(8,128)S(1)}) custom-call(bf16[2,768,768]{2,1,0:T(8,128)(2,1)S(1)} %bitcast.29, f32[768,128]{1,0:T(8,128)S(1)} %pad.4.tail_ref), custom_call_target="tpu_custom_call" | custom-call | tf_op jit(solution)/shard_map/pallas_call | solution.py:301
  74.1 0.5 slice.14
  75.3 0.0 copy-done.9
  75.4 0.0 copy-done.8
  75.4 0.0 copy-done.7
  75.4 0.6 multiply_subtract_fusion.1
  76.0 0.0 copy-done
  76.0 1.1 %fusion.2 = f32[768,256]{1,0:T(8,128)S(1)} fusion(f32[768,256]{1,0:T(8,128)S(1)} %copy-done, f32[768,896]{1,0:T(8,128)S(1)} %get-tuple-element.11), kind=kOutput, calls=%fused_computation.2 | convolution fusion | flops 905969664 | bytes 3932160 | tf_op jit(solution)/shard_map/dot_general | solution.py:20
  77.1 0.0 copy-start.5
  77.1 0.0 copy-start.6
  77.1 0.0 copy-start.4
  77.1 2.6 %multiply_reduce_fusion = (f32[]{:T(128)}, f32[768,256]{1,0:T(8,128)S(1)}) fusion(f32[768,256]{1,0:T(8,128)S(1)} %fusion.2, f32[768,896]{1,0:T(8,128)S(1)} %get-tuple-element.11), kind=kOutput, calls=%fused_computation.14 | convolution fusion | flops 906362880 | bytes 3932164 | tf_op jit(solution)/shard_map/dot_general | solution.py:343
  80.5 0.0 copy-done.5
  80.5 0.0 copy-done.6
  80.5 0.0 copy-start.2
  80.5 0.0 copy-start.3
  80.5 0.0 copy-done.4
  80.6 1.2 %fusion.25 = (bf16[48,768]{1,0:T(8,128)(2,1)}, f32[48,768]{1,0:T(8,128)}) fusion(f32[48,768]{1,0:T(8,128)S(1)} %copy-done.4, f32[768,256]{1,0:T(8,128)S(1)} %copy-done, f32[48,256]{1,0:T(8,128)S(1)} %get-tuple-element.16, f32[48,256]{1,0:T(8,128)S(1)} %get-tuple-element.15), kind=kOutput, calls=%fused_computation.41 | convolution fusion | flops 56893440 | bytes 1253376 | tf_op jit(solution)/shard_map/dot_general | solution.py:364
  81.7 0.8 fusion.9
  82.6 0.5 fusion.8
  83.1 0.0 copy-done.2
  83.1 0.0 copy-done.3
  83.1 0.8 fusion.26
  83.9 0.5 fusion.7
  84.4 0.8 fusion.27
  85.2 0.5 fusion.6
  85.7 0.8 fusion.28
  86.5 0.5 fusion.5
  87.0 0.8 fusion.29
  87.8 1.4 %fusion.4 = f32[768,256]{1,0:T(8,128)} fusion(f32[768,256]{1,0:T(8,128)S(1)} %fusion.5, f32[256,256]{1,0:T(8,128)S(1)} %fusion.29), kind=kOutput, calls=%fused_computation.5 | convolution fusion | flops 302579712 | bytes 1835008 | tf_op jit(solution)/shard_map/dot_general | solution.py:20
  (3 shorter events, 0.1 us)
Async XLA Ops:
  0.6 75.4 %copy-start = (f32[768,256]{1,0:T(8,128)S(1)}, f32[768,256]{1,0:T(8,128)}, u32[]{:S(2)}) copy-start(f32[768,256]{1,0:T(8,128)} %param.12) | copy-start | bytes 2359300
  0.6 74.7 %copy-start.9 = (f32[8,48]{1,0:T(8,128)S(1)}, f32[8,48]{1,0:T(8,128)}, u32[]{:S(2)}) copy-start(f32[8,48]{1,0:T(8,128)} %param.17) | copy-start | bytes 4612
  0.7 74.7 %copy-start.8 = (f32[8,48]{1,0:T(8,128)S(1)}, f32[8,48]{1,0:T(8,128)}, u32[]{:S(2)}) copy-start(f32[8,48]{1,0:T(8,128)} %param.16) | copy-start | bytes 4612
  0.7 74.7 %copy-start.7 = (f32[8,48]{1,0:T(8,128)S(1)}, f32[8,48]{1,0:T(8,128)}, u32[]{:S(2)}) copy-start(f32[8,48]{1,0:T(8,128)} %param.15) | copy-start | bytes 4612
  1.6 1.7 %copy-start.1 = (bf16[2,1,1,768,768]{4,3,2,1,0:T(8,128)(2,1)S(1)}, bf16[2,1,1,768,768]{4,3,2,1,0:T(8,128)(2,1)}, u32[]{:S(2)}) copy-start(bf16[2,1,1,768,768]{4,3,2,1,0:T(8,128)(2,1)} %param.9) | copy-start | bytes 7077892
  77.1 3.4 %copy-start.5 = (f32[48,256]{1,0:T(8,128)S(1)}, f32[48,256]{1,0:T(8,128)}, u32[]{:S(2)}) copy-start(f32[48,256]{1,0:T(8,128)} %param.13) | copy-start | bytes 147460
  77.1 3.4 %copy-start.6 = (f32[48,256]{1,0:T(8,128)S(1)}, f32[48,256]{1,0:T(8,128)}, u32[]{:S(2)}) copy-start(f32[48,256]{1,0:T(8,128)} %param.14) | copy-start | bytes 147460
  77.1 3.4 %copy-start.4 = (f32[48,768]{1,0:T(8,128)S(1)}, f32[48,768]{1,0:T(8,128)}, u32[]{:S(2)}) copy-start(f32[48,768]{1,0:T(8,128)} %param.11) | copy-start | bytes 442372
  80.5 2.5 %copy-start.2 = (f32[48,256]{1,0:T(8,128)}, f32[48,256]{1,0:T(8,128)S(1)}, u32[]{:S(2)}) copy-start(f32[48,256]{1,0:T(8,128)S(1)} %get-tuple-element.15) | copy-start | bytes 147460
  80.5 2.5 %copy-start.3 = (f32[48,256]{1,0:T(8,128)}, f32[48,256]{1,0:T(8,128)S(1)}, u32[]{:S(2)}) copy-start(f32[48,256]{1,0:T(8,128)S(1)} %get-tuple-element.16) | copy-start | bytes 147460

commit v14 on v13

--- a/solution.py
+++ b/solution.py
@@ -55,7 +55,7 @@
     pair_dev = (g, z + 1 - 2 * zp)
 
     barrier = pltpu.get_barrier_semaphore()
-    peers = [core_dev(0), pair_dev]
+    peers = [core_dev(0)] + [(g, 1 - zp + 2 * j) for j in range(nh)]
     peers += [x_dev((pos_a + k) % nx) for k in range(1, nx)]
     peers += [y_dev((pos_b + k) % ny) for k in range(1, ny)]
     peers += [z_dev((zi + k) % nh) for k in range(1, nh)]
@@ -170,59 +170,56 @@
     reduce_stage(x_sum, ny, pos_b, y_dev, y_recv, y_pad.at[:, pl.ds(0, cols)], y_piece)
     reduce_stage(y_pad, nh, zi, z_dev, z_recv, z_sum, z_piece)
 
-    s = next_sem()
-    c = pltpu.make_async_remote_copy(
-        src_ref=z_sum, dst_ref=pair_recv, send_sem=send_sem.at[s], recv_sem=recv_sem.at[s],
-        device_id=pair_dev, device_id_type=MESH)
-    c.start()
-    c.wait()
-    z_full[...] = z_sum[...] + pair_recv[...]
-
     x_out = x_wide.at[:, pl.ds(0, cols)]
+    y_parts = pair_recv
 
     def slab(q):
         return pl.ds(pl.multiple_of(q * cz, 128), cz)
 
+    sbase = counter[0]
+    counter[0] += nz - 1
+    rbase = counter[0]
+    counter[0] += nz
     z_sends = []
-    for k in far_first(nh):
-        j = (zi + k) % nh
-        s = next_sem()
+    for idx, off in enumerate(far_first(nz)):
         c = pltpu.make_async_remote_copy(
-            src_ref=z_full, dst_ref=y_out.at[:, slab(zi)], send_sem=send_sem.at[s],
-            recv_sem=recv_sem.at[s], device_id=z_dev(j), device_id_type=MESH)
+            src_ref=z_sum, dst_ref=y_parts.at[zp, :, slab(zi)], send_sem=send_sem.at[sbase + idx],
+            recv_sem=recv_sem.at[rbase + z], device_id=(g, (z + off) % nz), device_id_type=MESH)
         c.start()
-        z_sends.append((c, s, k))
-    y_out[:, slab(zi)] = z_full[...]
+        z_sends.append(c)
+    y_parts[zp, :, slab(zi)] = z_sum[...]
     fwd_base = counter[0]
     counter[0] += nh * (ny - 1)
     slab_order = [0] + sorted(range(1, nh), key=lambda k: (min(k, nh - k), k))
     b_copies = []
 
-    def forward(t, k):
-        q = (zi + nh - k) % nh
-        src_slab = z_full if k == 0 else y_out.at[:, slab(q)]
+    def forward(t, q):
         for kb in range(1, ny):
             jb = (pos_b + kb) % ny
             sb = fwd_base + t * (ny - 1) + kb - 1
             cb = pltpu.make_async_remote_copy(
-                src_ref=src_slab, dst_ref=x_wide.at[y_piece(pos_b), slab(q)], send_sem=send_sem.at[sb],
-                recv_sem=recv_sem.at[sb], device_id=y_dev(jb), device_id_type=MESH)
+                src_ref=y_out.at[:, slab(q)], dst_ref=x_wide.at[y_piece(pos_b), slab(q)],
+                send_sem=send_sem.at[sb], recv_sem=recv_sem.at[sb], device_id=y_dev(jb), device_id_type=MESH)
             cb.start()
             b_copies.append(cb)
 
-    forward(0, 0)
-    z_by_k = {k: (c, s) for c, s, k in z_sends}
+    def wait_part(p, q):
+        zs = 2 * q + p
+        pltpu.make_async_remote_copy(
+            src_ref=z_sum, dst_ref=y_parts.at[p, :, slab(q)], send_sem=send_sem.at[sbase],
+            recv_sem=recv_sem.at[rbase + zs], device_id=(g, zs), device_id_type=MESH).wait_recv()
+
     for t, k in enumerate(slab_order):
+        q = (zi + nh - k) % nh
         if k == 0:
-            continue
-        c, s = z_by_k[k]
-        q = (zi + nh - k) % nh
-        pltpu.make_async_remote_copy(
-            src_ref=z_full, dst_ref=y_out.at[:, slab(q)], send_sem=send_sem.at[s],
-            recv_sem=recv_sem.at[s], device_id=z_dev(q), device_id_type=MESH).wait_recv()
-        forward(t, k)
+            wait_part(1 - zp, q)
+        else:
+            wait_part(0, q)
+            wait_part(1, q)
+        y_out[:, slab(q)] = y_parts[0, :, slab(q)] + y_parts[1, :, slab(q)]
+        forward(t, q)
     x_wide[y_piece(pos_b), :] = y_out[...]
-    for c, s, k in z_sends:
+    for c in z_sends:
         c.wait_send()
     for cb in b_copies:
         cb.wait_send()
@@ -296,7 +293,7 @@
     ry = rx // ny
     zcols = 128 * nh * ((cols + 128 * nh - 1) // (128 * nh))
     cz = zcols // nh
-    n_sems = 2 * (1 + (nx - 1) + (ny - 1) + (nh - 1)) + 1 + 2 * (nx - 1) + (nh - 1) * (ny - 1)
+    n_sems = 2 * (1 + (nx - 1) + (ny - 1) + (nh - 1)) + 1 + 2 * (nx - 1) + (nh - 1) * (ny - 1) + 2 * nz
     f32 = jnp.float32
     return pl.pallas_call(
         functools.partial(_allreduce_kernel, nx, ny, nz),
@@ -313,7 +310,7 @@
             pltpu.VMEM((ry, zcols), f32),
             pltpu.VMEM((nh - 1, ry, cz), f32),
             pltpu.VMEM((ry, cz), f32),
-            pltpu.VMEM((ry, cz), f32),
+            pltpu.VMEM((2, ry, zcols), f32),
             pltpu.VMEM((ry, cz), f32),
             pltpu.VMEM((ry, zcols), f32),
             pltpu.VMEM((rx, zcols), f32),

time: 89.7 us -> 89 us (level)
  no operation moved by 1% of the time
where the time goes in v14:
time: 89 us; the launch traced here: 88.8 us
  Pallas kernels  70.5 us (79%)
  matrix products  12.2 us (14%)
  local copies, waits for them, and re-layouts  2.37 us (3%)
  between operations  2.33 us (3%)
  other arithmetic  1.45 us (2%)
    pallas_call x1, Pallas kernels, allreduce(): pl.pallas_call(functools.partial(_allreduce_kernel, nx, ny, nz), out_shap...  70.5 us
    dot_general x11, matrix products, matmul(): jnp.dot(left, right, precision=HIGH, preferred_element_type=jnp.float32)  8.42 us
    dot_general x1, matrix products, per_device(): lax.dot_general(total, projected_all, (((0,), (0,)), ((), ())), precision...  2.63 us

profile of v14, /device:TPU:1, one launch (start us, length us, event | category | flops | bytes accessed | tf_op | source)
XLA Modules:
  0.0 88.8 jit_solution(11667913383337754365)
XLA Ops:
  0.6 0.0 copy-start
  0.6 0.0 copy-start.9
  0.7 0.0 copy-start.8
  0.7 0.0 copy-start.7
  0.7 0.8 convert_add_fusion
  1.5 0.1 add.49
  1.6 0.0 copy-start.1
  1.7 1.7 %copy-done.1 = bf16[2,1,1,768,768]{4,3,2,1,0:T(8,128)(2,1)S(1)} copy-done((bf16[2,1,1,768,768]{4,3,2,1,0:T(8,128)(2,1)S(1)}, bf16[2,1,1,768,768]{4,3,2,1,0:T(8,128)(2,1)}, u32[]{:S(2)}) %copy-start.1) | copy-done | bytes 2359320
  3.3 70.5 %shard_map.152 = (f32[768,896]{1,0:T(8,128)S(1)}, f32[8,128]{1,0:T(8,128)S(1)}) custom-call(bf16[2,768,768]{2,1,0:T(8,128)(2,1)S(1)} %bitcast.29, f32[768,128]{1,0:T(8,128)S(1)} %pad.4.tail_ref), custom_call_target="tpu_custom_call" | custom-call | tf_op jit(solution)/shard_map/pallas_call | solution.py:298
  73.8 0.5 slice.14
  75.0 0.0 copy-done.9
  75.0 0.0 copy-done.8
  75.0 0.0 copy-done.7
  75.0 0.6 multiply_subtract_fusion.1
  75.7 0.0 copy-done
  75.7 1.1 %fusion.2 = f32[768,256]{1,0:T(8,128)S(1)} fusion(f32[768,256]{1,0:T(8,128)S(1)} %copy-done, f32[768,896]{1,0:T(8,128)S(1)} %get-tuple-element.11), kind=kOutput, calls=%fused_computation.2 | convolution fusion | flops 905969664 | bytes 3932160 | tf_op jit(solution)/shard_map/dot_general | solution.py:20
  76.8 0.0 copy-start.5
  76.8 0.0 copy-start.6
  76.8 0.0 copy-start.4
  76.8 2.6 %multiply_reduce_fusion = (f32[]{:T(128)}, f32[768,256]{1,0:T(8,128)S(1)}) fusion(f32[768,256]{1,0:T(8,128)S(1)} %fusion.2, f32[768,896]{1,0:T(8,128)S(1)} %get-tuple-element.11), kind=kOutput, calls=%fused_computation.14 | convolution fusion | flops 906362880 | bytes 3932164 | tf_op jit(solution)/shard_map/dot_general | solution.py:340
  80.1 0.0 copy-done.5
  80.1 0.0 copy-done.6
  80.2 0.0 copy-start.2
  80.2 0.0 copy-start.3
  80.2 0.0 copy-done.4
  80.2 1.2 %fusion.25 = (bf16[48,768]{1,0:T(8,128)(2,1)}, f32[48,768]{1,0:T(8,128)}) fusion(f32[48,768]{1,0:T(8,128)S(1)} %copy-done.4, f32[768,256]{1,0:T(8,128)S(1)} %copy-done, f32[48,256]{1,0:T(8,128)S(1)} %get-tuple-element.16, f32[48,256]{1,0:T(8,128)S(1)} %get-tuple-element.15), kind=kOutput, calls=%fused_computation.41 | convolution fusion | flops 56893440 | bytes 1253376 | tf_op jit(solution)/shard_map/dot_general | solution.py:361
  81.4 0.8 fusion.9
  82.2 0.5 fusion.8
  82.7 0.0 copy-done.2
  82.7 0.0 copy-done.3
  82.7 0.8 fusion.26
  83.5 0.5 fusion.7
  84.0 0.8 fusion.27
  84.9 0.5 fusion.6
  85.4 0.8 fusion.28
  86.2 0.5 fusion.5
  86.7 0.8 fusion.29
  87.5 1.4 %fusion.4 = f32[768,256]{1,0:T(8,128)} fusion(f32[768,256]{1,0:T(8,128)S(1)} %fusion.5, f32[256,256]{1,0:T(8,128)S(1)} %fusion.29), kind=kOutput, calls=%fused_computation.5 | convolution fusion | flops 302579712 | bytes 1835008 | tf_op jit(solution)/shard_map/dot_general | solution.py:20
  (3 shorter events, 0.1 us)
Async XLA Ops:
  0.6 75.0 %copy-start = (f32[768,256]{1,0:T(8,128)S(1)}, f32[768,256]{1,0:T(8,128)}, u32[]{:S(2)}) copy-start(f32[768,256]{1,0:T(8,128)} %param.12) | copy-start | bytes 2359300
  0.6 74.4 %copy-start.9 = (f32[8,48]{1,0:T(8,128)S(1)}, f32[8,48]{1,0:T(8,128)}, u32[]{:S(2)}) copy-start(f32[8,48]{1,0:T(8,128)} %param.17) | copy-start | bytes 4612
  0.7 74.4 %copy-start.8 = (f32[8,48]{1,0:T(8,128)S(1)}, f32[8,48]{1,0:T(8,128)}, u32[]{:S(2)}) copy-start(f32[8,48]{1,0:T(8,128)} %param.16) | copy-start | bytes 4612
  0.7 74.4 %copy-start.7 = (f32[8,48]{1,0:T(8,128)S(1)}, f32[8,48]{1,0:T(8,128)}, u32[]{:S(2)}) copy-start(f32[8,48]{1,0:T(8,128)} %param.15) | copy-start | bytes 4612
  1.6 1.7 %copy-start.1 = (bf16[2,1,1,768,768]{4,3,2,1,0:T(8,128)(2,1)S(1)}, bf16[2,1,1,768,768]{4,3,2,1,0:T(8,128)(2,1)}, u32[]{:S(2)}) copy-start(bf16[2,1,1,768,768]{4,3,2,1,0:T(8,128)(2,1)} %param.9) | copy-start | bytes 7077892
  76.8 3.4 %copy-start.5 = (f32[48,256]{1,0:T(8,128)S(1)}, f32[48,256]{1,0:T(8,128)}, u32[]{:S(2)}) copy-start(f32[48,256]{1,0:T(8,128)} %param.13) | copy-start | bytes 147460
  76.8 3.4 %copy-start.6 = (f32[48,256]{1,0:T(8,128)S(1)}, f32[48,256]{1,0:T(8,128)}, u32[]{:S(2)}) copy-start(f32[48,256]{1,0:T(8,128)} %param.14) | copy-start | bytes 147460
  76.8 3.4 %copy-start.4 = (f32[48,768]{1,0:T(8,128)S(1)}, f32[48,768]{1,0:T(8,128)}, u32[]{:S(2)}) copy-start(f32[48,768]{1,0:T(8,128)} %param.11) | copy-start | bytes 442372
  80.2 2.5 %copy-start.2 = (f32[48,256]{1,0:T(8,128)}, f32[48,256]{1,0:T(8,128)S(1)}, u32[]{:S(2)}) copy-start(f32[48,256]{1,0:T(8,128)S(1)} %get-tuple-element.15) | copy-start | bytes 147460
  80.2 2.5 %copy-start.3 = (f32[48,256]{1,0:T(8,128)}, f32[48,256]{1,0:T(8,128)S(1)}, u32[]{:S(2)}) copy-start(f32[48,256]{1,0:T(8,128)S(1)} %get-tuple-element.16) | copy-start | bytes 147460

commit v15 on v14

--- a/solution.py
+++ b/solution.py
@@ -280,7 +280,7 @@
             recv_sem=recv_sem.at[s], device_id=core_dev(0), device_id_type=MESH).wait_recv()
     other = out_ref[core_piece(1 - core)]
     rest = jnp.sum(jnp.sum(other * other, axis=0, keepdims=True), axis=1, keepdims=True)
-    sq_ref[...] = jnp.broadcast_to(own + rest, sq_ref.shape)
+    sq_ref[...] = own + rest
 
 
 def allreduce(g, tail, nx, ny, nz):
@@ -297,7 +297,7 @@
     f32 = jnp.float32
     return pl.pallas_call(
         functools.partial(_allreduce_kernel, nx, ny, nz),
-        out_shape=(jax.ShapeDtypeStruct((rows, cols), f32), jax.ShapeDtypeStruct((8, 128), f32)),
+        out_shape=(jax.ShapeDtypeStruct((rows, cols), f32), jax.ShapeDtypeStruct((1, 1), f32)),
         in_specs=[pl.BlockSpec(memory_space=pltpu.VMEM)] * 2,
         out_specs=(pl.BlockSpec(memory_space=pltpu.VMEM),) * 2,
         scratch_shapes=[

time: 89 us -> 89 us (level)
  no operation moved by 1% of the time
where the time goes in v15:
time: 89 us; the launch traced here: 88.8 us
  Pallas kernels  71 us (80%)
  matrix products  12.2 us (14%)
  between operations  2.31 us (3%)
  local copies, waits for them, and re-layouts  1.85 us (2%)
  other arithmetic  1.45 us (2%)
    pallas_call x1, Pallas kernels, allreduce(): pl.pallas_call(functools.partial(_allreduce_kernel, nx, ny, nz), out_shap...  71 us
    dot_general x11, matrix products, matmul(): jnp.dot(left, right, precision=HIGH, preferred_element_type=jnp.float32)  8.42 us
    dot_general x1, matrix products, per_device(): lax.dot_general(total, projected_all, (((0,), (0,)), ((), ())), precision...  2.63 us

profile of v15, /device:TPU:1, one launch (start us, length us, event | category | flops | bytes accessed | tf_op | source)
XLA Modules:
  0.0 88.8 jit_solution(16582415904723471969)
XLA Ops:
  0.6 0.0 copy-start
  0.6 0.0 copy-start.9
  0.7 0.0 copy-start.8
  0.7 0.0 copy-start.7
  0.7 0.8 convert_add_fusion
  1.5 0.1 add.49
  1.6 0.0 copy-start.1
  1.7 1.7 %copy-done.1 = bf16[2,1,1,768,768]{4,3,2,1,0:T(8,128)(2,1)S(1)} copy-done((bf16[2,1,1,768,768]{4,3,2,1,0:T(8,128)(2,1)S(1)}, bf16[2,1,1,768,768]{4,3,2,1,0:T(8,128)(2,1)}, u32[]{:S(2)}) %copy-start.1) | copy-done | bytes 2359320
  3.3 71.0 %shard_map.152 = (f32[768,896]{1,0:T(8,128)S(1)}, f32[1,1]{1,0:T(1,128)}) custom-call(bf16[2,768,768]{2,1,0:T(8,128)(2,1)S(1)} %bitcast.29, f32[768,128]{1,0:T(8,128)S(1)} %pad.4.tail_ref), custom_call_target="tpu_custom_call" | custom-call | tf_op jit(solution)/shard_map/pallas_call | solution.py:298
  75.0 0.0 copy-done.9
  75.0 0.0 copy-done.8
  75.0 0.0 copy-done.7
  75.0 0.6 multiply_subtract_fusion.1
  75.7 0.0 copy-done
  75.7 1.1 %fusion.2 = f32[768,256]{1,0:T(8,128)S(1)} fusion(f32[768,256]{1,0:T(8,128)S(1)} %copy-done, f32[768,896]{1,0:T(8,128)S(1)} %get-tuple-element.11), kind=kOutput, calls=%fused_computation.2 | convolution fusion | flops 905969664 | bytes 3932160 | tf_op jit(solution)/shard_map/dot_general | solution.py:20
  76.8 0.0 copy-start.5
  76.8 0.0 copy-start.6
  76.8 0.0 copy-start.4
  76.8 2.6 %multiply_reduce_fusion = (f32[]{:T(128)}, f32[768,256]{1,0:T(8,128)S(1)}) fusion(f32[768,256]{1,0:T(8,128)S(1)} %fusion.2, f32[768,896]{1,0:T(8,128)S(1)} %get-tuple-element.11), kind=kOutput, calls=%fused_computation.14 | convolution fusion | flops 906362880 | bytes 3932164 | tf_op jit(solution)/shard_map/dot_general | solution.py:340
  80.1 0.0 copy-done.5
  80.1 0.0 copy-done.6
  80.2 0.0 copy-start.2
  80.2 0.0 copy-start.3
  80.2 0.0 copy-done.4
  80.2 1.2 %fusion.25 = (bf16[48,768]{1,0:T(8,128)(2,1)}, f32[48,768]{1,0:T(8,128)}) fusion(f32[48,768]{1,0:T(8,128)S(1)} %copy-done.4, f32[768,256]{1,0:T(8,128)S(1)} %copy-done, f32[48,256]{1,0:T(8,128)S(1)} %get-tuple-element.16, f32[48,256]{1,0:T(8,128)S(1)} %get-tuple-element.15), kind=kOutput, calls=%fused_computation.41 | convolution fusion | flops 56893440 | bytes 1253376 | tf_op jit(solution)/shard_map/dot_general | solution.py:361
  81.4 0.8 fusion.9
  82.2 0.5 fusion.8
  82.7 0.0 copy-done.2
  82.7 0.0 copy-done.3
  82.7 0.8 fusion.26
  83.5 0.5 fusion.7
  84.0 0.8 fusion.27
  84.9 0.5 fusion.6
  85.4 0.8 fusion.28
  86.2 0.5 fusion.5
  86.7 0.8 fusion.29
  87.5 1.4 %fusion.4 = f32[768,256]{1,0:T(8,128)} fusion(f32[768,256]{1,0:T(8,128)S(1)} %fusion.5, f32[256,256]{1,0:T(8,128)S(1)} %fusion.29), kind=kOutput, calls=%fused_computation.5 | convolution fusion | flops 302579712 | bytes 1835008 | tf_op jit(solution)/shard_map/dot_general | solution.py:20
  (3 shorter events, 0.1 us)
Async XLA Ops:
  0.6 75.0 %copy-start = (f32[768,256]{1,0:T(8,128)S(1)}, f32[768,256]{1,0:T(8,128)}, u32[]{:S(2)}) copy-start(f32[768,256]{1,0:T(8,128)} %param.12) | copy-start | bytes 2359300
  0.6 74.4 %copy-start.9 = (f32[8,48]{1,0:T(8,128)S(1)}, f32[8,48]{1,0:T(8,128)}, u32[]{:S(2)}) copy-start(f32[8,48]{1,0:T(8,128)} %param.17) | copy-start | bytes 4612
  0.7 74.4 %copy-start.8 = (f32[8,48]{1,0:T(8,128)S(1)}, f32[8,48]{1,0:T(8,128)}, u32[]{:S(2)}) copy-start(f32[8,48]{1,0:T(8,128)} %param.16) | copy-start | bytes 4612
  0.7 74.4 %copy-start.7 = (f32[8,48]{1,0:T(8,128)S(1)}, f32[8,48]{1,0:T(8,128)}, u32[]{:S(2)}) copy-start(f32[8,48]{1,0:T(8,128)} %param.15) | copy-start | bytes 4612
  1.6 1.7 %copy-start.1 = (bf16[2,1,1,768,768]{4,3,2,1,0:T(8,128)(2,1)S(1)}, bf16[2,1,1,768,768]{4,3,2,1,0:T(8,128)(2,1)}, u32[]{:S(2)}) copy-start(bf16[2,1,1,768,768]{4,3,2,1,0:T(8,128)(2,1)} %param.9) | copy-start | bytes 7077892
  76.8 3.4 %copy-start.5 = (f32[48,256]{1,0:T(8,128)S(1)}, f32[48,256]{1,0:T(8,128)}, u32[]{:S(2)}) copy-start(f32[48,256]{1,0:T(8,128)} %param.13) | copy-start | bytes 147460
  76.8 3.4 %copy-start.6 = (f32[48,256]{1,0:T(8,128)S(1)}, f32[48,256]{1,0:T(8,128)}, u32[]{:S(2)}) copy-start(f32[48,256]{1,0:T(8,128)} %param.14) | copy-start | bytes 147460
  76.8 3.4 %copy-start.4 = (f32[48,768]{1,0:T(8,128)S(1)}, f32[48,768]{1,0:T(8,128)}, u32[]{:S(2)}) copy-start(f32[48,768]{1,0:T(8,128)} %param.11) | copy-start | bytes 442372
  80.2 2.5 %copy-start.2 = (f32[48,256]{1,0:T(8,128)}, f32[48,256]{1,0:T(8,128)S(1)}, u32[]{:S(2)}) copy-start(f32[48,256]{1,0:T(8,128)S(1)} %get-tuple-element.15) | copy-start | bytes 147460
  80.2 2.5 %copy-start.3 = (f32[48,256]{1,0:T(8,128)}, f32[48,256]{1,0:T(8,128)S(1)}, u32[]{:S(2)}) copy-start(f32[48,256]{1,0:T(8,128)S(1)} %get-tuple-element.16) | copy-start | bytes 147460

commit v16 on v14

--- a/solution.py
+++ b/solution.py
@@ -238,7 +238,7 @@
         return pl.ds(pl.multiple_of(off + j * rx, 8), rx)
 
     a_sends = []
-    for k in range(1, nx):
+    for k in far_first(nx):
         j = (pos_a + k) % nx
         s = next_sem()
         c = pltpu.make_async_remote_copy(
@@ -254,7 +254,7 @@
     c.start()
     fwd.append((c, s, pos_a))
     core_out[x_piece(pos_a)] = x_out[...]
-    for c, s, k in a_sends:
+    for c, s, k in sorted(a_sends, key=lambda t: t[2]):
         j = (pos_a + nx - k) % nx
         pltpu.make_async_remote_copy(
             src_ref=x_out, dst_ref=core_out.at[x_piece(j)], send_sem=send_sem.at[s],

time: 89 us -> 88.7 us (level)
  no operation moved by 1% of the time
where the time goes in v16:
time: 88.7 us; the launch traced here: 88.5 us
  Pallas kernels  70.1 us (79%)
  matrix products  12.2 us (14%)
  local copies, waits for them, and re-layouts  2.37 us (3%)
  between operations  2.33 us (3%)
  other arithmetic  1.45 us (2%)
    pallas_call x1, Pallas kernels, allreduce(): pl.pallas_call(functools.partial(_allreduce_kernel, nx, ny, nz), out_shap...  70.1 us
    dot_general x11, matrix products, matmul(): jnp.dot(left, right, precision=HIGH, preferred_element_type=jnp.float32)  8.42 us
    dot_general x1, matrix products, per_device(): lax.dot_general(total, projected_all, (((0,), (0,)), ((), ())), precision...  2.63 us

profile of v16, /device:TPU:1, one launch (start us, length us, event | category | flops | bytes accessed | tf_op | source)
XLA Modules:
  0.0 88.5 jit_solution(7725723350539709252)
XLA Ops:
  0.6 0.0 copy-start
  0.6 0.0 copy-start.9
  0.7 0.0 copy-start.8
  0.7 0.0 copy-start.7
  0.7 0.8 convert_add_fusion
  1.5 0.1 add.49
  1.6 0.0 copy-start.1
  1.7 1.7 %copy-done.1 = bf16[2,1,1,768,768]{4,3,2,1,0:T(8,128)(2,1)S(1)} copy-done((bf16[2,1,1,768,768]{4,3,2,1,0:T(8,128)(2,1)S(1)}, bf16[2,1,1,768,768]{4,3,2,1,0:T(8,128)(2,1)}, u32[]{:S(2)}) %copy-start.1) | copy-done | bytes 2359320
  3.3 70.1 %shard_map.152 = (f32[768,896]{1,0:T(8,128)S(1)}, f32[8,128]{1,0:T(8,128)S(1)}) custom-call(bf16[2,768,768]{2,1,0:T(8,128)(2,1)S(1)} %bitcast.29, f32[768,128]{1,0:T(8,128)S(1)} %pad.4.tail_ref), custom_call_target="tpu_custom_call" | custom-call | tf_op jit(solution)/shard_map/pallas_call | solution.py:298
  73.4 0.5 slice.14
  74.7 0.0 copy-done.9
  74.7 0.0 copy-done.8
  74.7 0.0 copy-done.7
  74.7 0.6 multiply_subtract_fusion.1
  75.3 0.0 copy-done
  75.3 1.1 %fusion.2 = f32[768,256]{1,0:T(8,128)S(1)} fusion(f32[768,256]{1,0:T(8,128)S(1)} %copy-done, f32[768,896]{1,0:T(8,128)S(1)} %get-tuple-element.11), kind=kOutput, calls=%fused_computation.2 | convolution fusion | flops 905969664 | bytes 3932160 | tf_op jit(solution)/shard_map/dot_general | solution.py:20
  76.4 0.0 copy-start.5
  76.4 0.0 copy-start.6
  76.5 0.0 copy-start.4
  76.5 2.6 %multiply_reduce_fusion = (f32[]{:T(128)}, f32[768,256]{1,0:T(8,128)S(1)}) fusion(f32[768,256]{1,0:T(8,128)S(1)} %fusion.2, f32[768,896]{1,0:T(8,128)S(1)} %get-tuple-element.11), kind=kOutput, calls=%fused_computation.14 | convolution fusion | flops 906362880 | bytes 3932164 | tf_op jit(solution)/shard_map/dot_general | solution.py:340
  79.8 0.0 copy-done.5
  79.8 0.0 copy-done.6
  79.8 0.0 copy-start.2
  79.9 0.0 copy-start.3
  79.9 0.0 copy-done.4
  79.9 1.2 %fusion.25 = (bf16[48,768]{1,0:T(8,128)(2,1)}, f32[48,768]{1,0:T(8,128)}) fusion(f32[48,768]{1,0:T(8,128)S(1)} %copy-done.4, f32[768,256]{1,0:T(8,128)S(1)} %copy-done, f32[48,256]{1,0:T(8,128)S(1)} %get-tuple-element.16, f32[48,256]{1,0:T(8,128)S(1)} %get-tuple-element.15), kind=kOutput, calls=%fused_computation.41 | convolution fusion | flops 56893440 | bytes 1253376 | tf_op jit(solution)/shard_map/dot_general | solution.py:361
  81.1 0.8 fusion.9
  81.9 0.5 fusion.8
  82.4 0.0 copy-done.2
  82.4 0.0 copy-done.3
  82.4 0.8 fusion.26
  83.2 0.5 fusion.7
  83.7 0.8 fusion.27
  84.5 0.5 fusion.6
  85.0 0.8 fusion.28
  85.8 0.5 fusion.5
  86.3 0.8 fusion.29
  87.1 1.4 %fusion.4 = f32[768,256]{1,0:T(8,128)} fusion(f32[768,256]{1,0:T(8,128)S(1)} %fusion.5, f32[256,256]{1,0:T(8,128)S(1)} %fusion.29), kind=kOutput, calls=%fused_computation.5 | convolution fusion | flops 302579712 | bytes 1835008 | tf_op jit(solution)/shard_map/dot_general | solution.py:20
  (3 shorter events, 0.1 us)
Async XLA Ops:
  0.6 74.7 %copy-start = (f32[768,256]{1,0:T(8,128)S(1)}, f32[768,256]{1,0:T(8,128)}, u32[]{:S(2)}) copy-start(f32[768,256]{1,0:T(8,128)} %param.12) | copy-start | bytes 2359300
  0.6 74.0 %copy-start.9 = (f32[8,48]{1,0:T(8,128)S(1)}, f32[8,48]{1,0:T(8,128)}, u32[]{:S(2)}) copy-start(f32[8,48]{1,0:T(8,128)} %param.17) | copy-start | bytes 4612
  0.7 74.0 %copy-start.8 = (f32[8,48]{1,0:T(8,128)S(1)}, f32[8,48]{1,0:T(8,128)}, u32[]{:S(2)}) copy-start(f32[8,48]{1,0:T(8,128)} %param.16) | copy-start | bytes 4612
  0.7 74.0 %copy-start.7 = (f32[8,48]{1,0:T(8,128)S(1)}, f32[8,48]{1,0:T(8,128)}, u32[]{:S(2)}) copy-start(f32[8,48]{1,0:T(8,128)} %param.15) | copy-start | bytes 4612
  1.6 1.7 %copy-start.1 = (bf16[2,1,1,768,768]{4,3,2,1,0:T(8,128)(2,1)S(1)}, bf16[2,1,1,768,768]{4,3,2,1,0:T(8,128)(2,1)}, u32[]{:S(2)}) copy-start(bf16[2,1,1,768,768]{4,3,2,1,0:T(8,128)(2,1)} %param.9) | copy-start | bytes 7077892
  76.4 3.4 %copy-start.5 = (f32[48,256]{1,0:T(8,128)S(1)}, f32[48,256]{1,0:T(8,128)}, u32[]{:S(2)}) copy-start(f32[48,256]{1,0:T(8,128)} %param.13) | copy-start | bytes 147460
  76.4 3.4 %copy-start.6 = (f32[48,256]{1,0:T(8,128)S(1)}, f32[48,256]{1,0:T(8,128)}, u32[]{:S(2)}) copy-start(f32[48,256]{1,0:T(8,128)} %param.14) | copy-start | bytes 147460
  76.5 3.4 %copy-start.4 = (f32[48,768]{1,0:T(8,128)S(1)}, f32[48,768]{1,0:T(8,128)}, u32[]{:S(2)}) copy-start(f32[48,768]{1,0:T(8,128)} %param.11) | copy-start | bytes 442372
  79.8 2.5 %copy-start.2 = (f32[48,256]{1,0:T(8,128)}, f32[48,256]{1,0:T(8,128)S(1)}, u32[]{:S(2)}) copy-start(f32[48,256]{1,0:T(8,128)S(1)} %get-tuple-element.15) | copy-start | bytes 147460
  79.9 2.5 %copy-start.3 = (f32[48,256]{1,0:T(8,128)}, f32[48,256]{1,0:T(8,128)S(1)}, u32[]{:S(2)}) copy-start(f32[48,256]{1,0:T(8,128)S(1)} %get-tuple-element.16) | copy-start | bytes 147460
